TPU v7x, 256 devices: a whole 4x4x8 slice. The times are simulated.
256 devices in a mesh: dp: 4 (over x), group: 4 (over y), member: 16 (over z, core).
Axes of the slice: x: 4, y: 4, z: 8, core: 2. Of those that a mesh axis runs over, the one named last changes fastest.
Arguments:
- tokens: bfloat16 [2048, 2880], P(('dp', 'group', 'member')), may hold values from -6 to 6
- cotangent: bfloat16 [2048, 2880], P(('dp', 'group', 'member')), may hold values from -6 to 6
- expert_ids: int32 [2048, 4], P(('dp', 'group', 'member')), may hold values from 0 to 7, all different within a row; in each aligned block of 8 rows (0 to 7, 8 to 15, ...) at most 8 rows name the same one
- gate_weights: float32 [2048, 4], P(('dp', 'group', 'member')), may hold values from 0.25 to 1
- w_gate: bfloat16 [8, 2880, 2880], P('group', 'member'), may hold values from -0.109375 to 0.109375
- w_up: bfloat16 [8, 2880, 2880], P('group', 'member'), may hold values from -0.109375 to 0.109375
- w_down: bfloat16 [8, 2880, 2880], P('group', 'member'), may hold values from -0.109375 to 0.109375
Outputs:
- grad_tokens: bfloat16 [2048, 2880], P(('dp', 'group', 'member'))
- grad_gate: bfloat16 [8, 2880, 2880], P('group', 'member', 'dp')
- grad_up: bfloat16 [8, 2880, 2880], P('group', 'member', 'dp')
- grad_down: bfloat16 [8, 2880, 2880], P('group', 'member', 'dp')
Inputs may be any that keep to these rules, and one draw needn't show every extreme that they name: `expert_ids`: each row names 4 different experts. Among the rows of one device no expert is named by more than 8 rows, a bound that some block reaches of them.
All inputs are finite; a program needn't handle non-finite values.
Results may differ from a plain program's by a relative error of at most 0.02.
Values may be sent and summed in bfloat16 or wider, within the bound.
No kernel may reach another device: no remote copies, remote signals or barrier semaphores. Data moves between devices by JAX's collectives and lax.ppermute only.
A program may use at most 128 MiB of HBM per device.

v0:
```python
import jax
import jax.numpy as jnp
from jax import lax
from jax.experimental import pallas as pl
from jax.experimental.pallas import tpu as pltpu
from jax.sharding import PartitionSpec as P


LANE = 128
PAD = 64
MIB = 1 << 20
OFFSETS = (0, -1, 1, -2, 2, -3, 3, 4)
VMEM = pl.BlockSpec(memory_space=pltpu.VMEM)
SMEM = pl.BlockSpec(memory_space=pltpu.SMEM)


def up_to(n, k):
    return -(-n // k) * k


def prepare(tokens, cotangent, expert_ids, gate_weights, padded):
    rows, width = tokens.shape
    room = padded - width
    quarter = room // 4
    bf = jnp.bfloat16

    def kernel(*refs):
        out_ref, sems = refs[4], refs[9]
        copies = [pltpu.make_async_copy(refs[i], refs[5 + i], sems.at[i]) for i in range(4)]
        for copy in copies:
            copy.start()
        for copy in copies:
            copy.wait()
        tok_ref, cot_ref, id_ref, weight_ref = refs[5:9]
        lane = lax.broadcasted_iota(jnp.int32, (rows, room), 1)
        expert = jnp.where(lane < quarter, lane, lane - quarter)
        diagonal = lax.broadcasted_iota(jnp.int32, (rows, rows), 0) == lax.broadcasted_iota(jnp.int32, (rows, rows), 1)
        coef = jnp.zeros((rows, room), jnp.float32)
        for k in range(id_ref.shape[0]):
            ids = jnp.sum(jnp.where(diagonal, id_ref[k : k + 1, :], 0), axis=1, keepdims=True)
            weights = jnp.sum(jnp.where(diagonal, weight_ref[k : k + 1, :], 0.0), axis=1, keepdims=True)
            coef = coef + jnp.where(ids == expert, weights, 0.0)
        high = coef.astype(bf).astype(jnp.float32)
        tail = jnp.where(lane < quarter, high, jnp.where(lane < 2 * quarter, coef - high, 0.0))
        out_ref[0, :, :width] = tok_ref[...]
        out_ref[0, :, width:] = tail.astype(bf)
        out_ref[1, :, :width] = cot_ref[...]
        out_ref[1, :, width:] = jnp.zeros((rows, room), bf)

    operands = (tokens, cotangent, expert_ids.T, gate_weights.T)
    return pl.pallas_call(
        kernel,
        out_shape=jax.ShapeDtypeStruct((2, rows, padded), bf),
        in_specs=[pl.BlockSpec(memory_space=pltpu.HBM)] * 4,
        out_specs=VMEM,
        scratch_shapes=[pltpu.VMEM(x.shape, x.dtype) for x in operands] + [pltpu.SemaphoreType.DMA((4,))],
        name="prepare",
    )(*operands)


def join(pieces):
    lead, rows, width = pieces[0].shape

    def kernel(*refs):
        for i, ref in enumerate(refs[:-1]):
            refs[-1][:, i * rows : (i + 1) * rows, :] = ref[...]

    return pl.pallas_call(
        kernel,
        out_shape=jax.ShapeDtypeStruct((lead, rows * len(pieces), width), pieces[0].dtype),
        compiler_params=pltpu.CompilerParams(vmem_limit_bytes=4 * MIB),
        name="join",
    )(*pieces)


def pack_weights(w_gate, w_up, w_down):
    n_exp, hid, width = w_gate.shape
    pad = up_to(hid, PAD)

    def kernel(g_ref, u_ref, d_ref, cat_ref, down_ref):
        i = pl.program_id(0)
        zero = jnp.zeros((pad - hid, width), jnp.bfloat16)
        cat_ref[hid:, :] = zero
        down_ref[hid:, :] = zero
        down_ref[:hid, :] = d_ref[0]

        @pl.when(i < n_exp)
        def _():
            cat_ref[:hid, :] = g_ref[0]

        @pl.when(i >= n_exp)
        def _():
            cat_ref[:hid, :] = u_ref[0]

    return pl.pallas_call(
        kernel,
        grid=(2 * n_exp,),
        out_shape=(
            jax.ShapeDtypeStruct((2 * n_exp * pad, width), jnp.bfloat16),
            jax.ShapeDtypeStruct((n_exp * pad, width), jnp.bfloat16),
        ),
        in_specs=[
            pl.BlockSpec((1, hid, width), lambda i: (jnp.minimum(i, n_exp - 1), 0, 0)),
            pl.BlockSpec((1, hid, width), lambda i: (jnp.maximum(i - n_exp, 0), 0, 0)),
            pl.BlockSpec((1, hid, width), lambda i: (i // 2, 0, 0)),
        ],
        out_specs=(
            pl.BlockSpec((pad, width), lambda i: (i, 0)),
            pl.BlockSpec((pad, width), lambda i: (i // 2, 0)),
        ),
        compiler_params=pltpu.CompilerParams(vmem_limit_bytes=14 * MIB),
        name="pack_weights",
    )(w_gate, w_up, w_down)


def forward(own, far, first, cat, down, width, n_exp, n_group, n_dp):
    half = sum(p.shape[1] for p in own)
    tall = 2 * half
    span = down.shape[0]
    pad = span // n_exp
    cols = width // n_dp
    bf = jnp.bfloat16
    f32 = jnp.float32
    nt = (((1,), (1,)), ((), ()))
    pieces = tuple(own) + tuple(far)
    block = 8 * n_group
    n_near = half // block

    def kernel(first_ref, *refs):
        rows = refs[: len(pieces)]
        cat_ref, down_ref, act_ref, near_ref, away_ref, cut_ref = refs[len(pieces) :]
        x = jnp.concatenate([r[0, :, :width] for r in rows], axis=0)
        y = jnp.concatenate([r[1, :, :width] for r in rows], axis=0)
        pre = lax.dot_general(x, cat_ref[...], nt, preferred_element_type=f32)
        back = lax.dot_general(y, down_ref[...], nt, preferred_element_type=f32)
        for d in range(n_dp):
            cut_ref[0, d] = x[:, d * cols : (d + 1) * cols]
            cut_ref[1, d] = y[:, d * cols : (d + 1) * cols]
        gate = pre[:, :span]
        up = pre[:, span:]
        tail = jnp.concatenate([r[0, :, width:] for r in rows], axis=0).astype(f32)
        lanes = lax.broadcasted_iota(jnp.int32, tail.shape, 1)
        quarter = tail.shape[1] // 4
        column = lax.broadcasted_iota(jnp.int32, gate.shape, 1)
        coef = jnp.zeros_like(gate)
        for e in range(n_exp):
            wanted = first_ref[0] + e
            hit = (lanes == wanted) | (lanes == wanted + quarter)
            mine = jnp.sum(jnp.where(hit, tail, 0.0), axis=1, keepdims=True)
            coef = jnp.where((column >= e * pad) & (column < (e + 1) * pad), mine, coef)
        sig = jax.nn.sigmoid(gate)
        silu = gate * sig
        back = back * coef
        act_ref[:, :span] = (back * up * sig * (1.0 + gate * (1.0 - sig))).astype(bf)
        act_ref[:, span : 2 * span] = (back * silu).astype(bf)
        act_ref[:, 2 * span :] = (coef * (silu * up)).astype(bf)
        part = jnp.dot(act_ref[:, : 2 * span], cat_ref[...], preferred_element_type=f32).astype(bf)
        for c, ref in enumerate((near_ref, away_ref)):
            for z in range(n_near):
                for g in range(n_group):
                    at = c * half + z * block + g * 8
                    ref[g, z] = part[at : at + 8]

    sums = jax.ShapeDtypeStruct((n_group, n_near, 8, width), bf)
    return pl.pallas_call(
        kernel,
        out_shape=(
            jax.ShapeDtypeStruct((tall, 3 * span), bf),
            sums,
            sums,
            jax.ShapeDtypeStruct((2, n_dp, tall, cols), bf),
        ),
        in_specs=[SMEM] + [VMEM] * (len(pieces) + 2),
        out_specs=(VMEM,) * 4,
        compiler_params=pltpu.CompilerParams(vmem_limit_bytes=12 * MIB),
        cost_estimate=pl.CostEstimate(
            flops=2 * tall * width * 5 * span, bytes_accessed=12 * MIB, transcendentals=tall * span
        ),
        name="forward",
    )(first, *pieces, cat, down)


def column_sums(place, offsets, n_dp, act_1, act_2, cut_1, cut_2, hid, n_exp, after=()):
    span = act_1.shape[1] // 3
    pad = span // n_exp
    cols = cut_1.shape[-1]
    tn = (((0,), (0,)), ((), ()))
    count = len(offsets)

    def kernel(place_ref, a_ref, b_ref, c_ref, d_ref, *rest):
        del place_ref
        outs = rest[len(after) :]
        act = jnp.concatenate([a_ref[...], b_ref[...]], axis=0)
        for kind in range(3):
            side = kind // 2
            x = jnp.concatenate([c_ref[side, 0], d_ref[side, 0]], axis=0)
            part = lax.dot_general(
                act[:, kind * span : (kind + 1) * span], x, tn, preferred_element_type=jnp.float32
            ).astype(jnp.bfloat16)
            for step in range(count):

                @pl.when(pl.program_id(0) == step)
                def _(step=step):
                    for e in range(n_exp):
                        outs[step * n_exp + e][kind] = part[e * pad : e * pad + hid, :]

    def picked(i, w):
        k = offsets[0]
        for step in range(1, count):
            k = jnp.where(i == step, offsets[step], k)
        return (0, lax.rem(w[0] + k, n_dp), 0, 0)

    fixed = lambda n: (lambda i, w: (0,) * n)
    outs = pl.pallas_call(
        kernel,
        out_shape=(jax.ShapeDtypeStruct((3, hid, cols), jnp.bfloat16),) * (n_exp * count),
        grid_spec=pltpu.PrefetchScalarGridSpec(
            num_scalar_prefetch=1,
            grid=(count,),
            in_specs=[
                pl.BlockSpec(act_1.shape, fixed(2)),
                pl.BlockSpec(act_2.shape, fixed(2)),
                pl.BlockSpec((2, 1) + cut_1.shape[2:], picked),
                pl.BlockSpec((2, 1) + cut_2.shape[2:], picked),
            ]
            + [pl.BlockSpec(memory_space=pl.ANY)] * len(after),
            out_specs=(VMEM,) * (n_exp * count),
        ),
        compiler_params=pltpu.CompilerParams(vmem_limit_bytes=12 * MIB),
        cost_estimate=pl.CostEstimate(
            flops=2 * 512 * 3 * span * cols * count, bytes_accessed=4 * MIB * count, transcendentals=0
        ),
        name="column_sums",
    )(place, act_1, act_2, cut_1, cut_2, *after)
    return [outs[i * n_exp : (i + 1) * n_exp] for i in range(count)]


def finish(parts):
    n_exp = len(parts)
    _, hid, cols = parts[0][0].shape

    def kernel(*refs):
        outs = refs[-3:]
        at = 0
        for e in range(n_exp):
            mine = refs[at : at + len(parts[e])]
            at += len(parts[e])
            for kind in range(3):
                total = mine[0][kind].astype(jnp.float32)
                for r in mine[1:]:
                    total = total + r[kind].astype(jnp.float32)
                outs[kind][:, e, :] = total.astype(jnp.bfloat16)

    flat = [a for p in parts for a in p]
    outs = pl.pallas_call(
        kernel,
        grid=(pl.cdiv(cols, 2 * LANE),),
        out_shape=(jax.ShapeDtypeStruct((hid, n_exp, cols), jnp.bfloat16),) * 3,
        in_specs=[pl.BlockSpec((3, hid, 2 * LANE), lambda i: (0, 0, i)) for _ in flat],
        out_specs=(pl.BlockSpec((hid, n_exp, 2 * LANE), lambda i: (0, 0, i)),) * 3,
        compiler_params=pltpu.CompilerParams(vmem_limit_bytes=12 * MIB),
        name="finish",
    )(*flat)
    return tuple(o.transpose(1, 0, 2) for o in outs)


def small(kernel, out_shape, operands):
    return pl.pallas_call(
        kernel,
        out_shape=out_shape,
        in_specs=[VMEM] * len(operands),
        out_specs=jax.tree.map(lambda _: VMEM, out_shape),
        compiler_params=pltpu.CompilerParams(vmem_limit_bytes=4 * MIB),
    )(*operands)


def halves(lo, hi):
    lead, rows, width = lo.shape
    half = rows // 2

    def kernel(lo_ref, hi_ref, top_ref, bottom_ref):
        top_ref[...] = lo_ref[:, :half, :]
        bottom_ref[...] = hi_ref[:, half:, :]

    piece = jax.ShapeDtypeStruct((lead, half, width), lo.dtype)
    return small(kernel, (piece, piece), (lo, hi))


def add(a, b, after):
    def kernel(a_ref, b_ref, _, out_ref):
        for k in range(a.shape[0]):
            out_ref[k] = (a_ref[k].astype(jnp.float32) + b_ref[k].astype(jnp.float32)).astype(a.dtype)

    return pl.pallas_call(
        kernel,
        out_shape=jax.ShapeDtypeStruct(a.shape, a.dtype),
        in_specs=[VMEM, VMEM, pl.BlockSpec(memory_space=pl.ANY)],
        out_specs=VMEM,
        compiler_params=pltpu.CompilerParams(vmem_limit_bytes=4 * MIB),
        name="add",
    )(a, b, after)


def merge_cores(near, arrived):
    n_group = near[0].shape[0]
    chips = sum(a.shape[1] for a in near)

    def kernel(*refs):
        outs = refs[4:]
        at = 0
        for a_ref, b_ref in zip(refs[:2], refs[2:4]):
            for j in range(a_ref.shape[1]):
                for k in range(n_group):
                    total = a_ref[k, j].astype(jnp.float32) + b_ref[k, j].astype(jnp.float32)
                    outs[k][at] = total.astype(jnp.bfloat16)
                at += 1

    one = jax.ShapeDtypeStruct((chips,) + near[0].shape[2:], near[0].dtype)
    return small(kernel, (one,) * n_group, (*near, *arrived))


def by_chip(parts):
    chips = parts[0].shape[0]
    half = chips // 2

    def kernel(*refs):
        outs = refs[len(parts) :]
        for j, offset in enumerate(OFFSETS):
            total = refs[0][j].astype(jnp.float32)
            for r in refs[1 : len(parts)]:
                total = total + r[j].astype(jnp.float32)
            ahead = offset % chips
            outs[ahead // half][ahead % half] = total.astype(jnp.bfloat16)

    one = jax.ShapeDtypeStruct((half,) + parts[0].shape[1:], parts[0].dtype)
    return small(kernel, (one, one), tuple(parts))


def fold(kept, arrived):
    half = kept.shape[0] // 2

    def kernel(a_ref, b_ref, *outs):
        for j in range(2 * half):
            total = a_ref[j].astype(jnp.float32) + b_ref[j].astype(jnp.float32)
            outs[j // half][j % half] = total.astype(jnp.bfloat16)

    one = jax.ShapeDtypeStruct((half,) + kept.shape[1:], kept.dtype)
    return small(kernel, (one, one), (kept, arrived))


def total_of(a, b):
    def kernel(a_ref, b_ref, out_ref):
        out_ref[...] = (a_ref[0].astype(jnp.float32) + b_ref[0].astype(jnp.float32)).astype(jnp.bfloat16)

    return small(kernel, jax.ShapeDtypeStruct(a.shape[1:], a.dtype), (a, b))


def shifted(x, axis, step):
    n = lax.axis_size(axis)
    return lax.ppermute(x, axis, [(i, (i - step) % n) for i in range(n)])


def partner(x):
    n = lax.axis_size("member")
    return lax.ppermute(x, "member", [(i, i ^ 1) for i in range(n)])


def step_of(tokens, cotangent, expert_ids, gate_weights, w_gate, w_up, w_down):
    n_group = lax.axis_size("group")
    n_dp = lax.axis_size("dp")
    n_exp, hid, width = w_gate.shape
    padded = up_to(width, LANE)
    place = lax.axis_index("dp").astype(jnp.int32).reshape(1)
    first = (lax.axis_index("group") * n_exp).astype(jnp.int32).reshape(1)
    mine = prepare(tokens, cotangent, expert_ids, gate_weights, padded)
    mine, place, first = lax.optimization_barrier((mine, place, first))
    own = join([mine] + [shifted(mine, "group", k) for k in range(1, n_group)])
    lo, hi, lo_far, hi_far = [own], [own], [], []
    own_far = partner(own)
    cat, down = pack_weights(w_gate, w_up, w_down)
    for step in range(3):
        lo.append(shifted(lo[-1], "member", -2))
        hi.append(shifted(hi[-1], "member", 2))
        if step == 0:
            lo[-1], hi[-1], cat, down = lax.optimization_barrier((lo[-1], hi[-1], cat, down))
        if step == 1:
            lo[-1], hi[-1], own_far, lo_far[0], hi_far[0] = lax.optimization_barrier(
                (lo[-1], hi[-1], own_far, lo_far[0], hi_far[0])
            )
        lo_far.append(partner(lo[-1]))
        hi_far.append(partner(hi[-1]))
    act_1, near_1, away_1, cut_1 = forward(
        [own, lo[1], hi[1], lo[2], hi[2]],
        [own_far, lo_far[0], hi_far[0], lo_far[1], hi_far[1]],
        first, cat, down, width, n_exp, n_group, n_dp,
    )
    lo[3], hi[3], act_1 = lax.optimization_barrier((lo[3], hi[3], act_1))
    top, bottom = halves(lo[3], hi[3])
    top = shifted(top, "member", -2)
    bottom = shifted(bottom, "member", 2)
    act_2, near_2, away_2, cut_2 = forward(
        [lo[3], hi[3], top, bottom],
        [lo_far[2], hi_far[2], partner(top), partner(bottom)],
        first, cat, down, width, n_exp, n_group, n_dp,
    )

    def shares(offsets, after=()):
        return column_sums(place, offsets, n_dp, act_1, act_2, cut_1, cut_2, hid, n_exp, after)

    ((far_0, far_1),) = shares((2,))
    right_0 = shifted(far_0, "dp", -1)
    left_1 = shifted(far_1, "dp", 1)
    (next_0, next_1), (prev_0, prev_1), (here_0, here_1) = shares((1, 3, 0), (far_0,))
    near_1, away_1, near_2, away_2, next_1, prev_0 = lax.optimization_barrier(
        (near_1, away_1, near_2, away_2, next_1, prev_0)
    )
    from_left_1 = shifted(next_1, "dp", -1)
    from_right_0 = shifted(prev_0, "dp", 1)
    both = merge_cores((near_1, near_2), (partner(away_1), partner(away_2)))
    kept, sent = by_chip([both[0]] + [shifted(both[k], "group", -k) for k in range(1, n_group)])
    from_left_0 = shifted(add(next_0, right_0, kept), "dp", -1)
    from_right_1 = shifted(add(prev_1, left_1, kept), "dp", 1)
    kept, sent = fold(kept, shifted(sent, "member", -8))
    kept, sent = fold(kept, shifted(sent, "member", -4))
    grad_tokens = total_of(kept, shifted(sent, "member", -2))
    grads = finish([[here_0, from_right_0, from_left_0], [here_1, from_left_1, from_right_1]])
    return (grad_tokens,) + tuple(grads)


def solution(mesh):
    placed = P(("dp", "group", "member"), None)
    weight = P("group", "member", None)
    grad = P("group", "member", "dp")
    return jax.shard_map(
        step_of,
        mesh=mesh,
        in_specs=(placed, placed, placed, placed, weight, weight, weight),
        out_specs=(placed, grad, grad, grad),
        check_vma=False,
    )
```

profile of v0, /device:TPU:1, one launch (start us, length us, event | category | flops | bytes accessed | tf_op | source)
XLA Modules:
  0.0 142.6 jit_solution(212335366005161127)
XLA Ops:
  0.6 1.7 %prepare.1.refs_0_ = bf16[2,8,2944]{2,1,0:T(8,128)(2,1)} custom-call(bf16[8,2880]{1,0:T(8,128)(2,1)} %refs_0_.1, bf16[8,2880]{1,0:T(8,128)(2,1)} %refs_1_.1, s32[4,8]{1,0:T(4,128)} %bitcast.7, f32[4,8]{1,0:T(4,128)} %bitcast.8), custom_call_target="tpu_custom_call" | custom-call | tf_op jit(solution)/shard_map/prepare/pallas_call | solution.py:51
  2.3 2.2 %collective-permute-start.2 = (bf16[2,8,2944]{2,1,0:T(8,128)(2,1)}, bf16[2,8,2944]{2,1,0:T(8,128)(2,1)S(1)}, u32[]{:S(2)}, u32[]{:S(2)}) collective-permute-start(bf16[2,8,2944]{2,1,0:T(8,128)(2,1)} %prepare.1.refs_0_), channel_id=1, source_target_pairs={{0,16},{16,32},{32,48},{48,0},{1,17},{17,33},{33,49},{49,1},{2,18}... | collective-permute-start | bytes 282632 | tf_op jit(solution)/shard_map/ppermute | solution.py:360
  4.5 2.6 %collective-permute-start.1 = (bf16[2,8,2944]{2,1,0:T(8,128)(2,1)}, bf16[2,8,2944]{2,1,0:T(8,128)(2,1)S(1)}, u32[]{:S(2)}, u32[]{:S(2)}) collective-permute-start(bf16[2,8,2944]{2,1,0:T(8,128)(2,1)} %prepare.1.refs_0_), channel_id=1, source_target_pairs={{0,32},{16,48},{32,0},{48,16},{1,33},{17,49},{33,1},{49,17},{2,34}... | collective-permute-start | bytes 282632 | tf_op jit(solution)/shard_map/ppermute | solution.py:360
  8.2 3.0 %collective-permute-done.1.refs_2_ = bf16[2,8,2944]{2,1,0:T(8,128)(2,1)S(1)} collective-permute-done((bf16[2,8,2944]{2,1,0:T(8,128)(2,1)}, bf16[2,8,2944]{2,1,0:T(8,128)(2,1)S(1)}, u32[]{:S(2)}, u32[]{:S(2)}) %collective-permute-start.1) | collective-permute-done | bytes 94240 | tf_op jit(solution)/shard_map/ppermute | solution.py:360
  12.1 5.7 %collective-permute-start.4 = (bf16[2,32,2944]{2,1,0:T(8,128)(2,1)S(1)}, bf16[2,32,2944]{2,1,0:T(8,128)(2,1)S(1)}, u32[]{:S(2)}, u32[]{:S(2)}) collective-permute-start(bf16[2,32,2944]{2,1,0:T(8,128)(2,1)S(1)} %join.1.refs_0_), channel_id=1, source_target_pairs={{0,14},{1,15},{2,0},{3,1},{4,2},{5,3},{6,4},{7,5},{8,6},{9,7},{10,... | collective-permute-start | bytes 1130504 | tf_op jit(solution)/shard_map/ppermute | solution.py:360
  17.8 1.8 %copy.11.g_ref = bf16[2,180,2880]{2,1,0:T(8,128)(2,1)S(1)} copy(bf16[2,180,2880]{2,0,1:T(2,128)(2,1)} %param.11) | data formatting | bytes 4147200 | tf_op args[4]
  22.2 2.3 %collective-permute-start.7 = (bf16[2,32,2944]{2,1,0:T(8,128)(2,1)S(1)}, bf16[2,32,2944]{2,1,0:T(8,128)(2,1)S(1)}, u32[]{:S(2)}, u32[]{:S(2)}) collective-permute-start(bf16[2,32,2944]{2,1,0:T(8,128)(2,1)S(1)} %join.1.refs_0_), channel_id=1, source_target_pairs={{0,1},{1,0},{2,3},{3,2},{4,5},{5,4},{6,7},{7,6},{8,9},{9,8},{10,11... | collective-permute-start | bytes 1130504 | tf_op jit(solution)/shard_map/ppermute | solution.py:365
  24.5 2.6 %collective-permute-done.3.refs_1_ = bf16[2,32,2944]{2,1,0:T(8,128)(2,1)S(1)} collective-permute-done((bf16[2,32,2944]{2,1,0:T(8,128)(2,1)S(1)}, bf16[2,32,2944]{2,1,0:T(8,128)(2,1)S(1)}, u32[]{:S(2)}, u32[]{:S(2)}) %collective-permute-start.3) | collective-permute-done | bytes 376864 | tf_op jit(solution)/shard_map/ppermute | solution.py:360
  27.1 3.1 %collective-permute-start.8 = (bf16[2,32,2944]{2,1,0:T(8,128)(2,1)S(1)}, bf16[2,32,2944]{2,1,0:T(8,128)(2,1)S(1)}, u32[]{:S(2)}, u32[]{:S(2)}) collective-permute-start(bf16[2,32,2944]{2,1,0:T(8,128)(2,1)S(1)} %collective-permute-done.3.refs_1_), channel_id=1, source_target_pairs={{0,1},{1,0},{2,3},{3,2},{4,5},{5,4},{6,7},{7,6},{8,9},{9,8},{10,11... | collective-permute-start | bytes 1130504 | tf_op jit(solution)/shard_map/ppermute | solution.py:365
  30.2 3.0 %collective-permute-start.6 = (bf16[2,32,2944]{2,1,0:T(8,128)(2,1)S(1)}, bf16[2,32,2944]{2,1,0:T(8,128)(2,1)S(1)}, u32[]{:S(2)}, u32[]{:S(2)}) collective-permute-start(bf16[2,32,2944]{2,1,0:T(8,128)(2,1)S(1)} %collective-permute-done.4.refs_2_), channel_id=1, source_target_pairs={{0,14},{1,15},{2,0},{3,1},{4,2},{5,3},{6,4},{7,5},{8,6},{9,7},{10,... | collective-permute-start | bytes 1130504 | tf_op jit(solution)/shard_map/ppermute | solution.py:360
  33.1 8.6 %collective-permute-done.5.refs_3_ = bf16[2,32,2944]{2,1,0:T(8,128)(2,1)S(1)} collective-permute-done((bf16[2,32,2944]{2,1,0:T(8,128)(2,1)S(1)}, bf16[2,32,2944]{2,1,0:T(8,128)(2,1)S(1)}, u32[]{:S(2)}, u32[]{:S(2)}) %collective-permute-start.5) | collective-permute-done | bytes 376864 | tf_op jit(solution)/shard_map/ppermute | solution.py:360
  42.7 2.9 %collective-permute-start.13 = (bf16[2,32,2944]{2,1,0:T(8,128)(2,1)S(1)}, bf16[2,32,2944]{2,1,0:T(8,128)(2,1)S(1)}, u32[]{:S(2)}, u32[]{:S(2)}) collective-permute-start(bf16[2,32,2944]{2,1,0:T(8,128)(2,1)S(1)} %collective-permute-done.6.refs_4_), channel_id=1, source_target_pairs={{0,14},{1,15},{2,0},{3,1},{4,2},{5,3},{6,4},{7,5},{8,6},{9,7},{10,... | collective-permute-start | bytes 1130504 | tf_op jit(solution)/shard_map/ppermute | solution.py:360
  45.5 5.3 %forward.2 = (bf16[320,1152]{1,0:T(8,128)(2,1)S(1)}, bf16[4,5,8,2880]{3,2,1,0:T(8,128)(2,1)S(1)}, bf16[4,5,8,2880]{3,2,1,0:T(8,128)(2,1)S(1)}, bf16[2,4,320,720]{3,2,1,0:T(8,128)(2,1)S(1)}) custom-call(s32[1]{0:T(128)} %bitcast.3.first_ref, bf16[2,32,2944]{2,1,0:T(8,128)(2,1)S(1)} %join.1.refs_0_, bf16[2,32,2944]{2,1,0:T(8,128)(2,1)S(1)} %collective-permute-done.3.refs_1_, ...), custom_call_target="tpu_custom_call" | custom-call | flops 3538944000 | bytes 12582912 | tf_op jit(solution)/shard_map/forward/pallas_call | solution.py:165
  50.8 3.3 %collective-permute-done.12.lo_ref.refs_0_ = bf16[2,32,2944]{2,1,0:T(8,128)(2,1)S(1)} collective-permute-done((bf16[2,32,2944]{2,1,0:T(8,128)(2,1)S(1)}, bf16[2,32,2944]{2,1,0:T(8,128)(2,1)S(1)}, u32[]{:S(2)}, u32[]{:S(2)}) %collective-permute-start.12) | collective-permute-done | bytes 376864 | tf_op jit(solution)/shard_map/ppermute | solution.py:360
  55.5 2.8 %collective-permute-start.15 = (bf16[2,16,2944]{2,1,0:T(8,128)(2,1)S(1)}, bf16[2,16,2944]{2,1,0:T(8,128)(2,1)S(1)}, u32[]{:S(2)}, u32[]{:S(2)}) collective-permute-start(bf16[2,16,2944]{2,1,0:T(8,128)(2,1)S(1)} %get-tuple-element.77), channel_id=1, source_target_pairs={{0,14},{1,15},{2,0},{3,1},{4,2},{5,3},{6,4},{7,5},{8,6},{9,7},{10,... | collective-permute-start | bytes 565256 | tf_op jit(solution)/shard_map/ppermute | solution.py:360
  58.3 2.4 %collective-permute-done.14.refs_2_ = bf16[2,16,2944]{2,1,0:T(8,128)(2,1)S(1)} collective-permute-done((bf16[2,16,2944]{2,1,0:T(8,128)(2,1)S(1)}, bf16[2,16,2944]{2,1,0:T(8,128)(2,1)S(1)}, u32[]{:S(2)}, u32[]{:S(2)}) %collective-permute-start.14) | collective-permute-done | bytes 188448 | tf_op jit(solution)/shard_map/ppermute | solution.py:360
  60.7 1.9 %collective-permute-start.18 = (bf16[2,16,2944]{2,1,0:T(8,128)(2,1)S(1)}, bf16[2,16,2944]{2,1,0:T(8,128)(2,1)S(1)}, u32[]{:S(2)}, u32[]{:S(2)}) collective-permute-start(bf16[2,16,2944]{2,1,0:T(8,128)(2,1)S(1)} %collective-permute-done.14.refs_2_), channel_id=1, source_target_pairs={{0,1},{1,0},{2,3},{3,2},{4,5},{5,4},{6,7},{7,6},{8,9},{9,8},{10,11... | collective-permute-start | bytes 565256 | tf_op jit(solution)/shard_map/ppermute | solution.py:365
  64.3 4.0 %forward.3 = (bf16[192,1152]{1,0:T(8,128)(2,1)S(1)}, bf16[4,3,8,2880]{3,2,1,0:T(8,128)(2,1)S(1)}, bf16[4,3,8,2880]{3,2,1,0:T(8,128)(2,1)S(1)}, bf16[2,4,192,720]{3,2,1,0:T(8,128)(2,1)S(1)}) custom-call(s32[1]{0:T(128)} %bitcast.3.first_ref, bf16[2,32,2944]{2,1,0:T(8,128)(2,1)S(1)} %collective-permute-done.12.lo_ref.refs_0_, ...), custom_call_target="tpu_custom_call" | custom-call | flops 2123366400 | bytes 12582912 | tf_op jit(solution)/shard_map/forward/pallas_call | solution.py:165
  69.5 6.2 %column_sums.3 = (bf16[3,180,720]{2,1,0:T(8,128)(2,1)S(1)}, bf16[3,180,720]{2,1,0:T(8,128)(2,1)S(1)}, bf16[3,180,720]{2,1,0:T(8,128)(2,1)S(1)}, bf16[3,180,720]{...) custom-call(s32[1]{0:T(128)} %bitcast.2.place_ref, ...), custom_call_target="tpu_custom_call" | custom-call | flops 2548039680 | bytes 12582912 | tf_op jit(solution)/shard_map/column_sums/pallas_call | solution.py:214
  80.2 2.7 %collective-permute-start.23 = (bf16[8,8,2880]{2,1,0:T(8,128)(2,1)S(1)}, bf16[8,8,2880]{2,1,0:T(8,128)(2,1)S(1)}, u32[]{:S(2)}, u32[]{:S(2)}) collective-permute-start(bf16[8,8,2880]{2,1,0:T(8,128)(2,1)S(1)} %get-tuple-element.94), channel_id=1, source_target_pairs={{0,32},{16,48},{32,0},{48,16},{1,33},{17,49},{33,1},{49,17},{2,34}... | collective-permute-start | bytes 1105928 | tf_op jit(solution)/shard_map/ppermute | solution.py:360
  83.9 6.3 %collective-permute-done.22.refs_1_ = bf16[8,8,2880]{2,1,0:T(8,128)(2,1)S(1)} collective-permute-done((bf16[8,8,2880]{2,1,0:T(8,128)(2,1)S(1)}, bf16[8,8,2880]{2,1,0:T(8,128)(2,1)S(1)}, u32[]{:S(2)}, u32[]{:S(2)}) %collective-permute-start.22) | collective-permute-done | bytes 368672 | tf_op jit(solution)/shard_map/ppermute | solution.py:360
  90.2 2.9 %collective-permute-start.28 = (bf16[3,180,720]{2,1,0:T(8,128)(2,1)S(1)}, bf16[3,180,720]{2,1,0:T(8,128)(2,1)S(1)}, u32[]{:S(2)}, u32[]{:S(2)}) collective-permute-start(bf16[3,180,720]{2,1,0:T(8,128)(2,1)S(1)} %get-tuple-element.103), channel_id=1, source_target_pairs={{0,192},{64,0},{128,64},{192,128},{1,193},{65,1},{129,65},{193,129... | collective-permute-start | bytes 2332808 | tf_op jit(solution)/shard_map/ppermute | solution.py:360
  93.1 5.9 %collective-permute-done.23.refs_2_ = bf16[8,8,2880]{2,1,0:T(8,128)(2,1)S(1)} collective-permute-done((bf16[8,8,2880]{2,1,0:T(8,128)(2,1)S(1)}, bf16[8,8,2880]{2,1,0:T(8,128)(2,1)S(1)}, u32[]{:S(2)}, u32[]{:S(2)}) %collective-permute-start.23) | collective-permute-done | bytes 368672 | tf_op jit(solution)/shard_map/ppermute | solution.py:360
  99.1 1.6 %collective-permute-start.31 = (bf16[3,180,720]{2,1,0:T(8,128)(2,1)S(1)}, bf16[3,180,720]{2,1,0:T(8,128)(2,1)S(1)}, u32[]{:S(2)}, u32[]{:S(2)}) collective-permute-start(bf16[3,180,720]{2,1,0:T(8,128)(2,1)S(1)} %get-tuple-element.106), channel_id=1, source_target_pairs={{0,64},{64,128},{128,192},{192,0},{1,65},{65,129},{129,193},{193,1... | collective-permute-start | bytes 2332808 | tf_op jit(solution)/shard_map/ppermute | solution.py:360
  104.1 3.1 %collective-permute-start.25 = (bf16[4,8,2880]{2,1,0:T(8,128)(2,1)S(1)}, bf16[4,8,2880]{2,1,0:T(8,128)(2,1)S(1)}, u32[]{:S(2)}, u32[]{:S(2)}) collective-permute-start(bf16[4,8,2880]{2,1,0:T(8,128)(2,1)S(1)} %get-tuple-element.97), channel_id=1, source_target_pairs={{0,8},{1,9},{2,10},{3,11},{4,12},{5,13},{6,14},{7,15},{8,0},{9,1},... | collective-permute-start | bytes 552968 | tf_op jit(solution)/shard_map/ppermute | solution.py:360
  107.2 5.4 %collective-permute-done.25.b_ref = bf16[4,8,2880]{2,1,0:T(8,128)(2,1)S(1)} collective-permute-done((bf16[4,8,2880]{2,1,0:T(8,128)(2,1)S(1)}, bf16[4,8,2880]{2,1,0:T(8,128)(2,1)S(1)}, u32[]{:S(2)}, u32[]{:S(2)}) %collective-permute-start.25) | collective-permute-done | bytes 184352 | tf_op jit(solution)/shard_map/ppermute | solution.py:360
  112.6 7.1 %collective-permute-start.26 = (bf16[2,8,2880]{2,1,0:T(8,128)(2,1)S(1)}, bf16[2,8,2880]{2,1,0:T(8,128)(2,1)S(1)}, u32[]{:S(2)}, u32[]{:S(2)}) collective-permute-start(bf16[2,8,2880]{2,1,0:T(8,128)(2,1)S(1)} %get-tuple-element.99), channel_id=1, source_target_pairs={{0,4},{1,5},{2,6},{3,7},{4,8},{5,9},{6,10},{7,11},{8,12},{9,13},{1... | collective-permute-start | bytes 276488 | tf_op jit(solution)/shard_map/ppermute | solution.py:360
  119.8 3.5 %collective-permute-done.26.b_ref = bf16[2,8,2880]{2,1,0:T(8,128)(2,1)S(1)} collective-permute-done((bf16[2,8,2880]{2,1,0:T(8,128)(2,1)S(1)}, bf16[2,8,2880]{2,1,0:T(8,128)(2,1)S(1)}, u32[]{:S(2)}, u32[]{:S(2)}) %collective-permute-start.26) | collective-permute-done | bytes 92192 | tf_op jit(solution)/shard_map/ppermute | solution.py:360
  123.3 1.6 %collective-permute-start.27 = (bf16[1,8,2880]{2,1,0:T(8,128)(2,1)S(1)}, bf16[1,8,2880]{2,1,0:T(8,128)(2,1)S(1)}, u32[]{:S(2)}, u32[]{:S(2)}) collective-permute-start(bf16[1,8,2880]{2,1,0:T(8,128)(2,1)S(1)} %get-tuple-element.101), channel_id=1, source_target_pairs={{0,2},{1,3},{2,4},{3,5},{4,6},{5,7},{6,8},{7,9},{8,10},{9,11},{10,... | collective-permute-start | bytes 138248 | tf_op jit(solution)/shard_map/ppermute | solution.py:360
  125.0 2.9 %collective-permute-done.27.b_ref = bf16[1,8,2880]{2,1,0:T(8,128)(2,1)S(1)} collective-permute-done((bf16[1,8,2880]{2,1,0:T(8,128)(2,1)S(1)}, bf16[1,8,2880]{2,1,0:T(8,128)(2,1)S(1)}, u32[]{:S(2)}, u32[]{:S(2)}) %collective-permute-start.27) | collective-permute-done | bytes 46112 | tf_op jit(solution)/shard_map/ppermute | solution.py:360
  128.5 9.2 %collective-permute-done.30.refs_2_ = bf16[3,180,720]{2,1,0:T(8,128)(2,1)S(1)} collective-permute-done((bf16[3,180,720]{2,1,0:T(8,128)(2,1)S(1)}, bf16[3,180,720]{2,1,0:T(8,128)(2,1)S(1)}, u32[]{:S(2)}, u32[]{:S(2)}) %collective-permute-start.30) | collective-permute-done | bytes 777632 | tf_op jit(solution)/shard_map/ppermute | solution.py:360
  137.7 4.8 %finish.1 = (bf16[180,2,720]{2,1,0:T(2,128)(2,1)}, bf16[180,2,720]{2,1,0:T(2,128)(2,1)}, bf16[180,2,720]{2,1,0:T(2,128)(2,1)}) custom-call(bf16[3,180,720]{2,1,0:T(8,128)(2,1)S(1)} %get-tuple-element.102.refs_0_, bf16[3,180,720]{2,1,0:T(8,128)(2,1)S(1)} %collective-permute-done.28.refs_1_, bf16[3,180,720]{2,1,0:T(8,128)(2,1)S(1)} %collective-permute-done.30.refs_2_, ...), custom_call_target="tpu_custom_call" | custom-call | tf_op jit(solution)/shard_map/finish/pallas_call | solution.py:255
  (61 shorter events, 19.4 us)
Async XLA Ops:
  2.3 5.9 %collective-permute-start.2 = (bf16[2,8,2944]{2,1,0:T(8,128)(2,1)}, bf16[2,8,2944]{2,1,0:T(8,128)(2,1)S(1)}, u32[]{:S(2)}, u32[]{:S(2)}) collective-permute-start(bf16[2,8,2944]{2,1,0:T(8,128)(2,1)} %prepare.1.refs_0_), channel_id=1, source_target_pairs={{0,16},{16,32},{32,48},{48,0},{1,17},{17,33},{33,49},{49,1},{2,18}... | collective-permute-start | bytes 282632 | tf_op jit(solution)/shard_map/ppermute | solution.py:360
  4.5 6.7 %collective-permute-start.1 = (bf16[2,8,2944]{2,1,0:T(8,128)(2,1)}, bf16[2,8,2944]{2,1,0:T(8,128)(2,1)S(1)}, u32[]{:S(2)}, u32[]{:S(2)}) collective-permute-start(bf16[2,8,2944]{2,1,0:T(8,128)(2,1)} %prepare.1.refs_0_), channel_id=1, source_target_pairs={{0,32},{16,48},{32,0},{48,16},{1,33},{17,49},{33,1},{49,17},{2,34}... | collective-permute-start | bytes 282632 | tf_op jit(solution)/shard_map/ppermute | solution.py:360
  7.1 4.1 %collective-permute-start = (bf16[2,8,2944]{2,1,0:T(8,128)(2,1)}, bf16[2,8,2944]{2,1,0:T(8,128)(2,1)S(1)}, u32[]{:S(2)}, u32[]{:S(2)}) collective-permute-start(bf16[2,8,2944]{2,1,0:T(8,128)(2,1)} %prepare.1.refs_0_), channel_id=1, source_target_pairs={{0,48},{16,0},{32,16},{48,32},{1,49},{17,1},{33,17},{49,33},{2,50}... | collective-permute-start | bytes 282632 | tf_op jit(solution)/shard_map/ppermute | solution.py:360
  12.1 12.4 %collective-permute-start.4 = (bf16[2,32,2944]{2,1,0:T(8,128)(2,1)S(1)}, bf16[2,32,2944]{2,1,0:T(8,128)(2,1)S(1)}, u32[]{:S(2)}, u32[]{:S(2)}) collective-permute-start(bf16[2,32,2944]{2,1,0:T(8,128)(2,1)S(1)} %join.1.refs_0_), channel_id=1, source_target_pairs={{0,14},{1,15},{2,0},{3,1},{4,2},{5,3},{6,4},{7,5},{8,6},{9,7},{10,... | collective-permute-start | bytes 1130504 | tf_op jit(solution)/shard_map/ppermute | solution.py:360
  17.8 9.3 %collective-permute-start.3 = (bf16[2,32,2944]{2,1,0:T(8,128)(2,1)S(1)}, bf16[2,32,2944]{2,1,0:T(8,128)(2,1)S(1)}, u32[]{:S(2)}, u32[]{:S(2)}) collective-permute-start(bf16[2,32,2944]{2,1,0:T(8,128)(2,1)S(1)} %join.1.refs_0_), channel_id=1, source_target_pairs={{0,2},{1,3},{2,4},{3,5},{4,6},{5,7},{6,8},{7,9},{8,10},{9,11},{10,... | collective-permute-start | bytes 1130504 | tf_op jit(solution)/shard_map/ppermute | solution.py:360
  22.2 11.0 %collective-permute-start.7 = (bf16[2,32,2944]{2,1,0:T(8,128)(2,1)S(1)}, bf16[2,32,2944]{2,1,0:T(8,128)(2,1)S(1)}, u32[]{:S(2)}, u32[]{:S(2)}) collective-permute-start(bf16[2,32,2944]{2,1,0:T(8,128)(2,1)S(1)} %join.1.refs_0_), channel_id=1, source_target_pairs={{0,1},{1,0},{2,3},{3,2},{4,5},{5,4},{6,7},{7,6},{8,9},{9,8},{10,11... | collective-permute-start | bytes 1130504 | tf_op jit(solution)/shard_map/ppermute | solution.py:365
  27.1 6.1 %collective-permute-start.8 = (bf16[2,32,2944]{2,1,0:T(8,128)(2,1)S(1)}, bf16[2,32,2944]{2,1,0:T(8,128)(2,1)S(1)}, u32[]{:S(2)}, u32[]{:S(2)}) collective-permute-start(bf16[2,32,2944]{2,1,0:T(8,128)(2,1)S(1)} %collective-permute-done.3.refs_1_), channel_id=1, source_target_pairs={{0,1},{1,0},{2,3},{3,2},{4,5},{5,4},{6,7},{7,6},{8,9},{9,8},{10,11... | collective-permute-start | bytes 1130504 | tf_op jit(solution)/shard_map/ppermute | solution.py:365
  30.2 11.5 %collective-permute-start.5 = (bf16[2,32,2944]{2,1,0:T(8,128)(2,1)S(1)}, bf16[2,32,2944]{2,1,0:T(8,128)(2,1)S(1)}, u32[]{:S(2)}, u32[]{:S(2)}) collective-permute-start(bf16[2,32,2944]{2,1,0:T(8,128)(2,1)S(1)} %collective-permute-done.3.refs_1_), channel_id=1, source_target_pairs={{0,2},{1,3},{2,4},{3,5},{4,6},{5,7},{6,8},{7,9},{8,10},{9,11},{10,... | collective-permute-start | bytes 1130504 | tf_op jit(solution)/shard_map/ppermute | solution.py:360
  30.2 11.5 %collective-permute-start.9 = (bf16[2,32,2944]{2,1,0:T(8,128)(2,1)S(1)}, bf16[2,32,2944]{2,1,0:T(8,128)(2,1)S(1)}, u32[]{:S(2)}, u32[]{:S(2)}) collective-permute-start(bf16[2,32,2944]{2,1,0:T(8,128)(2,1)S(1)} %collective-permute-done.4.refs_2_), channel_id=1, source_target_pairs={{0,1},{1,0},{2,3},{3,2},{4,5},{5,4},{6,7},{7,6},{8,9},{9,8},{10,11... | collective-permute-start | bytes 1130504 | tf_op jit(solution)/shard_map/ppermute | solution.py:365
  30.2 11.5 %collective-permute-start.6 = (bf16[2,32,2944]{2,1,0:T(8,128)(2,1)S(1)}, bf16[2,32,2944]{2,1,0:T(8,128)(2,1)S(1)}, u32[]{:S(2)}, u32[]{:S(2)}) collective-permute-start(bf16[2,32,2944]{2,1,0:T(8,128)(2,1)S(1)} %collective-permute-done.4.refs_2_), channel_id=1, source_target_pairs={{0,14},{1,15},{2,0},{3,1},{4,2},{5,3},{6,4},{7,5},{8,6},{9,7},{10,... | collective-permute-start | bytes 1130504 | tf_op jit(solution)/shard_map/ppermute | solution.py:360
  41.7 3.8 %collective-permute-start.10 = (bf16[2,32,2944]{2,1,0:T(8,128)(2,1)S(1)}, bf16[2,32,2944]{2,1,0:T(8,128)(2,1)S(1)}, u32[]{:S(2)}, u32[]{:S(2)}) collective-permute-start(bf16[2,32,2944]{2,1,0:T(8,128)(2,1)S(1)} %collective-permute-done.5.refs_3_), channel_id=1, source_target_pairs={{0,1},{1,0},{2,3},{3,2},{4,5},{5,4},{6,7},{7,6},{8,9},{9,8},{10,11... | collective-permute-start | bytes 1130504 | tf_op jit(solution)/shard_map/ppermute | solution.py:365
  42.6 3.0 %collective-permute-start.11 = (bf16[2,32,2944]{2,1,0:T(8,128)(2,1)S(1)}, bf16[2,32,2944]{2,1,0:T(8,128)(2,1)S(1)}, u32[]{:S(2)}, u32[]{:S(2)}) collective-permute-start(bf16[2,32,2944]{2,1,0:T(8,128)(2,1)S(1)} %collective-permute-done.6.refs_4_), channel_id=1, source_target_pairs={{0,1},{1,0},{2,3},{3,2},{4,5},{5,4},{6,7},{7,6},{8,9},{9,8},{10,11... | collective-permute-start | bytes 1130504 | tf_op jit(solution)/shard_map/ppermute | solution.py:365
  42.7 11.5 %collective-permute-start.12 = (bf16[2,32,2944]{2,1,0:T(8,128)(2,1)S(1)}, bf16[2,32,2944]{2,1,0:T(8,128)(2,1)S(1)}, u32[]{:S(2)}, u32[]{:S(2)}) collective-permute-start(bf16[2,32,2944]{2,1,0:T(8,128)(2,1)S(1)} %collective-permute-done.5.refs_3_), channel_id=1, source_target_pairs={{0,2},{1,3},{2,4},{3,5},{4,6},{5,7},{6,8},{7,9},{8,10},{9,11},{10,... | collective-permute-start | bytes 1130504 | tf_op jit(solution)/shard_map/ppermute | solution.py:360
  42.7 11.5 %collective-permute-start.13 = (bf16[2,32,2944]{2,1,0:T(8,128)(2,1)S(1)}, bf16[2,32,2944]{2,1,0:T(8,128)(2,1)S(1)}, u32[]{:S(2)}, u32[]{:S(2)}) collective-permute-start(bf16[2,32,2944]{2,1,0:T(8,128)(2,1)S(1)} %collective-permute-done.6.refs_4_), channel_id=1, source_target_pairs={{0,14},{1,15},{2,0},{3,1},{4,2},{5,3},{6,4},{7,5},{8,6},{9,7},{10,... | collective-permute-start | bytes 1130504 | tf_op jit(solution)/shard_map/ppermute | solution.py:360
  54.2 6.5 %collective-permute-start.14 = (bf16[2,16,2944]{2,1,0:T(8,128)(2,1)S(1)}, bf16[2,16,2944]{2,1,0:T(8,128)(2,1)S(1)}, u32[]{:S(2)}, u32[]{:S(2)}) collective-permute-start(bf16[2,16,2944]{2,1,0:T(8,128)(2,1)S(1)} %get-tuple-element.76), channel_id=1, source_target_pairs={{0,2},{1,3},{2,4},{3,5},{4,6},{5,7},{6,8},{7,9},{8,10},{9,11},{10,... | collective-permute-start | bytes 565256 | tf_op jit(solution)/shard_map/ppermute | solution.py:360
  54.3 9.0 %collective-permute-start.16 = (bf16[2,32,2944]{2,1,0:T(8,128)(2,1)S(1)}, bf16[2,32,2944]{2,1,0:T(8,128)(2,1)S(1)}, u32[]{:S(2)}, u32[]{:S(2)}) collective-permute-start(bf16[2,32,2944]{2,1,0:T(8,128)(2,1)S(1)} %collective-permute-done.12.lo_ref.refs_0_), channel_id=1, source_target_pairs={{0,1},{1,0},{2,3},{3,2},{4,5},{5,4},{6,7},{7,6},{8,9},{9,8},{10,11... | collective-permute-start | bytes 1130504 | tf_op jit(solution)/shard_map/ppermute | solution.py:365
  55.4 7.8 %collective-permute-start.17 = (bf16[2,32,2944]{2,1,0:T(8,128)(2,1)S(1)}, bf16[2,32,2944]{2,1,0:T(8,128)(2,1)S(1)}, u32[]{:S(2)}, u32[]{:S(2)}) collective-permute-start(bf16[2,32,2944]{2,1,0:T(8,128)(2,1)S(1)} %collective-permute-done.13.hi_ref.refs_1_), channel_id=1, source_target_pairs={{0,1},{1,0},{2,3},{3,2},{4,5},{5,4},{6,7},{7,6},{8,9},{9,8},{10,11... | collective-permute-start | bytes 1130504 | tf_op jit(solution)/shard_map/ppermute | solution.py:365
  55.5 7.1 %collective-permute-start.15 = (bf16[2,16,2944]{2,1,0:T(8,128)(2,1)S(1)}, bf16[2,16,2944]{2,1,0:T(8,128)(2,1)S(1)}, u32[]{:S(2)}, u32[]{:S(2)}) collective-permute-start(bf16[2,16,2944]{2,1,0:T(8,128)(2,1)S(1)} %get-tuple-element.77), channel_id=1, source_target_pairs={{0,14},{1,15},{2,0},{3,1},{4,2},{5,3},{6,4},{7,5},{8,6},{9,7},{10,... | collective-permute-start | bytes 565256 | tf_op jit(solution)/shard_map/ppermute | solution.py:360
  60.7 3.0 %collective-permute-start.18 = (bf16[2,16,2944]{2,1,0:T(8,128)(2,1)S(1)}, bf16[2,16,2944]{2,1,0:T(8,128)(2,1)S(1)}, u32[]{:S(2)}, u32[]{:S(2)}) collective-permute-start(bf16[2,16,2944]{2,1,0:T(8,128)(2,1)S(1)} %collective-permute-done.14.refs_2_), channel_id=1, source_target_pairs={{0,1},{1,0},{2,3},{3,2},{4,5},{5,4},{6,7},{7,6},{8,9},{9,8},{10,11... | collective-permute-start | bytes 565256 | tf_op jit(solution)/shard_map/ppermute | solution.py:365
  75.6 3.4 %collective-permute-start.20 = (bf16[4,5,8,2880]{3,2,1,0:T(8,128)(2,1)S(1)}, bf16[4,5,8,2880]{3,2,1,0:T(8,128)(2,1)S(1)}, u32[]{:S(2)}, u32[]{:S(2)}) collective-permute-start(bf16[4,5,8,2880]{3,2,1,0:T(8,128)(2,1)S(1)} %get-tuple-element.90), channel_id=1, source_target_pairs={{0,1},{1,0},{2,3},{3,2},{4,5},{5,4},{6,7},{7,6},{8,9},{9,8},{10,11... | collective-permute-start | bytes 2764808 | tf_op jit(solution)/shard_map/ppermute | solution.py:365
  76.2 24.7 %collective-permute-start.29 = (bf16[3,180,720]{2,1,0:T(8,128)(2,1)S(1)}, bf16[3,180,720]{2,1,0:T(8,128)(2,1)S(1)}, u32[]{:S(2)}, u32[]{:S(2)}) collective-permute-start(bf16[3,180,720]{2,1,0:T(8,128)(2,1)S(1)} %get-tuple-element.85.rest_0_), channel_id=1, source_target_pairs={{0,64},{64,128},{128,192},{192,0},{1,65},{65,129},{129,193},{193,1... | collective-permute-start | bytes 2332808 | tf_op jit(solution)/shard_map/ppermute | solution.py:360
  77.5 24.9 %collective-permute-start.32 = (bf16[3,180,720]{2,1,0:T(8,128)(2,1)S(1)}, bf16[3,180,720]{2,1,0:T(8,128)(2,1)S(1)}, u32[]{:S(2)}, u32[]{:S(2)}) collective-permute-start(bf16[3,180,720]{2,1,0:T(8,128)(2,1)S(1)} %get-tuple-element.108), channel_id=1, source_target_pairs={{0,192},{64,0},{128,64},{192,128},{1,193},{65,1},{129,65},{193,129... | collective-permute-start | bytes 2332808 | tf_op jit(solution)/shard_map/ppermute | solution.py:360
  79.4 10.8 %collective-permute-start.22 = (bf16[8,8,2880]{2,1,0:T(8,128)(2,1)S(1)}, bf16[8,8,2880]{2,1,0:T(8,128)(2,1)S(1)}, u32[]{:S(2)}, u32[]{:S(2)}) collective-permute-start(bf16[8,8,2880]{2,1,0:T(8,128)(2,1)S(1)} %get-tuple-element.93), channel_id=1, source_target_pairs={{0,16},{16,32},{32,48},{48,0},{1,17},{17,33},{33,49},{49,1},{2,18}... | collective-permute-start | bytes 1105928 | tf_op jit(solution)/shard_map/ppermute | solution.py:360
  80.2 18.8 %collective-permute-start.23 = (bf16[8,8,2880]{2,1,0:T(8,128)(2,1)S(1)}, bf16[8,8,2880]{2,1,0:T(8,128)(2,1)S(1)}, u32[]{:S(2)}, u32[]{:S(2)}) collective-permute-start(bf16[8,8,2880]{2,1,0:T(8,128)(2,1)S(1)} %get-tuple-element.94), channel_id=1, source_target_pairs={{0,32},{16,48},{32,0},{48,16},{1,33},{17,49},{33,1},{49,17},{2,34}... | collective-permute-start | bytes 1105928 | tf_op jit(solution)/shard_map/ppermute | solution.py:360
  82.9 17.8 %collective-permute-start.24 = (bf16[8,8,2880]{2,1,0:T(8,128)(2,1)S(1)}, bf16[8,8,2880]{2,1,0:T(8,128)(2,1)S(1)}, u32[]{:S(2)}, u32[]{:S(2)}) collective-permute-start(bf16[8,8,2880]{2,1,0:T(8,128)(2,1)S(1)} %get-tuple-element.95), channel_id=1, source_target_pairs={{0,48},{16,0},{32,16},{48,32},{1,49},{17,1},{33,17},{49,33},{2,50}... | collective-permute-start | bytes 1105928 | tf_op jit(solution)/shard_map/ppermute | solution.py:360
  90.2 38.3 %collective-permute-start.28 = (bf16[3,180,720]{2,1,0:T(8,128)(2,1)S(1)}, bf16[3,180,720]{2,1,0:T(8,128)(2,1)S(1)}, u32[]{:S(2)}, u32[]{:S(2)}) collective-permute-start(bf16[3,180,720]{2,1,0:T(8,128)(2,1)S(1)} %get-tuple-element.103), channel_id=1, source_target_pairs={{0,192},{64,0},{128,64},{192,128},{1,193},{65,1},{129,65},{193,129... | collective-permute-start | bytes 2332808 | tf_op jit(solution)/shard_map/ppermute | solution.py:360
  99.1 29.5 %collective-permute-start.31 = (bf16[3,180,720]{2,1,0:T(8,128)(2,1)S(1)}, bf16[3,180,720]{2,1,0:T(8,128)(2,1)S(1)}, u32[]{:S(2)}, u32[]{:S(2)}) collective-permute-start(bf16[3,180,720]{2,1,0:T(8,128)(2,1)S(1)} %get-tuple-element.106), channel_id=1, source_target_pairs={{0,64},{64,128},{128,192},{192,0},{1,65},{65,129},{129,193},{193,1... | collective-permute-start | bytes 2332808 | tf_op jit(solution)/shard_map/ppermute | solution.py:360
  101.1 36.6 %collective-permute-start.30 = (bf16[3,180,720]{2,1,0:T(8,128)(2,1)S(1)}, bf16[3,180,720]{2,1,0:T(8,128)(2,1)S(1)}, u32[]{:S(2)}, u32[]{:S(2)}) collective-permute-start(bf16[3,180,720]{2,1,0:T(8,128)(2,1)S(1)} %add.2), channel_id=1, source_target_pairs={{0,64},{64,128},{128,192},{192,0},{1,65},{65,129},{129,193},{193,1... | collective-permute-start | bytes 2332808 | tf_op jit(solution)/shard_map/ppermute | solution.py:360
  102.6 35.1 %collective-permute-start.33 = (bf16[3,180,720]{2,1,0:T(8,128)(2,1)S(1)}, bf16[3,180,720]{2,1,0:T(8,128)(2,1)S(1)}, u32[]{:S(2)}, u32[]{:S(2)}) collective-permute-start(bf16[3,180,720]{2,1,0:T(8,128)(2,1)S(1)} %add.3), channel_id=1, source_target_pairs={{0,192},{64,0},{128,64},{192,128},{1,193},{65,1},{129,65},{193,129... | collective-permute-start | bytes 2332808 | tf_op jit(solution)/shard_map/ppermute | solution.py:360
  104.1 8.4 %collective-permute-start.25 = (bf16[4,8,2880]{2,1,0:T(8,128)(2,1)S(1)}, bf16[4,8,2880]{2,1,0:T(8,128)(2,1)S(1)}, u32[]{:S(2)}, u32[]{:S(2)}) collective-permute-start(bf16[4,8,2880]{2,1,0:T(8,128)(2,1)S(1)} %get-tuple-element.97), channel_id=1, source_target_pairs={{0,8},{1,9},{2,10},{3,11},{4,12},{5,13},{6,14},{7,15},{8,0},{9,1},... | collective-permute-start | bytes 552968 | tf_op jit(solution)/shard_map/ppermute | solution.py:360
  112.6 10.7 %collective-permute-start.26 = (bf16[2,8,2880]{2,1,0:T(8,128)(2,1)S(1)}, bf16[2,8,2880]{2,1,0:T(8,128)(2,1)S(1)}, u32[]{:S(2)}, u32[]{:S(2)}) collective-permute-start(bf16[2,8,2880]{2,1,0:T(8,128)(2,1)S(1)} %get-tuple-element.99), channel_id=1, source_target_pairs={{0,4},{1,5},{2,6},{3,7},{4,8},{5,9},{6,10},{7,11},{8,12},{9,13},{1... | collective-permute-start | bytes 276488 | tf_op jit(solution)/shard_map/ppermute | solution.py:360
  123.3 4.5 %collective-permute-start.27 = (bf16[1,8,2880]{2,1,0:T(8,128)(2,1)S(1)}, bf16[1,8,2880]{2,1,0:T(8,128)(2,1)S(1)}, u32[]{:S(2)}, u32[]{:S(2)}) collective-permute-start(bf16[1,8,2880]{2,1,0:T(8,128)(2,1)S(1)} %get-tuple-element.101), channel_id=1, source_target_pairs={{0,2},{1,3},{2,4},{3,5},{4,6},{5,7},{6,8},{7,9},{8,10},{9,11},{10,... | collective-permute-start | bytes 138248 | tf_op jit(solution)/shard_map/ppermute | solution.py:360
  (5 other events, 14.6 us)
where the time goes:
time: 143 us
  starting transfers between devices  57.4 us (40%)
  waiting for transfers between devices  54.3 us (38%)
  Pallas kernels  25.6 us (18%)
  local copies, waits for them, and re-layouts  4.51 us (3%)
    ppermute x23, waiting for transfers between devices, shifted(): return lax.ppermute(x, axis, [(i, (i - step) % n) for i in range(n)])  53 us
    ppermute x23, starting transfers between devices, shifted(): return lax.ppermute(x, axis, [(i, (i - step) % n) for i in range(n)])  46.6 us
    ppermute x11, starting transfers between devices, partner(): return lax.ppermute(x, 'member', [(i, i ^ 1) for i in range(n)])  10.8 us
    pallas_call x2, Pallas kernels, forward(): pl.pallas_call(kernel, out_shape=(jax.ShapeDtypeStruct((tall, 3 * span),...  9.34 us
    pallas_call x2, Pallas kernels, column_sums(): pl.pallas_call(kernel, out_shape=(jax.ShapeDtypeStruct((3, hid, cols), jn...  7.31 us
    pallas_call x1, Pallas kernels, finish(): pl.pallas_call(kernel, grid=(pl.cdiv(cols, 2 * LANE),), out_shape=(jax.Sh...  4.85 us
    unnamed x9, local copies, waits for them, and re-layouts  4.51 us
  transfers between devices with their start and end apart: 34, of which 14 were waited for; matrix products, arithmetic and copies ran while one was open for 2% of the time, Pallas kernels for 5%

commit v1 on v0

--- a/solution.py
+++ b/solution.py
@@ -394,7 +394,6 @@
         [own_far, lo_far[0], hi_far[0], lo_far[1], hi_far[1]],
         first, cat, down, width, n_exp, n_group, n_dp,
     )
-    lo[3], hi[3], act_1 = lax.optimization_barrier((lo[3], hi[3], act_1))
     top, bottom = halves(lo[3], hi[3])
     top = shifted(top, "member", -2)
     bottom = shifted(bottom, "member", 2)
@@ -410,14 +409,16 @@
     ((far_0, far_1),) = shares((2,))
     right_0 = shifted(far_0, "dp", -1)
     left_1 = shifted(far_1, "dp", 1)
+    away_1 = partner(away_1)
+    away_2 = partner(away_2)
+    both = merge_cores((near_1, near_2), (away_1, away_2))
+    others = []
+    for k in range(1, n_group):
+        others.append(shifted(both[k], "group", -k))
     (next_0, next_1), (prev_0, prev_1), (here_0, here_1) = shares((1, 3, 0), (far_0,))
-    near_1, away_1, near_2, away_2, next_1, prev_0 = lax.optimization_barrier(
-        (near_1, away_1, near_2, away_2, next_1, prev_0)
-    )
     from_left_1 = shifted(next_1, "dp", -1)
     from_right_0 = shifted(prev_0, "dp", 1)
-    both = merge_cores((near_1, near_2), (partner(away_1), partner(away_2)))
-    kept, sent = by_chip([both[0]] + [shifted(both[k], "group", -k) for k in range(1, n_group)])
+    kept, sent = by_chip([both[0]] + others)
     from_left_0 = shifted(add(next_0, right_0, kept), "dp", -1)
     from_right_1 = shifted(add(prev_1, left_1, kept), "dp", 1)
     kept, sent = fold(kept, shifted(sent, "member", -8))

time: 143 us -> 137 us (0.958)
  starting transfers between devices: 57.4 us -> 53.5 us
  waiting for transfers between devices: 54.3 us -> 51.2 us
    ppermute x23, starting transfers between devices: 46.6 us -> 38.7 us  [shifted(): return lax.ppermute(x, axis, [(i, (i - step) % n) for i in range(n)])]
    ppermute x11, starting transfers between devices: 10.8 us -> 14.8 us  [partner(): return lax.ppermute(x, 'member', [(i, i ^ 1) for i in range(n)])]
    ppermute x23, waiting for transfers between devices: 53 us -> 51.2 us  [shifted(): return lax.ppermute(x, axis, [(i, (i - step) % n) for i in range(n)])]
  transfers between devices with their start and end apart: 34 -> 34, of which waited for: 14 -> 11; matrix products, arithmetic and copies ran while one was open for 2% -> 2% of each run, Pallas kernels for 5% -> 14%
where the time goes in v1:
time: 137 us; the launch traced here: 136 us
  starting transfers between devices  53.5 us (39%)
  waiting for transfers between devices  51.2 us (37%)
  Pallas kernels  25.6 us (19%)
  local copies, waits for them, and re-layouts  4.51 us (3%)
    ppermute x23, waiting for transfers between devices, shifted(): return lax.ppermute(x, axis, [(i, (i - step) % n) for i in range(n)])  51.2 us
    ppermute x23, starting transfers between devices, shifted(): return lax.ppermute(x, axis, [(i, (i - step) % n) for i in range(n)])  38.7 us
    ppermute x11, starting transfers between devices, partner(): return lax.ppermute(x, 'member', [(i, i ^ 1) for i in range(n)])  14.8 us
    pallas_call x2, Pallas kernels, forward(): pl.pallas_call(kernel, out_shape=(jax.ShapeDtypeStruct((tall, 3 * span),...  9.34 us
    pallas_call x2, Pallas kernels, column_sums(): pl.pallas_call(kernel, out_shape=(jax.ShapeDtypeStruct((3, hid, cols), jn...  7.26 us
    pallas_call x1, Pallas kernels, finish(): pl.pallas_call(kernel, grid=(pl.cdiv(cols, 2 * LANE),), out_shape=(jax.Sh...  4.85 us
    unnamed x9, local copies, waits for them, and re-layouts  4.51 us
  transfers between devices with their start and end apart: 34, of which 11 were waited for; matrix products, arithmetic and copies ran while one was open for 2% of the time, Pallas kernels for 14%

profile of v1, /device:TPU:1, one launch (start us, length us, event | category | flops | bytes accessed | tf_op | source)
XLA Modules:
  0.0 135.6 jit_solution(6830650905656201422)
XLA Ops:
  0.6 1.7 %prepare.1.refs_0_ = bf16[2,8,2944]{2,1,0:T(8,128)(2,1)} custom-call(bf16[8,2880]{1,0:T(8,128)(2,1)} %refs_0_.1, bf16[8,2880]{1,0:T(8,128)(2,1)} %refs_1_.1, s32[4,8]{1,0:T(4,128)} %bitcast.7, f32[4,8]{1,0:T(4,128)} %bitcast.8), custom_call_target="tpu_custom_call" | custom-call | tf_op jit(solution)/shard_map/prepare/pallas_call | solution.py:51
  2.3 3.6 %collective-permute-start = (bf16[2,8,2944]{2,1,0:T(8,128)(2,1)}, bf16[2,8,2944]{2,1,0:T(8,128)(2,1)S(1)}, u32[]{:S(2)}, u32[]{:S(2)}) collective-permute-start(bf16[2,8,2944]{2,1,0:T(8,128)(2,1)} %prepare.1.refs_0_), channel_id=1, source_target_pairs={{0,48},{16,0},{32,16},{48,32},{1,49},{17,1},{33,17},{49,33},{2,50}... | collective-permute-start | bytes 282632 | tf_op jit(solution)/shard_map/ppermute | solution.py:360
  7.9 3.3 %collective-permute-done.1.refs_2_ = bf16[2,8,2944]{2,1,0:T(8,128)(2,1)S(1)} collective-permute-done((bf16[2,8,2944]{2,1,0:T(8,128)(2,1)}, bf16[2,8,2944]{2,1,0:T(8,128)(2,1)S(1)}, u32[]{:S(2)}, u32[]{:S(2)}) %collective-permute-start.1) | collective-permute-done | bytes 94240 | tf_op jit(solution)/shard_map/ppermute | solution.py:360
  11.2 2.6 %collective-permute-done.2.refs_3_ = bf16[2,8,2944]{2,1,0:T(8,128)(2,1)S(1)} collective-permute-done((bf16[2,8,2944]{2,1,0:T(8,128)(2,1)}, bf16[2,8,2944]{2,1,0:T(8,128)(2,1)S(1)}, u32[]{:S(2)}, u32[]{:S(2)}) %collective-permute-start.2) | collective-permute-done | bytes 94240 | tf_op jit(solution)/shard_map/ppermute | solution.py:360
  14.8 1.7 %collective-permute-start.3 = (bf16[2,32,2944]{2,1,0:T(8,128)(2,1)S(1)}, bf16[2,32,2944]{2,1,0:T(8,128)(2,1)S(1)}, u32[]{:S(2)}, u32[]{:S(2)}) collective-permute-start(bf16[2,32,2944]{2,1,0:T(8,128)(2,1)S(1)} %join.1.refs_0_), channel_id=1, source_target_pairs={{0,2},{1,3},{2,4},{3,5},{4,6},{5,7},{6,8},{7,9},{8,10},{9,11},{10,... | collective-permute-start | bytes 1130504 | tf_op jit(solution)/shard_map/ppermute | solution.py:360
  16.5 4.0 %collective-permute-start.4 = (bf16[2,32,2944]{2,1,0:T(8,128)(2,1)S(1)}, bf16[2,32,2944]{2,1,0:T(8,128)(2,1)S(1)}, u32[]{:S(2)}, u32[]{:S(2)}) collective-permute-start(bf16[2,32,2944]{2,1,0:T(8,128)(2,1)S(1)} %join.1.refs_0_), channel_id=1, source_target_pairs={{0,14},{1,15},{2,0},{3,1},{4,2},{5,3},{6,4},{7,5},{8,6},{9,7},{10,... | collective-permute-start | bytes 1130504 | tf_op jit(solution)/shard_map/ppermute | solution.py:360
  20.5 1.8 %copy.11.g_ref = bf16[2,180,2880]{2,1,0:T(8,128)(2,1)S(1)} copy(bf16[2,180,2880]{2,0,1:T(2,128)(2,1)} %param.11) | data formatting | bytes 4147200 | tf_op args[4]
  22.6 1.4 %copy-done.2 = bf16[2,180,2880]{2,0,1:T(2,128)(2,1)S(1)} copy-done((bf16[2,180,2880]{2,0,1:T(2,128)(2,1)S(1)}, bf16[2,180,2880]{2,0,1:T(2,128)(2,1)}, u32[]{:S(2)}) %copy-start.2) | copy-done | bytes 2073624
  26.2 2.4 %collective-permute-done.3.refs_1_ = bf16[2,32,2944]{2,1,0:T(8,128)(2,1)S(1)} collective-permute-done((bf16[2,32,2944]{2,1,0:T(8,128)(2,1)S(1)}, bf16[2,32,2944]{2,1,0:T(8,128)(2,1)S(1)}, u32[]{:S(2)}, u32[]{:S(2)}) %collective-permute-start.3) | collective-permute-done | bytes 376864 | tf_op jit(solution)/shard_map/ppermute | solution.py:360
  28.6 2.7 %collective-permute-start.6 = (bf16[2,32,2944]{2,1,0:T(8,128)(2,1)S(1)}, bf16[2,32,2944]{2,1,0:T(8,128)(2,1)S(1)}, u32[]{:S(2)}, u32[]{:S(2)}) collective-permute-start(bf16[2,32,2944]{2,1,0:T(8,128)(2,1)S(1)} %collective-permute-done.4.refs_2_), channel_id=1, source_target_pairs={{0,14},{1,15},{2,0},{3,1},{4,2},{5,3},{6,4},{7,5},{8,6},{9,7},{10,... | collective-permute-start | bytes 1130504 | tf_op jit(solution)/shard_map/ppermute | solution.py:360
  31.3 2.1 %collective-permute-start.8 = (bf16[2,32,2944]{2,1,0:T(8,128)(2,1)S(1)}, bf16[2,32,2944]{2,1,0:T(8,128)(2,1)S(1)}, u32[]{:S(2)}, u32[]{:S(2)}) collective-permute-start(bf16[2,32,2944]{2,1,0:T(8,128)(2,1)S(1)} %collective-permute-done.3.refs_1_), channel_id=1, source_target_pairs={{0,1},{1,0},{2,3},{3,2},{4,5},{5,4},{6,7},{7,6},{8,9},{9,8},{10,11... | collective-permute-start | bytes 1130504 | tf_op jit(solution)/shard_map/ppermute | solution.py:365
  33.4 5.2 %collective-permute-done.5.refs_3_ = bf16[2,32,2944]{2,1,0:T(8,128)(2,1)S(1)} collective-permute-done((bf16[2,32,2944]{2,1,0:T(8,128)(2,1)S(1)}, bf16[2,32,2944]{2,1,0:T(8,128)(2,1)S(1)}, u32[]{:S(2)}, u32[]{:S(2)}) %collective-permute-start.5) | collective-permute-done | bytes 376864 | tf_op jit(solution)/shard_map/ppermute | solution.py:360
  39.6 1.7 %collective-permute-start.13 = (bf16[2,32,2944]{2,1,0:T(8,128)(2,1)S(1)}, bf16[2,32,2944]{2,1,0:T(8,128)(2,1)S(1)}, u32[]{:S(2)}, u32[]{:S(2)}) collective-permute-start(bf16[2,32,2944]{2,1,0:T(8,128)(2,1)S(1)} %collective-permute-done.6.refs_4_), channel_id=1, source_target_pairs={{0,14},{1,15},{2,0},{3,1},{4,2},{5,3},{6,4},{7,5},{8,6},{9,7},{10,... | collective-permute-start | bytes 1130504 | tf_op jit(solution)/shard_map/ppermute | solution.py:360
  41.3 3.0 %collective-permute-start.10 = (bf16[2,32,2944]{2,1,0:T(8,128)(2,1)S(1)}, bf16[2,32,2944]{2,1,0:T(8,128)(2,1)S(1)}, u32[]{:S(2)}, u32[]{:S(2)}) collective-permute-start(bf16[2,32,2944]{2,1,0:T(8,128)(2,1)S(1)} %collective-permute-done.5.refs_3_), channel_id=1, source_target_pairs={{0,1},{1,0},{2,3},{3,2},{4,5},{5,4},{6,7},{7,6},{8,9},{9,8},{10,11... | collective-permute-start | bytes 1130504 | tf_op jit(solution)/shard_map/ppermute | solution.py:365
  44.3 3.5 %collective-permute-done.12.lo_ref.refs_0_ = bf16[2,32,2944]{2,1,0:T(8,128)(2,1)S(1)} collective-permute-done((bf16[2,32,2944]{2,1,0:T(8,128)(2,1)S(1)}, bf16[2,32,2944]{2,1,0:T(8,128)(2,1)S(1)}, u32[]{:S(2)}, u32[]{:S(2)}) %collective-permute-start.12) | collective-permute-done | bytes 376864 | tf_op jit(solution)/shard_map/ppermute | solution.py:360
  48.4 2.2 %collective-permute-start.15 = (bf16[2,16,2944]{2,1,0:T(8,128)(2,1)S(1)}, bf16[2,16,2944]{2,1,0:T(8,128)(2,1)S(1)}, u32[]{:S(2)}, u32[]{:S(2)}) collective-permute-start(bf16[2,16,2944]{2,1,0:T(8,128)(2,1)S(1)} %get-tuple-element.64), channel_id=1, source_target_pairs={{0,14},{1,15},{2,0},{3,1},{4,2},{5,3},{6,4},{7,5},{8,6},{9,7},{10,... | collective-permute-start | bytes 565256 | tf_op jit(solution)/shard_map/ppermute | solution.py:360
  50.6 3.8 %collective-permute-start.16 = (bf16[2,32,2944]{2,1,0:T(8,128)(2,1)S(1)}, bf16[2,32,2944]{2,1,0:T(8,128)(2,1)S(1)}, u32[]{:S(2)}, u32[]{:S(2)}) collective-permute-start(bf16[2,32,2944]{2,1,0:T(8,128)(2,1)S(1)} %collective-permute-done.12.lo_ref.refs_0_), channel_id=1, source_target_pairs={{0,1},{1,0},{2,3},{3,2},{4,5},{5,4},{6,7},{7,6},{8,9},{9,8},{10,11... | collective-permute-start | bytes 1130504 | tf_op jit(solution)/shard_map/ppermute | solution.py:365
  54.4 3.5 %collective-permute-start.18 = (bf16[2,16,2944]{2,1,0:T(8,128)(2,1)S(1)}, bf16[2,16,2944]{2,1,0:T(8,128)(2,1)S(1)}, u32[]{:S(2)}, u32[]{:S(2)}) collective-permute-start(bf16[2,16,2944]{2,1,0:T(8,128)(2,1)S(1)} %collective-permute-done.14.refs_2_), channel_id=1, source_target_pairs={{0,1},{1,0},{2,3},{3,2},{4,5},{5,4},{6,7},{7,6},{8,9},{9,8},{10,11... | collective-permute-start | bytes 565256 | tf_op jit(solution)/shard_map/ppermute | solution.py:365
  58.3 5.3 %forward.2 = (bf16[320,1152]{1,0:T(8,128)(2,1)S(1)}, bf16[4,5,8,2880]{3,2,1,0:T(8,128)(2,1)S(1)}, bf16[4,5,8,2880]{3,2,1,0:T(8,128)(2,1)S(1)}, bf16[2,4,320,720]{3,2,1,0:T(8,128)(2,1)S(1)}) custom-call(s32[1]{0:T(128)} %bitcast.3.first_ref, bf16[2,32,2944]{2,1,0:T(8,128)(2,1)S(1)} %join.1.refs_0_, bf16[2,32,2944]{2,1,0:T(8,128)(2,1)S(1)} %collective-permute-done.3.refs_1_, ...), custom_call_target="tpu_custom_call" | custom-call | flops 3538944000 | bytes 12582912 | tf_op jit(solution)/shard_map/forward/pallas_call | solution.py:165
  63.9 4.0 %forward.3 = (bf16[192,1152]{1,0:T(8,128)(2,1)S(1)}, bf16[4,3,8,2880]{3,2,1,0:T(8,128)(2,1)S(1)}, bf16[4,3,8,2880]{3,2,1,0:T(8,128)(2,1)S(1)}, bf16[2,4,192,720]{3,2,1,0:T(8,128)(2,1)S(1)}) custom-call(s32[1]{0:T(128)} %bitcast.3.first_ref, bf16[2,32,2944]{2,1,0:T(8,128)(2,1)S(1)} %collective-permute-done.12.lo_ref.refs_0_, ...), custom_call_target="tpu_custom_call" | custom-call | flops 2123366400 | bytes 12582912 | tf_op jit(solution)/shard_map/forward/pallas_call | solution.py:165
  70.8 1.6 %collective-permute-start.32 = (bf16[3,180,720]{2,1,0:T(8,128)(2,1)S(1)}, bf16[3,180,720]{2,1,0:T(8,128)(2,1)S(1)}, u32[]{:S(2)}, u32[]{:S(2)}) collective-permute-start(bf16[3,180,720]{2,1,0:T(8,128)(2,1)S(1)} %get-tuple-element.90), channel_id=1, source_target_pairs={{0,192},{64,0},{128,64},{192,128},{1,193},{65,1},{129,65},{193,129... | collective-permute-start | bytes 2332808 | tf_op jit(solution)/shard_map/ppermute | solution.py:360
  72.9 2.6 %collective-permute-start.24 = (bf16[8,8,2880]{2,1,0:T(8,128)(2,1)S(1)}, bf16[8,8,2880]{2,1,0:T(8,128)(2,1)S(1)}, u32[]{:S(2)}, u32[]{:S(2)}) collective-permute-start(bf16[8,8,2880]{2,1,0:T(8,128)(2,1)S(1)} %get-tuple-element.71), channel_id=1, source_target_pairs={{0,48},{16,0},{32,16},{48,32},{1,49},{17,1},{33,17},{49,33},{2,50}... | collective-permute-start | bytes 1105928 | tf_op jit(solution)/shard_map/ppermute | solution.py:360
  75.5 6.1 %column_sums.3 = (bf16[3,180,720]{2,1,0:T(8,128)(2,1)S(1)}, bf16[3,180,720]{2,1,0:T(8,128)(2,1)S(1)}, bf16[3,180,720]{2,1,0:T(8,128)(2,1)S(1)}, bf16[3,180,720]{...) custom-call(s32[1]{0:T(128)} %bitcast.2.place_ref, ...), custom_call_target="tpu_custom_call" | custom-call | flops 2548039680 | bytes 12582912 | tf_op jit(solution)/shard_map/column_sums/pallas_call | solution.py:214
  81.6 10.2 %collective-permute-done.22.refs_1_ = bf16[8,8,2880]{2,1,0:T(8,128)(2,1)S(1)} collective-permute-done((bf16[8,8,2880]{2,1,0:T(8,128)(2,1)S(1)}, bf16[8,8,2880]{2,1,0:T(8,128)(2,1)S(1)}, u32[]{:S(2)}, u32[]{:S(2)}) %collective-permute-start.22) | collective-permute-done | bytes 368672 | tf_op jit(solution)/shard_map/ppermute | solution.py:360
  94.0 2.7 %collective-permute-start.33 = (bf16[3,180,720]{2,1,0:T(8,128)(2,1)S(1)}, bf16[3,180,720]{2,1,0:T(8,128)(2,1)S(1)}, u32[]{:S(2)}, u32[]{:S(2)}) collective-permute-start(bf16[3,180,720]{2,1,0:T(8,128)(2,1)S(1)} %add.3), channel_id=1, source_target_pairs={{0,192},{64,0},{128,64},{192,128},{1,193},{65,1},{129,65},{193,129... | collective-permute-start | bytes 2332808 | tf_op jit(solution)/shard_map/ppermute | solution.py:360
  96.7 2.9 %collective-permute-start.25 = (bf16[4,8,2880]{2,1,0:T(8,128)(2,1)S(1)}, bf16[4,8,2880]{2,1,0:T(8,128)(2,1)S(1)}, u32[]{:S(2)}, u32[]{:S(2)}) collective-permute-start(bf16[4,8,2880]{2,1,0:T(8,128)(2,1)S(1)} %get-tuple-element.73), channel_id=1, source_target_pairs={{0,8},{1,9},{2,10},{3,11},{4,12},{5,13},{6,14},{7,15},{8,0},{9,1},... | collective-permute-start | bytes 552968 | tf_op jit(solution)/shard_map/ppermute | solution.py:360
  99.6 5.6 %collective-permute-done.25.b_ref = bf16[4,8,2880]{2,1,0:T(8,128)(2,1)S(1)} collective-permute-done((bf16[4,8,2880]{2,1,0:T(8,128)(2,1)S(1)}, bf16[4,8,2880]{2,1,0:T(8,128)(2,1)S(1)}, u32[]{:S(2)}, u32[]{:S(2)}) %collective-permute-start.25) | collective-permute-done | bytes 184352 | tf_op jit(solution)/shard_map/ppermute | solution.py:360
  105.2 7.3 %collective-permute-start.26 = (bf16[2,8,2880]{2,1,0:T(8,128)(2,1)S(1)}, bf16[2,8,2880]{2,1,0:T(8,128)(2,1)S(1)}, u32[]{:S(2)}, u32[]{:S(2)}) collective-permute-start(bf16[2,8,2880]{2,1,0:T(8,128)(2,1)S(1)} %get-tuple-element.75), channel_id=1, source_target_pairs={{0,4},{1,5},{2,6},{3,7},{4,8},{5,9},{6,10},{7,11},{8,12},{9,13},{1... | collective-permute-start | bytes 276488 | tf_op jit(solution)/shard_map/ppermute | solution.py:360
  112.5 4.2 %collective-permute-done.26.b_ref = bf16[2,8,2880]{2,1,0:T(8,128)(2,1)S(1)} collective-permute-done((bf16[2,8,2880]{2,1,0:T(8,128)(2,1)S(1)}, bf16[2,8,2880]{2,1,0:T(8,128)(2,1)S(1)}, u32[]{:S(2)}, u32[]{:S(2)}) %collective-permute-start.26) | collective-permute-done | bytes 92192 | tf_op jit(solution)/shard_map/ppermute | solution.py:360
  116.8 4.4 %collective-permute-done.27.b_ref = bf16[1,8,2880]{2,1,0:T(8,128)(2,1)S(1)} collective-permute-done((bf16[1,8,2880]{2,1,0:T(8,128)(2,1)S(1)}, bf16[1,8,2880]{2,1,0:T(8,128)(2,1)S(1)}, u32[]{:S(2)}, u32[]{:S(2)}) %collective-permute-start.27) | collective-permute-done | bytes 46112 | tf_op jit(solution)/shard_map/ppermute | solution.py:360
  121.9 8.9 %collective-permute-done.30.refs_2_ = bf16[3,180,720]{2,1,0:T(8,128)(2,1)S(1)} collective-permute-done((bf16[3,180,720]{2,1,0:T(8,128)(2,1)S(1)}, bf16[3,180,720]{2,1,0:T(8,128)(2,1)S(1)}, u32[]{:S(2)}, u32[]{:S(2)}) %collective-permute-start.30) | collective-permute-done | bytes 777632 | tf_op jit(solution)/shard_map/ppermute | solution.py:360
  130.7 4.8 %finish.1 = (bf16[180,2,720]{2,1,0:T(2,128)(2,1)}, bf16[180,2,720]{2,1,0:T(2,128)(2,1)}, bf16[180,2,720]{2,1,0:T(2,128)(2,1)}) custom-call(bf16[3,180,720]{2,1,0:T(8,128)(2,1)S(1)} %get-tuple-element.84.refs_0_, bf16[3,180,720]{2,1,0:T(8,128)(2,1)S(1)} %collective-permute-done.28.refs_1_, bf16[3,180,720]{2,1,0:T(8,128)(2,1)S(1)} %collective-permute-done.30.refs_2_, ...), custom_call_target="tpu_custom_call" | custom-call | tf_op jit(solution)/shard_map/finish/pallas_call | solution.py:255
  (61 shorter events, 13.9 us)
Async XLA Ops:
  2.3 5.5 %collective-permute-start = (bf16[2,8,2944]{2,1,0:T(8,128)(2,1)}, bf16[2,8,2944]{2,1,0:T(8,128)(2,1)S(1)}, u32[]{:S(2)}, u32[]{:S(2)}) collective-permute-start(bf16[2,8,2944]{2,1,0:T(8,128)(2,1)} %prepare.1.refs_0_), channel_id=1, source_target_pairs={{0,48},{16,0},{32,16},{48,32},{1,49},{17,1},{33,17},{49,33},{2,50}... | collective-permute-start | bytes 282632 | tf_op jit(solution)/shard_map/ppermute | solution.py:360
  5.9 5.2 %collective-permute-start.1 = (bf16[2,8,2944]{2,1,0:T(8,128)(2,1)}, bf16[2,8,2944]{2,1,0:T(8,128)(2,1)S(1)}, u32[]{:S(2)}, u32[]{:S(2)}) collective-permute-start(bf16[2,8,2944]{2,1,0:T(8,128)(2,1)} %prepare.1.refs_0_), channel_id=1, source_target_pairs={{0,32},{16,48},{32,0},{48,16},{1,33},{17,49},{33,1},{49,17},{2,34}... | collective-permute-start | bytes 282632 | tf_op jit(solution)/shard_map/ppermute | solution.py:360
  6.3 7.5 %collective-permute-start.2 = (bf16[2,8,2944]{2,1,0:T(8,128)(2,1)}, bf16[2,8,2944]{2,1,0:T(8,128)(2,1)S(1)}, u32[]{:S(2)}, u32[]{:S(2)}) collective-permute-start(bf16[2,8,2944]{2,1,0:T(8,128)(2,1)} %prepare.1.refs_0_), channel_id=1, source_target_pairs={{0,16},{16,32},{32,48},{48,0},{1,17},{17,33},{33,49},{49,1},{2,18}... | collective-permute-start | bytes 282632 | tf_op jit(solution)/shard_map/ppermute | solution.py:360
  14.8 13.8 %collective-permute-start.3 = (bf16[2,32,2944]{2,1,0:T(8,128)(2,1)S(1)}, bf16[2,32,2944]{2,1,0:T(8,128)(2,1)S(1)}, u32[]{:S(2)}, u32[]{:S(2)}) collective-permute-start(bf16[2,32,2944]{2,1,0:T(8,128)(2,1)S(1)} %join.1.refs_0_), channel_id=1, source_target_pairs={{0,2},{1,3},{2,4},{3,5},{4,6},{5,7},{6,8},{7,9},{8,10},{9,11},{10,... | collective-permute-start | bytes 1130504 | tf_op jit(solution)/shard_map/ppermute | solution.py:360
  16.5 12.1 %collective-permute-start.4 = (bf16[2,32,2944]{2,1,0:T(8,128)(2,1)S(1)}, bf16[2,32,2944]{2,1,0:T(8,128)(2,1)S(1)}, u32[]{:S(2)}, u32[]{:S(2)}) collective-permute-start(bf16[2,32,2944]{2,1,0:T(8,128)(2,1)S(1)} %join.1.refs_0_), channel_id=1, source_target_pairs={{0,14},{1,15},{2,0},{3,1},{4,2},{5,3},{6,4},{7,5},{8,6},{9,7},{10,... | collective-permute-start | bytes 1130504 | tf_op jit(solution)/shard_map/ppermute | solution.py:360
  24.9 8.5 %collective-permute-start.7 = (bf16[2,32,2944]{2,1,0:T(8,128)(2,1)S(1)}, bf16[2,32,2944]{2,1,0:T(8,128)(2,1)S(1)}, u32[]{:S(2)}, u32[]{:S(2)}) collective-permute-start(bf16[2,32,2944]{2,1,0:T(8,128)(2,1)S(1)} %join.1.refs_0_), channel_id=1, source_target_pairs={{0,1},{1,0},{2,3},{3,2},{4,5},{5,4},{6,7},{7,6},{8,9},{9,8},{10,11... | collective-permute-start | bytes 1130504 | tf_op jit(solution)/shard_map/ppermute | solution.py:365
  28.6 10.0 %collective-permute-start.5 = (bf16[2,32,2944]{2,1,0:T(8,128)(2,1)S(1)}, bf16[2,32,2944]{2,1,0:T(8,128)(2,1)S(1)}, u32[]{:S(2)}, u32[]{:S(2)}) collective-permute-start(bf16[2,32,2944]{2,1,0:T(8,128)(2,1)S(1)} %collective-permute-done.3.refs_1_), channel_id=1, source_target_pairs={{0,2},{1,3},{2,4},{3,5},{4,6},{5,7},{6,8},{7,9},{8,10},{9,11},{10,... | collective-permute-start | bytes 1130504 | tf_op jit(solution)/shard_map/ppermute | solution.py:360
  28.6 10.0 %collective-permute-start.6 = (bf16[2,32,2944]{2,1,0:T(8,128)(2,1)S(1)}, bf16[2,32,2944]{2,1,0:T(8,128)(2,1)S(1)}, u32[]{:S(2)}, u32[]{:S(2)}) collective-permute-start(bf16[2,32,2944]{2,1,0:T(8,128)(2,1)S(1)} %collective-permute-done.4.refs_2_), channel_id=1, source_target_pairs={{0,14},{1,15},{2,0},{3,1},{4,2},{5,3},{6,4},{7,5},{8,6},{9,7},{10,... | collective-permute-start | bytes 1130504 | tf_op jit(solution)/shard_map/ppermute | solution.py:360
  31.3 7.3 %collective-permute-start.8 = (bf16[2,32,2944]{2,1,0:T(8,128)(2,1)S(1)}, bf16[2,32,2944]{2,1,0:T(8,128)(2,1)S(1)}, u32[]{:S(2)}, u32[]{:S(2)}) collective-permute-start(bf16[2,32,2944]{2,1,0:T(8,128)(2,1)S(1)} %collective-permute-done.3.refs_1_), channel_id=1, source_target_pairs={{0,1},{1,0},{2,3},{3,2},{4,5},{5,4},{6,7},{7,6},{8,9},{9,8},{10,11... | collective-permute-start | bytes 1130504 | tf_op jit(solution)/shard_map/ppermute | solution.py:365
  33.4 5.2 %collective-permute-start.9 = (bf16[2,32,2944]{2,1,0:T(8,128)(2,1)S(1)}, bf16[2,32,2944]{2,1,0:T(8,128)(2,1)S(1)}, u32[]{:S(2)}, u32[]{:S(2)}) collective-permute-start(bf16[2,32,2944]{2,1,0:T(8,128)(2,1)S(1)} %collective-permute-done.4.refs_2_), channel_id=1, source_target_pairs={{0,1},{1,0},{2,3},{3,2},{4,5},{5,4},{6,7},{7,6},{8,9},{9,8},{10,11... | collective-permute-start | bytes 1130504 | tf_op jit(solution)/shard_map/ppermute | solution.py:365
  38.6 9.2 %collective-permute-start.12 = (bf16[2,32,2944]{2,1,0:T(8,128)(2,1)S(1)}, bf16[2,32,2944]{2,1,0:T(8,128)(2,1)S(1)}, u32[]{:S(2)}, u32[]{:S(2)}) collective-permute-start(bf16[2,32,2944]{2,1,0:T(8,128)(2,1)S(1)} %collective-permute-done.5.refs_3_), channel_id=1, source_target_pairs={{0,2},{1,3},{2,4},{3,5},{4,6},{5,7},{6,8},{7,9},{8,10},{9,11},{10,... | collective-permute-start | bytes 1130504 | tf_op jit(solution)/shard_map/ppermute | solution.py:360
  39.6 8.2 %collective-permute-start.13 = (bf16[2,32,2944]{2,1,0:T(8,128)(2,1)S(1)}, bf16[2,32,2944]{2,1,0:T(8,128)(2,1)S(1)}, u32[]{:S(2)}, u32[]{:S(2)}) collective-permute-start(bf16[2,32,2944]{2,1,0:T(8,128)(2,1)S(1)} %collective-permute-done.6.refs_4_), channel_id=1, source_target_pairs={{0,14},{1,15},{2,0},{3,1},{4,2},{5,3},{6,4},{7,5},{8,6},{9,7},{10,... | collective-permute-start | bytes 1130504 | tf_op jit(solution)/shard_map/ppermute | solution.py:360
  41.3 13.1 %collective-permute-start.10 = (bf16[2,32,2944]{2,1,0:T(8,128)(2,1)S(1)}, bf16[2,32,2944]{2,1,0:T(8,128)(2,1)S(1)}, u32[]{:S(2)}, u32[]{:S(2)}) collective-permute-start(bf16[2,32,2944]{2,1,0:T(8,128)(2,1)S(1)} %collective-permute-done.5.refs_3_), channel_id=1, source_target_pairs={{0,1},{1,0},{2,3},{3,2},{4,5},{5,4},{6,7},{7,6},{8,9},{9,8},{10,11... | collective-permute-start | bytes 1130504 | tf_op jit(solution)/shard_map/ppermute | solution.py:365
  44.3 14.0 %collective-permute-start.11 = (bf16[2,32,2944]{2,1,0:T(8,128)(2,1)S(1)}, bf16[2,32,2944]{2,1,0:T(8,128)(2,1)S(1)}, u32[]{:S(2)}, u32[]{:S(2)}) collective-permute-start(bf16[2,32,2944]{2,1,0:T(8,128)(2,1)S(1)} %collective-permute-done.6.refs_4_), channel_id=1, source_target_pairs={{0,1},{1,0},{2,3},{3,2},{4,5},{5,4},{6,7},{7,6},{8,9},{9,8},{10,11... | collective-permute-start | bytes 1130504 | tf_op jit(solution)/shard_map/ppermute | solution.py:365
  47.8 6.6 %collective-permute-start.14 = (bf16[2,16,2944]{2,1,0:T(8,128)(2,1)S(1)}, bf16[2,16,2944]{2,1,0:T(8,128)(2,1)S(1)}, u32[]{:S(2)}, u32[]{:S(2)}) collective-permute-start(bf16[2,16,2944]{2,1,0:T(8,128)(2,1)S(1)} %get-tuple-element.63), channel_id=1, source_target_pairs={{0,2},{1,3},{2,4},{3,5},{4,6},{5,7},{6,8},{7,9},{8,10},{9,11},{10,... | collective-permute-start | bytes 565256 | tf_op jit(solution)/shard_map/ppermute | solution.py:360
  48.4 9.6 %collective-permute-start.15 = (bf16[2,16,2944]{2,1,0:T(8,128)(2,1)S(1)}, bf16[2,16,2944]{2,1,0:T(8,128)(2,1)S(1)}, u32[]{:S(2)}, u32[]{:S(2)}) collective-permute-start(bf16[2,16,2944]{2,1,0:T(8,128)(2,1)S(1)} %get-tuple-element.64), channel_id=1, source_target_pairs={{0,14},{1,15},{2,0},{3,1},{4,2},{5,3},{6,4},{7,5},{8,6},{9,7},{10,... | collective-permute-start | bytes 565256 | tf_op jit(solution)/shard_map/ppermute | solution.py:360
  50.6 13.3 %collective-permute-start.16 = (bf16[2,32,2944]{2,1,0:T(8,128)(2,1)S(1)}, bf16[2,32,2944]{2,1,0:T(8,128)(2,1)S(1)}, u32[]{:S(2)}, u32[]{:S(2)}) collective-permute-start(bf16[2,32,2944]{2,1,0:T(8,128)(2,1)S(1)} %collective-permute-done.12.lo_ref.refs_0_), channel_id=1, source_target_pairs={{0,1},{1,0},{2,3},{3,2},{4,5},{5,4},{6,7},{7,6},{8,9},{9,8},{10,11... | collective-permute-start | bytes 1130504 | tf_op jit(solution)/shard_map/ppermute | solution.py:365
  54.4 9.5 %collective-permute-start.17 = (bf16[2,32,2944]{2,1,0:T(8,128)(2,1)S(1)}, bf16[2,32,2944]{2,1,0:T(8,128)(2,1)S(1)}, u32[]{:S(2)}, u32[]{:S(2)}) collective-permute-start(bf16[2,32,2944]{2,1,0:T(8,128)(2,1)S(1)} %collective-permute-done.13.hi_ref.refs_1_), channel_id=1, source_target_pairs={{0,1},{1,0},{2,3},{3,2},{4,5},{5,4},{6,7},{7,6},{8,9},{9,8},{10,11... | collective-permute-start | bytes 1130504 | tf_op jit(solution)/shard_map/ppermute | solution.py:365
  54.4 9.5 %collective-permute-start.18 = (bf16[2,16,2944]{2,1,0:T(8,128)(2,1)S(1)}, bf16[2,16,2944]{2,1,0:T(8,128)(2,1)S(1)}, u32[]{:S(2)}, u32[]{:S(2)}) collective-permute-start(bf16[2,16,2944]{2,1,0:T(8,128)(2,1)S(1)} %collective-permute-done.14.refs_2_), channel_id=1, source_target_pairs={{0,1},{1,0},{2,3},{3,2},{4,5},{5,4},{6,7},{7,6},{8,9},{9,8},{10,11... | collective-permute-start | bytes 565256 | tf_op jit(solution)/shard_map/ppermute | solution.py:365
  58.0 5.9 %collective-permute-start.19 = (bf16[2,16,2944]{2,1,0:T(8,128)(2,1)S(1)}, bf16[2,16,2944]{2,1,0:T(8,128)(2,1)S(1)}, u32[]{:S(2)}, u32[]{:S(2)}) collective-permute-start(bf16[2,16,2944]{2,1,0:T(8,128)(2,1)S(1)} %collective-permute-done.15.refs_3_), channel_id=1, source_target_pairs={{0,1},{1,0},{2,3},{3,2},{4,5},{5,4},{6,7},{7,6},{8,9},{9,8},{10,11... | collective-permute-start | bytes 565256 | tf_op jit(solution)/shard_map/ppermute | solution.py:365
  63.6 8.8 %collective-permute-start.20 = (bf16[4,5,8,2880]{3,2,1,0:T(8,128)(2,1)S(1)}, bf16[4,5,8,2880]{3,2,1,0:T(8,128)(2,1)S(1)}, u32[]{:S(2)}, u32[]{:S(2)}) collective-permute-start(bf16[4,5,8,2880]{3,2,1,0:T(8,128)(2,1)S(1)} %get-tuple-element.66), channel_id=1, source_target_pairs={{0,1},{1,0},{2,3},{3,2},{4,5},{5,4},{6,7},{7,6},{8,9},{9,8},{10,11... | collective-permute-start | bytes 2764808 | tf_op jit(solution)/shard_map/ppermute | solution.py:365
  69.5 24.0 %collective-permute-start.29 = (bf16[3,180,720]{2,1,0:T(8,128)(2,1)S(1)}, bf16[3,180,720]{2,1,0:T(8,128)(2,1)S(1)}, u32[]{:S(2)}, u32[]{:S(2)}) collective-permute-start(bf16[3,180,720]{2,1,0:T(8,128)(2,1)S(1)} %get-tuple-element.83.rest_0_), channel_id=1, source_target_pairs={{0,64},{64,128},{128,192},{192,0},{1,65},{65,129},{129,193},{193,1... | collective-permute-start | bytes 2332808 | tf_op jit(solution)/shard_map/ppermute | solution.py:360
  70.8 23.0 %collective-permute-start.32 = (bf16[3,180,720]{2,1,0:T(8,128)(2,1)S(1)}, bf16[3,180,720]{2,1,0:T(8,128)(2,1)S(1)}, u32[]{:S(2)}, u32[]{:S(2)}) collective-permute-start(bf16[3,180,720]{2,1,0:T(8,128)(2,1)S(1)} %get-tuple-element.90), channel_id=1, source_target_pairs={{0,192},{64,0},{128,64},{192,128},{1,193},{65,1},{129,65},{193,129... | collective-permute-start | bytes 2332808 | tf_op jit(solution)/shard_map/ppermute | solution.py:360
  72.7 19.1 %collective-permute-start.22 = (bf16[8,8,2880]{2,1,0:T(8,128)(2,1)S(1)}, bf16[8,8,2880]{2,1,0:T(8,128)(2,1)S(1)}, u32[]{:S(2)}, u32[]{:S(2)}) collective-permute-start(bf16[8,8,2880]{2,1,0:T(8,128)(2,1)S(1)} %get-tuple-element.69), channel_id=1, source_target_pairs={{0,16},{16,32},{32,48},{48,0},{1,17},{17,33},{33,49},{49,1},{2,18}... | collective-permute-start | bytes 1105928 | tf_op jit(solution)/shard_map/ppermute | solution.py:360
  72.8 20.0 %collective-permute-start.23 = (bf16[8,8,2880]{2,1,0:T(8,128)(2,1)S(1)}, bf16[8,8,2880]{2,1,0:T(8,128)(2,1)S(1)}, u32[]{:S(2)}, u32[]{:S(2)}) collective-permute-start(bf16[8,8,2880]{2,1,0:T(8,128)(2,1)S(1)} %get-tuple-element.70), channel_id=1, source_target_pairs={{0,32},{16,48},{32,0},{48,16},{1,33},{17,49},{33,1},{49,17},{2,34}... | collective-permute-start | bytes 1105928 | tf_op jit(solution)/shard_map/ppermute | solution.py:360
  72.9 20.3 %collective-permute-start.24 = (bf16[8,8,2880]{2,1,0:T(8,128)(2,1)S(1)}, bf16[8,8,2880]{2,1,0:T(8,128)(2,1)S(1)}, u32[]{:S(2)}, u32[]{:S(2)}) collective-permute-start(bf16[8,8,2880]{2,1,0:T(8,128)(2,1)S(1)} %get-tuple-element.71), channel_id=1, source_target_pairs={{0,48},{16,0},{32,16},{48,32},{1,49},{17,1},{33,17},{49,33},{2,50}... | collective-permute-start | bytes 1105928 | tf_op jit(solution)/shard_map/ppermute | solution.py:360
  91.8 30.1 %collective-permute-start.28 = (bf16[3,180,720]{2,1,0:T(8,128)(2,1)S(1)}, bf16[3,180,720]{2,1,0:T(8,128)(2,1)S(1)}, u32[]{:S(2)}, u32[]{:S(2)}) collective-permute-start(bf16[3,180,720]{2,1,0:T(8,128)(2,1)S(1)} %get-tuple-element.85), channel_id=1, source_target_pairs={{0,192},{64,0},{128,64},{192,128},{1,193},{65,1},{129,65},{193,129... | collective-permute-start | bytes 2332808 | tf_op jit(solution)/shard_map/ppermute | solution.py:360
  92.8 29.0 %collective-permute-start.31 = (bf16[3,180,720]{2,1,0:T(8,128)(2,1)S(1)}, bf16[3,180,720]{2,1,0:T(8,128)(2,1)S(1)}, u32[]{:S(2)}, u32[]{:S(2)}) collective-permute-start(bf16[3,180,720]{2,1,0:T(8,128)(2,1)S(1)} %get-tuple-element.88), channel_id=1, source_target_pairs={{0,64},{64,128},{128,192},{192,0},{1,65},{65,129},{129,193},{193,1... | collective-permute-start | bytes 2332808 | tf_op jit(solution)/shard_map/ppermute | solution.py:360
  93.7 37.1 %collective-permute-start.30 = (bf16[3,180,720]{2,1,0:T(8,128)(2,1)S(1)}, bf16[3,180,720]{2,1,0:T(8,128)(2,1)S(1)}, u32[]{:S(2)}, u32[]{:S(2)}) collective-permute-start(bf16[3,180,720]{2,1,0:T(8,128)(2,1)S(1)} %add.2), channel_id=1, source_target_pairs={{0,64},{64,128},{128,192},{192,0},{1,65},{65,129},{129,193},{193,1... | collective-permute-start | bytes 2332808 | tf_op jit(solution)/shard_map/ppermute | solution.py:360
  94.0 36.8 %collective-permute-start.33 = (bf16[3,180,720]{2,1,0:T(8,128)(2,1)S(1)}, bf16[3,180,720]{2,1,0:T(8,128)(2,1)S(1)}, u32[]{:S(2)}, u32[]{:S(2)}) collective-permute-start(bf16[3,180,720]{2,1,0:T(8,128)(2,1)S(1)} %add.3), channel_id=1, source_target_pairs={{0,192},{64,0},{128,64},{192,128},{1,193},{65,1},{129,65},{193,129... | collective-permute-start | bytes 2332808 | tf_op jit(solution)/shard_map/ppermute | solution.py:360
  96.7 8.4 %collective-permute-start.25 = (bf16[4,8,2880]{2,1,0:T(8,128)(2,1)S(1)}, bf16[4,8,2880]{2,1,0:T(8,128)(2,1)S(1)}, u32[]{:S(2)}, u32[]{:S(2)}) collective-permute-start(bf16[4,8,2880]{2,1,0:T(8,128)(2,1)S(1)} %get-tuple-element.73), channel_id=1, source_target_pairs={{0,8},{1,9},{2,10},{3,11},{4,12},{5,13},{6,14},{7,15},{8,0},{9,1},... | collective-permute-start | bytes 552968 | tf_op jit(solution)/shard_map/ppermute | solution.py:360
  105.2 11.5 %collective-permute-start.26 = (bf16[2,8,2880]{2,1,0:T(8,128)(2,1)S(1)}, bf16[2,8,2880]{2,1,0:T(8,128)(2,1)S(1)}, u32[]{:S(2)}, u32[]{:S(2)}) collective-permute-start(bf16[2,8,2880]{2,1,0:T(8,128)(2,1)S(1)} %get-tuple-element.75), channel_id=1, source_target_pairs={{0,4},{1,5},{2,6},{3,7},{4,8},{5,9},{6,10},{7,11},{8,12},{9,13},{1... | collective-permute-start | bytes 276488 | tf_op jit(solution)/shard_map/ppermute | solution.py:360
  (5 other events, 19.0 us)

commit v2 on v1

--- a/solution.py
+++ b/solution.py
@@ -189,7 +189,7 @@
 
     def kernel(place_ref, a_ref, b_ref, c_ref, d_ref, *rest):
         del place_ref
-        outs = rest[len(after) :]
+        outs, sums_ref = rest[len(after) : -1], rest[-1]
         act = jnp.concatenate([a_ref[...], b_ref[...]], axis=0)
         for kind in range(3):
             side = kind // 2
@@ -197,12 +197,14 @@
             part = lax.dot_general(
                 act[:, kind * span : (kind + 1) * span], x, tn, preferred_element_type=jnp.float32
             ).astype(jnp.bfloat16)
-            for step in range(count):
-
-                @pl.when(pl.program_id(0) == step)
-                def _(step=step):
-                    for e in range(n_exp):
-                        outs[step * n_exp + e][kind] = part[e * pad : e * pad + hid, :]
+            for e in range(n_exp):
+                sums_ref[e, :, kind * cols : (kind + 1) * cols] = part[e * pad : e * pad + hid, :]
+        for step in range(count):
+
+            @pl.when(pl.program_id(0) == step)
+            def _(step=step):
+                for e in range(n_exp):
+                    outs[step * n_exp + e][...] = sums_ref[e]
 
     def picked(i, w):
         k = offsets[0]
@@ -213,7 +215,7 @@
     fixed = lambda n: (lambda i, w: (0,) * n)
     outs = pl.pallas_call(
         kernel,
-        out_shape=(jax.ShapeDtypeStruct((3, hid, cols), jnp.bfloat16),) * (n_exp * count),
+        out_shape=(jax.ShapeDtypeStruct((hid, 3 * cols), jnp.bfloat16),) * (n_exp * count),
         grid_spec=pltpu.PrefetchScalarGridSpec(
             num_scalar_prefetch=1,
             grid=(count,),
@@ -225,6 +227,7 @@
             ]
             + [pl.BlockSpec(memory_space=pl.ANY)] * len(after),
             out_specs=(VMEM,) * (n_exp * count),
+            scratch_shapes=[pltpu.VMEM((n_exp, hid, 3 * cols), jnp.bfloat16)],
         ),
         compiler_params=pltpu.CompilerParams(vmem_limit_bytes=12 * MIB),
         cost_estimate=pl.CostEstimate(
@@ -237,27 +240,28 @@
 
 def finish(parts):
     n_exp = len(parts)
-    _, hid, cols = parts[0][0].shape
+    hid, cols = parts[0][0].shape[0], parts[0][0].shape[1] // 3
 
     def kernel(*refs):
         outs = refs[-3:]
-        at = 0
-        for e in range(n_exp):
-            mine = refs[at : at + len(parts[e])]
-            at += len(parts[e])
-            for kind in range(3):
-                total = mine[0][kind].astype(jnp.float32)
+        for kind in range(3):
+            span = slice(kind * cols, (kind + 1) * cols)
+            at = 0
+            for e in range(n_exp):
+                mine = refs[at : at + len(parts[e])]
+                at += len(parts[e])
+                total = mine[0][:, span].astype(jnp.float32)
                 for r in mine[1:]:
-                    total = total + r[kind].astype(jnp.float32)
+                    total = total + r[:, span].astype(jnp.float32)
                 outs[kind][:, e, :] = total.astype(jnp.bfloat16)
 
     flat = [a for p in parts for a in p]
     outs = pl.pallas_call(
         kernel,
-        grid=(pl.cdiv(cols, 2 * LANE),),
+        grid=(1,),
         out_shape=(jax.ShapeDtypeStruct((hid, n_exp, cols), jnp.bfloat16),) * 3,
-        in_specs=[pl.BlockSpec((3, hid, 2 * LANE), lambda i: (0, 0, i)) for _ in flat],
-        out_specs=(pl.BlockSpec((hid, n_exp, 2 * LANE), lambda i: (0, 0, i)),) * 3,
+        in_specs=[VMEM] * len(flat),
+        out_specs=(pl.BlockSpec((hid, n_exp, cols), lambda i: (0, 0, 0)),) * 3,
         compiler_params=pltpu.CompilerParams(vmem_limit_bytes=12 * MIB),
         name="finish",
     )(*flat)
@@ -288,8 +292,16 @@
 
 def add(a, b, after):
     def kernel(a_ref, b_ref, _, out_ref):
-        for k in range(a.shape[0]):
-            out_ref[k] = (a_ref[k].astype(jnp.float32) + b_ref[k].astype(jnp.float32)).astype(a.dtype)
+        wide = 4 * LANE
+        steps = a.shape[1] // wide
+
+        @pl.loop(0, steps)
+        def _(i):
+            span = pl.ds(pl.multiple_of(i * wide, wide), wide)
+            out_ref[:, span] = (a_ref[:, span].astype(jnp.float32) + b_ref[:, span].astype(jnp.float32)).astype(a.dtype)
+
+        rest = slice(steps * wide, a.shape[1])
+        out_ref[:, rest] = (a_ref[:, rest].astype(jnp.float32) + b_ref[:, rest].astype(jnp.float32)).astype(a.dtype)
 
     return pl.pallas_call(
         kernel,
@@ -309,11 +321,14 @@
         outs = refs[4:]
         at = 0
         for a_ref, b_ref in zip(refs[:2], refs[2:4]):
-            for j in range(a_ref.shape[1]):
+
+            @pl.loop(0, a_ref.shape[1])
+            def _(j, a_ref=a_ref, b_ref=b_ref, at=at):
                 for k in range(n_group):
                     total = a_ref[k, j].astype(jnp.float32) + b_ref[k, j].astype(jnp.float32)
-                    outs[k][at] = total.astype(jnp.bfloat16)
-                at += 1
+                    outs[k][at + j] = total.astype(jnp.bfloat16)
+
+            at += a_ref.shape[1]
 
     one = jax.ShapeDtypeStruct((chips,) + near[0].shape[2:], near[0].dtype)
     return small(kernel, (one,) * n_group, (*near, *arrived))
@@ -419,9 +434,12 @@
     from_left_1 = shifted(next_1, "dp", -1)
     from_right_0 = shifted(prev_0, "dp", 1)
     kept, sent = by_chip([both[0]] + others)
-    from_left_0 = shifted(add(next_0, right_0, kept), "dp", -1)
-    from_right_1 = shifted(add(prev_1, left_1, kept), "dp", 1)
-    kept, sent = fold(kept, shifted(sent, "member", -8))
+    sent = shifted(sent, "member", -8)
+    joined_0 = add(next_0, right_0, kept)
+    joined_1 = add(prev_1, left_1, kept)
+    from_left_0 = shifted(joined_0, "dp", -1)
+    from_right_1 = shifted(joined_1, "dp", 1)
+    kept, sent = fold(kept, sent)
     kept, sent = fold(kept, shifted(sent, "member", -4))
     grad_tokens = total_of(kept, shifted(sent, "member", -2))
     grads = finish([[here_0, from_right_0, from_left_0], [here_1, from_left_1, from_right_1]])

time: 137 us -> 133 us (0.971)
  Pallas kernels: 25.6 us -> 21.8 us
    pallas_call x3, Pallas kernels: 12.1 us -> 8.3 us  [the longest x2 5.73 us: column_sums(): pl.pallas_call(kernel, out_shape=(jax.ShapeDtypeStruct((hid, 3 * cols), j...]
  transfers between devices with their start and end apart: 34 -> 34, of which waited for: 11 -> 11; matrix products, arithmetic and copies ran while one was open for 2% -> 2% of each run, Pallas kernels for 14% -> 13%
where the time goes in v2:
time: 133 us; the launch traced here: 132 us
  starting transfers between devices  53.5 us (40%)
  waiting for transfers between devices  50.9 us (38%)
  Pallas kernels  21.8 us (16%)
  local copies, waits for them, and re-layouts  4.51 us (3%)
    ppermute x23, waiting for transfers between devices, shifted(): return lax.ppermute(x, axis, [(i, (i - step) % n) for i in range(n)])  50.8 us
    ppermute x23, starting transfers between devices, shifted(): return lax.ppermute(x, axis, [(i, (i - step) % n) for i in range(n)])  38.7 us
    ppermute x11, starting transfers between devices, partner(): return lax.ppermute(x, 'member', [(i, i ^ 1) for i in range(n)])  14.8 us
    pallas_call x2, Pallas kernels, forward(): pl.pallas_call(kernel, out_shape=(jax.ShapeDtypeStruct((tall, 3 * span),...  9.35 us
    pallas_call x2, Pallas kernels, column_sums(): pl.pallas_call(kernel, out_shape=(jax.ShapeDtypeStruct((hid, 3 * cols), j...  5.73 us
    unnamed x9, local copies, waits for them, and re-layouts  4.51 us
  transfers between devices with their start and end apart: 34, of which 11 were waited for; matrix products, arithmetic and copies ran while one was open for 2% of the time, Pallas kernels for 13%

profile of v2, /device:TPU:1, one launch (start us, length us, event | category | flops | bytes accessed | tf_op | source)
XLA Modules:
  0.0 131.5 jit_solution(14039762713014953808)
XLA Ops:
  0.6 1.7 %prepare.1.refs_0_ = bf16[2,8,2944]{2,1,0:T(8,128)(2,1)} custom-call(bf16[8,2880]{1,0:T(8,128)(2,1)} %refs_0_.1, bf16[8,2880]{1,0:T(8,128)(2,1)} %refs_1_.1, s32[4,8]{1,0:T(4,128)} %bitcast.7, f32[4,8]{1,0:T(4,128)} %bitcast.8), custom_call_target="tpu_custom_call" | custom-call | tf_op jit(solution)/shard_map/prepare/pallas_call | solution.py:51
  2.3 3.6 %collective-permute-start = (bf16[2,8,2944]{2,1,0:T(8,128)(2,1)}, bf16[2,8,2944]{2,1,0:T(8,128)(2,1)S(1)}, u32[]{:S(2)}, u32[]{:S(2)}) collective-permute-start(bf16[2,8,2944]{2,1,0:T(8,128)(2,1)} %prepare.1.refs_0_), channel_id=1, source_target_pairs={{0,48},{16,0},{32,16},{48,32},{1,49},{17,1},{33,17},{49,33},{2,50}... | collective-permute-start | bytes 282632 | tf_op jit(solution)/shard_map/ppermute | solution.py:375
  7.9 3.3 %collective-permute-done.1.refs_2_ = bf16[2,8,2944]{2,1,0:T(8,128)(2,1)S(1)} collective-permute-done((bf16[2,8,2944]{2,1,0:T(8,128)(2,1)}, bf16[2,8,2944]{2,1,0:T(8,128)(2,1)S(1)}, u32[]{:S(2)}, u32[]{:S(2)}) %collective-permute-start.1) | collective-permute-done | bytes 94240 | tf_op jit(solution)/shard_map/ppermute | solution.py:375
  11.2 2.6 %collective-permute-done.2.refs_3_ = bf16[2,8,2944]{2,1,0:T(8,128)(2,1)S(1)} collective-permute-done((bf16[2,8,2944]{2,1,0:T(8,128)(2,1)}, bf16[2,8,2944]{2,1,0:T(8,128)(2,1)S(1)}, u32[]{:S(2)}, u32[]{:S(2)}) %collective-permute-start.2) | collective-permute-done | bytes 94240 | tf_op jit(solution)/shard_map/ppermute | solution.py:375
  14.8 1.7 %collective-permute-start.3 = (bf16[2,32,2944]{2,1,0:T(8,128)(2,1)S(1)}, bf16[2,32,2944]{2,1,0:T(8,128)(2,1)S(1)}, u32[]{:S(2)}, u32[]{:S(2)}) collective-permute-start(bf16[2,32,2944]{2,1,0:T(8,128)(2,1)S(1)} %join.1.refs_0_), channel_id=1, source_target_pairs={{0,2},{1,3},{2,4},{3,5},{4,6},{5,7},{6,8},{7,9},{8,10},{9,11},{10,... | collective-permute-start | bytes 1130504 | tf_op jit(solution)/shard_map/ppermute | solution.py:375
  16.5 4.0 %collective-permute-start.4 = (bf16[2,32,2944]{2,1,0:T(8,128)(2,1)S(1)}, bf16[2,32,2944]{2,1,0:T(8,128)(2,1)S(1)}, u32[]{:S(2)}, u32[]{:S(2)}) collective-permute-start(bf16[2,32,2944]{2,1,0:T(8,128)(2,1)S(1)} %join.1.refs_0_), channel_id=1, source_target_pairs={{0,14},{1,15},{2,0},{3,1},{4,2},{5,3},{6,4},{7,5},{8,6},{9,7},{10,... | collective-permute-start | bytes 1130504 | tf_op jit(solution)/shard_map/ppermute | solution.py:375
  20.5 1.8 %copy.11.g_ref = bf16[2,180,2880]{2,1,0:T(8,128)(2,1)S(1)} copy(bf16[2,180,2880]{2,0,1:T(2,128)(2,1)} %param.11) | data formatting | bytes 4147200 | tf_op args[4]
  22.6 1.4 %copy-done.2 = bf16[2,180,2880]{2,0,1:T(2,128)(2,1)S(1)} copy-done((bf16[2,180,2880]{2,0,1:T(2,128)(2,1)S(1)}, bf16[2,180,2880]{2,0,1:T(2,128)(2,1)}, u32[]{:S(2)}) %copy-start.2) | copy-done | bytes 2073624
  26.2 2.4 %collective-permute-done.3.refs_1_ = bf16[2,32,2944]{2,1,0:T(8,128)(2,1)S(1)} collective-permute-done((bf16[2,32,2944]{2,1,0:T(8,128)(2,1)S(1)}, bf16[2,32,2944]{2,1,0:T(8,128)(2,1)S(1)}, u32[]{:S(2)}, u32[]{:S(2)}) %collective-permute-start.3) | collective-permute-done | bytes 376864 | tf_op jit(solution)/shard_map/ppermute | solution.py:375
  28.6 2.7 %collective-permute-start.6 = (bf16[2,32,2944]{2,1,0:T(8,128)(2,1)S(1)}, bf16[2,32,2944]{2,1,0:T(8,128)(2,1)S(1)}, u32[]{:S(2)}, u32[]{:S(2)}) collective-permute-start(bf16[2,32,2944]{2,1,0:T(8,128)(2,1)S(1)} %collective-permute-done.4.refs_2_), channel_id=1, source_target_pairs={{0,14},{1,15},{2,0},{3,1},{4,2},{5,3},{6,4},{7,5},{8,6},{9,7},{10,... | collective-permute-start | bytes 1130504 | tf_op jit(solution)/shard_map/ppermute | solution.py:375
  31.3 2.1 %collective-permute-start.8 = (bf16[2,32,2944]{2,1,0:T(8,128)(2,1)S(1)}, bf16[2,32,2944]{2,1,0:T(8,128)(2,1)S(1)}, u32[]{:S(2)}, u32[]{:S(2)}) collective-permute-start(bf16[2,32,2944]{2,1,0:T(8,128)(2,1)S(1)} %collective-permute-done.3.refs_1_), channel_id=1, source_target_pairs={{0,1},{1,0},{2,3},{3,2},{4,5},{5,4},{6,7},{7,6},{8,9},{9,8},{10,11... | collective-permute-start | bytes 1130504 | tf_op jit(solution)/shard_map/ppermute | solution.py:380
  33.4 5.2 %collective-permute-done.5.refs_3_ = bf16[2,32,2944]{2,1,0:T(8,128)(2,1)S(1)} collective-permute-done((bf16[2,32,2944]{2,1,0:T(8,128)(2,1)S(1)}, bf16[2,32,2944]{2,1,0:T(8,128)(2,1)S(1)}, u32[]{:S(2)}, u32[]{:S(2)}) %collective-permute-start.5) | collective-permute-done | bytes 376864 | tf_op jit(solution)/shard_map/ppermute | solution.py:375
  39.6 1.7 %collective-permute-start.13 = (bf16[2,32,2944]{2,1,0:T(8,128)(2,1)S(1)}, bf16[2,32,2944]{2,1,0:T(8,128)(2,1)S(1)}, u32[]{:S(2)}, u32[]{:S(2)}) collective-permute-start(bf16[2,32,2944]{2,1,0:T(8,128)(2,1)S(1)} %collective-permute-done.6.refs_4_), channel_id=1, source_target_pairs={{0,14},{1,15},{2,0},{3,1},{4,2},{5,3},{6,4},{7,5},{8,6},{9,7},{10,... | collective-permute-start | bytes 1130504 | tf_op jit(solution)/shard_map/ppermute | solution.py:375
  41.3 3.0 %collective-permute-start.10 = (bf16[2,32,2944]{2,1,0:T(8,128)(2,1)S(1)}, bf16[2,32,2944]{2,1,0:T(8,128)(2,1)S(1)}, u32[]{:S(2)}, u32[]{:S(2)}) collective-permute-start(bf16[2,32,2944]{2,1,0:T(8,128)(2,1)S(1)} %collective-permute-done.5.refs_3_), channel_id=1, source_target_pairs={{0,1},{1,0},{2,3},{3,2},{4,5},{5,4},{6,7},{7,6},{8,9},{9,8},{10,11... | collective-permute-start | bytes 1130504 | tf_op jit(solution)/shard_map/ppermute | solution.py:380
  44.3 3.5 %collective-permute-done.12.lo_ref.refs_0_ = bf16[2,32,2944]{2,1,0:T(8,128)(2,1)S(1)} collective-permute-done((bf16[2,32,2944]{2,1,0:T(8,128)(2,1)S(1)}, bf16[2,32,2944]{2,1,0:T(8,128)(2,1)S(1)}, u32[]{:S(2)}, u32[]{:S(2)}) %collective-permute-start.12) | collective-permute-done | bytes 376864 | tf_op jit(solution)/shard_map/ppermute | solution.py:375
  48.4 2.2 %collective-permute-start.15 = (bf16[2,16,2944]{2,1,0:T(8,128)(2,1)S(1)}, bf16[2,16,2944]{2,1,0:T(8,128)(2,1)S(1)}, u32[]{:S(2)}, u32[]{:S(2)}) collective-permute-start(bf16[2,16,2944]{2,1,0:T(8,128)(2,1)S(1)} %get-tuple-element.64), channel_id=1, source_target_pairs={{0,14},{1,15},{2,0},{3,1},{4,2},{5,3},{6,4},{7,5},{8,6},{9,7},{10,... | collective-permute-start | bytes 565256 | tf_op jit(solution)/shard_map/ppermute | solution.py:375
  50.6 3.8 %collective-permute-start.16 = (bf16[2,32,2944]{2,1,0:T(8,128)(2,1)S(1)}, bf16[2,32,2944]{2,1,0:T(8,128)(2,1)S(1)}, u32[]{:S(2)}, u32[]{:S(2)}) collective-permute-start(bf16[2,32,2944]{2,1,0:T(8,128)(2,1)S(1)} %collective-permute-done.12.lo_ref.refs_0_), channel_id=1, source_target_pairs={{0,1},{1,0},{2,3},{3,2},{4,5},{5,4},{6,7},{7,6},{8,9},{9,8},{10,11... | collective-permute-start | bytes 1130504 | tf_op jit(solution)/shard_map/ppermute | solution.py:380
  54.4 3.5 %collective-permute-start.18 = (bf16[2,16,2944]{2,1,0:T(8,128)(2,1)S(1)}, bf16[2,16,2944]{2,1,0:T(8,128)(2,1)S(1)}, u32[]{:S(2)}, u32[]{:S(2)}) collective-permute-start(bf16[2,16,2944]{2,1,0:T(8,128)(2,1)S(1)} %collective-permute-done.14.refs_2_), channel_id=1, source_target_pairs={{0,1},{1,0},{2,3},{3,2},{4,5},{5,4},{6,7},{7,6},{8,9},{9,8},{10,11... | collective-permute-start | bytes 565256 | tf_op jit(solution)/shard_map/ppermute | solution.py:380
  58.3 5.3 %forward.2 = (bf16[320,1152]{1,0:T(8,128)(2,1)S(1)}, bf16[4,5,8,2880]{3,2,1,0:T(8,128)(2,1)S(1)}, bf16[4,5,8,2880]{3,2,1,0:T(8,128)(2,1)S(1)}, bf16[2,4,320,720]{3,2,1,0:T(8,128)(2,1)S(1)}) custom-call(s32[1]{0:T(128)} %bitcast.3.first_ref, bf16[2,32,2944]{2,1,0:T(8,128)(2,1)S(1)} %join.1.refs_0_, bf16[2,32,2944]{2,1,0:T(8,128)(2,1)S(1)} %collective-permute-done.3.refs_1_, ...), custom_call_target="tpu_custom_call" | custom-call | flops 3538944000 | bytes 12582912 | tf_op jit(solution)/shard_map/forward/pallas_call | solution.py:165
  63.9 4.0 %forward.3 = (bf16[192,1152]{1,0:T(8,128)(2,1)S(1)}, bf16[4,3,8,2880]{3,2,1,0:T(8,128)(2,1)S(1)}, bf16[4,3,8,2880]{3,2,1,0:T(8,128)(2,1)S(1)}, bf16[2,4,192,720]{3,2,1,0:T(8,128)(2,1)S(1)}) custom-call(s32[1]{0:T(128)} %bitcast.3.first_ref, bf16[2,32,2944]{2,1,0:T(8,128)(2,1)S(1)} %collective-permute-done.12.lo_ref.refs_0_, ...), custom_call_target="tpu_custom_call" | custom-call | flops 2123366400 | bytes 12582912 | tf_op jit(solution)/shard_map/forward/pallas_call | solution.py:165
  71.0 1.6 %collective-permute-start.32 = (bf16[180,2160]{1,0:T(8,128)(2,1)S(1)}, bf16[180,2160]{1,0:T(8,128)(2,1)S(1)}, u32[]{:S(2)}, u32[]{:S(2)}) collective-permute-start(bf16[180,2160]{1,0:T(8,128)(2,1)S(1)} %get-tuple-element.90), channel_id=1, source_target_pairs={{0,192},{64,0},{128,64},{192,128},{1,193},{65,1},{129,65},{193,129... | collective-permute-start | bytes 2332808 | tf_op jit(solution)/shard_map/ppermute | solution.py:375
  73.1 2.6 %collective-permute-start.24 = (bf16[8,8,2880]{2,1,0:T(8,128)(2,1)S(1)}, bf16[8,8,2880]{2,1,0:T(8,128)(2,1)S(1)}, u32[]{:S(2)}, u32[]{:S(2)}) collective-permute-start(bf16[8,8,2880]{2,1,0:T(8,128)(2,1)S(1)} %get-tuple-element.71), channel_id=1, source_target_pairs={{0,48},{16,0},{32,16},{48,32},{1,49},{17,1},{33,17},{49,33},{2,50}... | collective-permute-start | bytes 1105928 | tf_op jit(solution)/shard_map/ppermute | solution.py:375
  75.7 4.4 %column_sums.3 = (bf16[180,2160]{1,0:T(8,128)(2,1)S(1)}, bf16[180,2160]{1,0:T(8,128)(2,1)S(1)}, bf16[180,2160]{1,0:T(8,128)(2,1)S(1)}, bf16[180,2160]{1,0:T(8,12...) custom-call(s32[1]{0:T(128)} %bitcast.2.place_ref, ...), custom_call_target="tpu_custom_call" | custom-call | flops 2548039680 | bytes 12582912 | tf_op jit(solution)/shard_map/column_sums/pallas_call | solution.py:216
  80.1 11.9 %collective-permute-done.22.refs_1_ = bf16[8,8,2880]{2,1,0:T(8,128)(2,1)S(1)} collective-permute-done((bf16[8,8,2880]{2,1,0:T(8,128)(2,1)S(1)}, bf16[8,8,2880]{2,1,0:T(8,128)(2,1)S(1)}, u32[]{:S(2)}, u32[]{:S(2)}) %collective-permute-start.22) | collective-permute-done | bytes 368672 | tf_op jit(solution)/shard_map/ppermute | solution.py:375
  94.2 2.7 %collective-permute-start.33 = (bf16[180,2160]{1,0:T(8,128)(2,1)S(1)}, bf16[180,2160]{1,0:T(8,128)(2,1)S(1)}, u32[]{:S(2)}, u32[]{:S(2)}) collective-permute-start(bf16[180,2160]{1,0:T(8,128)(2,1)S(1)} %add.3), channel_id=1, source_target_pairs={{0,192},{64,0},{128,64},{192,128},{1,193},{65,1},{129,65},{193,129... | collective-permute-start | bytes 2332808 | tf_op jit(solution)/shard_map/ppermute | solution.py:375
  96.9 2.9 %collective-permute-start.25 = (bf16[4,8,2880]{2,1,0:T(8,128)(2,1)S(1)}, bf16[4,8,2880]{2,1,0:T(8,128)(2,1)S(1)}, u32[]{:S(2)}, u32[]{:S(2)}) collective-permute-start(bf16[4,8,2880]{2,1,0:T(8,128)(2,1)S(1)} %get-tuple-element.73), channel_id=1, source_target_pairs={{0,8},{1,9},{2,10},{3,11},{4,12},{5,13},{6,14},{7,15},{8,0},{9,1},... | collective-permute-start | bytes 552968 | tf_op jit(solution)/shard_map/ppermute | solution.py:375
  99.8 5.6 %collective-permute-done.25.b_ref = bf16[4,8,2880]{2,1,0:T(8,128)(2,1)S(1)} collective-permute-done((bf16[4,8,2880]{2,1,0:T(8,128)(2,1)S(1)}, bf16[4,8,2880]{2,1,0:T(8,128)(2,1)S(1)}, u32[]{:S(2)}, u32[]{:S(2)}) %collective-permute-start.25) | collective-permute-done | bytes 184352 | tf_op jit(solution)/shard_map/ppermute | solution.py:375
  105.4 7.3 %collective-permute-start.26 = (bf16[2,8,2880]{2,1,0:T(8,128)(2,1)S(1)}, bf16[2,8,2880]{2,1,0:T(8,128)(2,1)S(1)}, u32[]{:S(2)}, u32[]{:S(2)}) collective-permute-start(bf16[2,8,2880]{2,1,0:T(8,128)(2,1)S(1)} %get-tuple-element.75), channel_id=1, source_target_pairs={{0,4},{1,5},{2,6},{3,7},{4,8},{5,9},{6,10},{7,11},{8,12},{9,13},{1... | collective-permute-start | bytes 276488 | tf_op jit(solution)/shard_map/ppermute | solution.py:375
  112.7 4.3 %collective-permute-done.26.b_ref = bf16[2,8,2880]{2,1,0:T(8,128)(2,1)S(1)} collective-permute-done((bf16[2,8,2880]{2,1,0:T(8,128)(2,1)S(1)}, bf16[2,8,2880]{2,1,0:T(8,128)(2,1)S(1)}, u32[]{:S(2)}, u32[]{:S(2)}) %collective-permute-start.26) | collective-permute-done | bytes 92192 | tf_op jit(solution)/shard_map/ppermute | solution.py:375
  117.1 4.4 %collective-permute-done.27.b_ref = bf16[1,8,2880]{2,1,0:T(8,128)(2,1)S(1)} collective-permute-done((bf16[1,8,2880]{2,1,0:T(8,128)(2,1)S(1)}, bf16[1,8,2880]{2,1,0:T(8,128)(2,1)S(1)}, u32[]{:S(2)}, u32[]{:S(2)}) %collective-permute-start.27) | collective-permute-done | bytes 46112 | tf_op jit(solution)/shard_map/ppermute | solution.py:375
  122.1 6.8 %collective-permute-done.30.refs_2_ = bf16[180,2160]{1,0:T(8,128)(2,1)S(1)} collective-permute-done((bf16[180,2160]{1,0:T(8,128)(2,1)S(1)}, bf16[180,2160]{1,0:T(8,128)(2,1)S(1)}, u32[]{:S(2)}, u32[]{:S(2)}) %collective-permute-start.30) | collective-permute-done | bytes 777632 | tf_op jit(solution)/shard_map/ppermute | solution.py:375
  128.9 2.6 %finish.1 = (bf16[180,2,720]{2,1,0:T(2,128)(2,1)}, bf16[180,2,720]{2,1,0:T(2,128)(2,1)}, bf16[180,2,720]{2,1,0:T(2,128)(2,1)}) custom-call(bf16[180,2160]{1,0:T(8,128)(2,1)S(1)} %get-tuple-element.84.refs_0_, bf16[180,2160]{1,0:T(8,128)(2,1)S(1)} %collective-permute-done.28.refs_1_, bf16[180,2160]{1,0:T(8,128)(2,1)S(1)} %collective-permute-done.30.refs_2_, ...), custom_call_target="tpu_custom_call" | custom-call | tf_op jit(solution)/shard_map/finish/pallas_call | solution.py:259
  (61 shorter events, 14.2 us)
Async XLA Ops:
  2.3 5.5 %collective-permute-start = (bf16[2,8,2944]{2,1,0:T(8,128)(2,1)}, bf16[2,8,2944]{2,1,0:T(8,128)(2,1)S(1)}, u32[]{:S(2)}, u32[]{:S(2)}) collective-permute-start(bf16[2,8,2944]{2,1,0:T(8,128)(2,1)} %prepare.1.refs_0_), channel_id=1, source_target_pairs={{0,48},{16,0},{32,16},{48,32},{1,49},{17,1},{33,17},{49,33},{2,50}... | collective-permute-start | bytes 282632 | tf_op jit(solution)/shard_map/ppermute | solution.py:375
  5.9 5.2 %collective-permute-start.1 = (bf16[2,8,2944]{2,1,0:T(8,128)(2,1)}, bf16[2,8,2944]{2,1,0:T(8,128)(2,1)S(1)}, u32[]{:S(2)}, u32[]{:S(2)}) collective-permute-start(bf16[2,8,2944]{2,1,0:T(8,128)(2,1)} %prepare.1.refs_0_), channel_id=1, source_target_pairs={{0,32},{16,48},{32,0},{48,16},{1,33},{17,49},{33,1},{49,17},{2,34}... | collective-permute-start | bytes 282632 | tf_op jit(solution)/shard_map/ppermute | solution.py:375
  6.3 7.5 %collective-permute-start.2 = (bf16[2,8,2944]{2,1,0:T(8,128)(2,1)}, bf16[2,8,2944]{2,1,0:T(8,128)(2,1)S(1)}, u32[]{:S(2)}, u32[]{:S(2)}) collective-permute-start(bf16[2,8,2944]{2,1,0:T(8,128)(2,1)} %prepare.1.refs_0_), channel_id=1, source_target_pairs={{0,16},{16,32},{32,48},{48,0},{1,17},{17,33},{33,49},{49,1},{2,18}... | collective-permute-start | bytes 282632 | tf_op jit(solution)/shard_map/ppermute | solution.py:375
  14.8 13.8 %collective-permute-start.3 = (bf16[2,32,2944]{2,1,0:T(8,128)(2,1)S(1)}, bf16[2,32,2944]{2,1,0:T(8,128)(2,1)S(1)}, u32[]{:S(2)}, u32[]{:S(2)}) collective-permute-start(bf16[2,32,2944]{2,1,0:T(8,128)(2,1)S(1)} %join.1.refs_0_), channel_id=1, source_target_pairs={{0,2},{1,3},{2,4},{3,5},{4,6},{5,7},{6,8},{7,9},{8,10},{9,11},{10,... | collective-permute-start | bytes 1130504 | tf_op jit(solution)/shard_map/ppermute | solution.py:375
  16.5 12.1 %collective-permute-start.4 = (bf16[2,32,2944]{2,1,0:T(8,128)(2,1)S(1)}, bf16[2,32,2944]{2,1,0:T(8,128)(2,1)S(1)}, u32[]{:S(2)}, u32[]{:S(2)}) collective-permute-start(bf16[2,32,2944]{2,1,0:T(8,128)(2,1)S(1)} %join.1.refs_0_), channel_id=1, source_target_pairs={{0,14},{1,15},{2,0},{3,1},{4,2},{5,3},{6,4},{7,5},{8,6},{9,7},{10,... | collective-permute-start | bytes 1130504 | tf_op jit(solution)/shard_map/ppermute | solution.py:375
  24.9 8.5 %collective-permute-start.7 = (bf16[2,32,2944]{2,1,0:T(8,128)(2,1)S(1)}, bf16[2,32,2944]{2,1,0:T(8,128)(2,1)S(1)}, u32[]{:S(2)}, u32[]{:S(2)}) collective-permute-start(bf16[2,32,2944]{2,1,0:T(8,128)(2,1)S(1)} %join.1.refs_0_), channel_id=1, source_target_pairs={{0,1},{1,0},{2,3},{3,2},{4,5},{5,4},{6,7},{7,6},{8,9},{9,8},{10,11... | collective-permute-start | bytes 1130504 | tf_op jit(solution)/shard_map/ppermute | solution.py:380
  28.6 10.0 %collective-permute-start.5 = (bf16[2,32,2944]{2,1,0:T(8,128)(2,1)S(1)}, bf16[2,32,2944]{2,1,0:T(8,128)(2,1)S(1)}, u32[]{:S(2)}, u32[]{:S(2)}) collective-permute-start(bf16[2,32,2944]{2,1,0:T(8,128)(2,1)S(1)} %collective-permute-done.3.refs_1_), channel_id=1, source_target_pairs={{0,2},{1,3},{2,4},{3,5},{4,6},{5,7},{6,8},{7,9},{8,10},{9,11},{10,... | collective-permute-start | bytes 1130504 | tf_op jit(solution)/shard_map/ppermute | solution.py:375
  28.6 10.0 %collective-permute-start.6 = (bf16[2,32,2944]{2,1,0:T(8,128)(2,1)S(1)}, bf16[2,32,2944]{2,1,0:T(8,128)(2,1)S(1)}, u32[]{:S(2)}, u32[]{:S(2)}) collective-permute-start(bf16[2,32,2944]{2,1,0:T(8,128)(2,1)S(1)} %collective-permute-done.4.refs_2_), channel_id=1, source_target_pairs={{0,14},{1,15},{2,0},{3,1},{4,2},{5,3},{6,4},{7,5},{8,6},{9,7},{10,... | collective-permute-start | bytes 1130504 | tf_op jit(solution)/shard_map/ppermute | solution.py:375
  31.3 7.3 %collective-permute-start.8 = (bf16[2,32,2944]{2,1,0:T(8,128)(2,1)S(1)}, bf16[2,32,2944]{2,1,0:T(8,128)(2,1)S(1)}, u32[]{:S(2)}, u32[]{:S(2)}) collective-permute-start(bf16[2,32,2944]{2,1,0:T(8,128)(2,1)S(1)} %collective-permute-done.3.refs_1_), channel_id=1, source_target_pairs={{0,1},{1,0},{2,3},{3,2},{4,5},{5,4},{6,7},{7,6},{8,9},{9,8},{10,11... | collective-permute-start | bytes 1130504 | tf_op jit(solution)/shard_map/ppermute | solution.py:380
  33.4 5.2 %collective-permute-start.9 = (bf16[2,32,2944]{2,1,0:T(8,128)(2,1)S(1)}, bf16[2,32,2944]{2,1,0:T(8,128)(2,1)S(1)}, u32[]{:S(2)}, u32[]{:S(2)}) collective-permute-start(bf16[2,32,2944]{2,1,0:T(8,128)(2,1)S(1)} %collective-permute-done.4.refs_2_), channel_id=1, source_target_pairs={{0,1},{1,0},{2,3},{3,2},{4,5},{5,4},{6,7},{7,6},{8,9},{9,8},{10,11... | collective-permute-start | bytes 1130504 | tf_op jit(solution)/shard_map/ppermute | solution.py:380
  38.6 9.2 %collective-permute-start.12 = (bf16[2,32,2944]{2,1,0:T(8,128)(2,1)S(1)}, bf16[2,32,2944]{2,1,0:T(8,128)(2,1)S(1)}, u32[]{:S(2)}, u32[]{:S(2)}) collective-permute-start(bf16[2,32,2944]{2,1,0:T(8,128)(2,1)S(1)} %collective-permute-done.5.refs_3_), channel_id=1, source_target_pairs={{0,2},{1,3},{2,4},{3,5},{4,6},{5,7},{6,8},{7,9},{8,10},{9,11},{10,... | collective-permute-start | bytes 1130504 | tf_op jit(solution)/shard_map/ppermute | solution.py:375
  39.6 8.2 %collective-permute-start.13 = (bf16[2,32,2944]{2,1,0:T(8,128)(2,1)S(1)}, bf16[2,32,2944]{2,1,0:T(8,128)(2,1)S(1)}, u32[]{:S(2)}, u32[]{:S(2)}) collective-permute-start(bf16[2,32,2944]{2,1,0:T(8,128)(2,1)S(1)} %collective-permute-done.6.refs_4_), channel_id=1, source_target_pairs={{0,14},{1,15},{2,0},{3,1},{4,2},{5,3},{6,4},{7,5},{8,6},{9,7},{10,... | collective-permute-start | bytes 1130504 | tf_op jit(solution)/shard_map/ppermute | solution.py:375
  41.3 13.1 %collective-permute-start.10 = (bf16[2,32,2944]{2,1,0:T(8,128)(2,1)S(1)}, bf16[2,32,2944]{2,1,0:T(8,128)(2,1)S(1)}, u32[]{:S(2)}, u32[]{:S(2)}) collective-permute-start(bf16[2,32,2944]{2,1,0:T(8,128)(2,1)S(1)} %collective-permute-done.5.refs_3_), channel_id=1, source_target_pairs={{0,1},{1,0},{2,3},{3,2},{4,5},{5,4},{6,7},{7,6},{8,9},{9,8},{10,11... | collective-permute-start | bytes 1130504 | tf_op jit(solution)/shard_map/ppermute | solution.py:380
  44.3 14.0 %collective-permute-start.11 = (bf16[2,32,2944]{2,1,0:T(8,128)(2,1)S(1)}, bf16[2,32,2944]{2,1,0:T(8,128)(2,1)S(1)}, u32[]{:S(2)}, u32[]{:S(2)}) collective-permute-start(bf16[2,32,2944]{2,1,0:T(8,128)(2,1)S(1)} %collective-permute-done.6.refs_4_), channel_id=1, source_target_pairs={{0,1},{1,0},{2,3},{3,2},{4,5},{5,4},{6,7},{7,6},{8,9},{9,8},{10,11... | collective-permute-start | bytes 1130504 | tf_op jit(solution)/shard_map/ppermute | solution.py:380
  47.8 6.6 %collective-permute-start.14 = (bf16[2,16,2944]{2,1,0:T(8,128)(2,1)S(1)}, bf16[2,16,2944]{2,1,0:T(8,128)(2,1)S(1)}, u32[]{:S(2)}, u32[]{:S(2)}) collective-permute-start(bf16[2,16,2944]{2,1,0:T(8,128)(2,1)S(1)} %get-tuple-element.63), channel_id=1, source_target_pairs={{0,2},{1,3},{2,4},{3,5},{4,6},{5,7},{6,8},{7,9},{8,10},{9,11},{10,... | collective-permute-start | bytes 565256 | tf_op jit(solution)/shard_map/ppermute | solution.py:375
  48.4 9.6 %collective-permute-start.15 = (bf16[2,16,2944]{2,1,0:T(8,128)(2,1)S(1)}, bf16[2,16,2944]{2,1,0:T(8,128)(2,1)S(1)}, u32[]{:S(2)}, u32[]{:S(2)}) collective-permute-start(bf16[2,16,2944]{2,1,0:T(8,128)(2,1)S(1)} %get-tuple-element.64), channel_id=1, source_target_pairs={{0,14},{1,15},{2,0},{3,1},{4,2},{5,3},{6,4},{7,5},{8,6},{9,7},{10,... | collective-permute-start | bytes 565256 | tf_op jit(solution)/shard_map/ppermute | solution.py:375
  50.6 13.3 %collective-permute-start.16 = (bf16[2,32,2944]{2,1,0:T(8,128)(2,1)S(1)}, bf16[2,32,2944]{2,1,0:T(8,128)(2,1)S(1)}, u32[]{:S(2)}, u32[]{:S(2)}) collective-permute-start(bf16[2,32,2944]{2,1,0:T(8,128)(2,1)S(1)} %collective-permute-done.12.lo_ref.refs_0_), channel_id=1, source_target_pairs={{0,1},{1,0},{2,3},{3,2},{4,5},{5,4},{6,7},{7,6},{8,9},{9,8},{10,11... | collective-permute-start | bytes 1130504 | tf_op jit(solution)/shard_map/ppermute | solution.py:380
  54.4 9.5 %collective-permute-start.17 = (bf16[2,32,2944]{2,1,0:T(8,128)(2,1)S(1)}, bf16[2,32,2944]{2,1,0:T(8,128)(2,1)S(1)}, u32[]{:S(2)}, u32[]{:S(2)}) collective-permute-start(bf16[2,32,2944]{2,1,0:T(8,128)(2,1)S(1)} %collective-permute-done.13.hi_ref.refs_1_), channel_id=1, source_target_pairs={{0,1},{1,0},{2,3},{3,2},{4,5},{5,4},{6,7},{7,6},{8,9},{9,8},{10,11... | collective-permute-start | bytes 1130504 | tf_op jit(solution)/shard_map/ppermute | solution.py:380
  54.4 9.5 %collective-permute-start.18 = (bf16[2,16,2944]{2,1,0:T(8,128)(2,1)S(1)}, bf16[2,16,2944]{2,1,0:T(8,128)(2,1)S(1)}, u32[]{:S(2)}, u32[]{:S(2)}) collective-permute-start(bf16[2,16,2944]{2,1,0:T(8,128)(2,1)S(1)} %collective-permute-done.14.refs_2_), channel_id=1, source_target_pairs={{0,1},{1,0},{2,3},{3,2},{4,5},{5,4},{6,7},{7,6},{8,9},{9,8},{10,11... | collective-permute-start | bytes 565256 | tf_op jit(solution)/shard_map/ppermute | solution.py:380
  58.0 5.9 %collective-permute-start.19 = (bf16[2,16,2944]{2,1,0:T(8,128)(2,1)S(1)}, bf16[2,16,2944]{2,1,0:T(8,128)(2,1)S(1)}, u32[]{:S(2)}, u32[]{:S(2)}) collective-permute-start(bf16[2,16,2944]{2,1,0:T(8,128)(2,1)S(1)} %collective-permute-done.15.refs_3_), channel_id=1, source_target_pairs={{0,1},{1,0},{2,3},{3,2},{4,5},{5,4},{6,7},{7,6},{8,9},{9,8},{10,11... | collective-permute-start | bytes 565256 | tf_op jit(solution)/shard_map/ppermute | solution.py:380
  63.6 9.0 %collective-permute-start.20 = (bf16[4,5,8,2880]{3,2,1,0:T(8,128)(2,1)S(1)}, bf16[4,5,8,2880]{3,2,1,0:T(8,128)(2,1)S(1)}, u32[]{:S(2)}, u32[]{:S(2)}) collective-permute-start(bf16[4,5,8,2880]{3,2,1,0:T(8,128)(2,1)S(1)} %get-tuple-element.66), channel_id=1, source_target_pairs={{0,1},{1,0},{2,3},{3,2},{4,5},{5,4},{6,7},{7,6},{8,9},{9,8},{10,11... | collective-permute-start | bytes 2764808 | tf_op jit(solution)/shard_map/ppermute | solution.py:380
  69.7 24.0 %collective-permute-start.29 = (bf16[180,2160]{1,0:T(8,128)(2,1)S(1)}, bf16[180,2160]{1,0:T(8,128)(2,1)S(1)}, u32[]{:S(2)}, u32[]{:S(2)}) collective-permute-start(bf16[180,2160]{1,0:T(8,128)(2,1)S(1)} %get-tuple-element.83.rest_0_), channel_id=1, source_target_pairs={{0,64},{64,128},{128,192},{192,0},{1,65},{65,129},{129,193},{193,1... | collective-permute-start | bytes 2332808 | tf_op jit(solution)/shard_map/ppermute | solution.py:375
  71.0 23.0 %collective-permute-start.32 = (bf16[180,2160]{1,0:T(8,128)(2,1)S(1)}, bf16[180,2160]{1,0:T(8,128)(2,1)S(1)}, u32[]{:S(2)}, u32[]{:S(2)}) collective-permute-start(bf16[180,2160]{1,0:T(8,128)(2,1)S(1)} %get-tuple-element.90), channel_id=1, source_target_pairs={{0,192},{64,0},{128,64},{192,128},{1,193},{65,1},{129,65},{193,129... | collective-permute-start | bytes 2332808 | tf_op jit(solution)/shard_map/ppermute | solution.py:375
  72.9 19.1 %collective-permute-start.22 = (bf16[8,8,2880]{2,1,0:T(8,128)(2,1)S(1)}, bf16[8,8,2880]{2,1,0:T(8,128)(2,1)S(1)}, u32[]{:S(2)}, u32[]{:S(2)}) collective-permute-start(bf16[8,8,2880]{2,1,0:T(8,128)(2,1)S(1)} %get-tuple-element.69), channel_id=1, source_target_pairs={{0,16},{16,32},{32,48},{48,0},{1,17},{17,33},{33,49},{49,1},{2,18}... | collective-permute-start | bytes 1105928 | tf_op jit(solution)/shard_map/ppermute | solution.py:375
  73.0 20.0 %collective-permute-start.23 = (bf16[8,8,2880]{2,1,0:T(8,128)(2,1)S(1)}, bf16[8,8,2880]{2,1,0:T(8,128)(2,1)S(1)}, u32[]{:S(2)}, u32[]{:S(2)}) collective-permute-start(bf16[8,8,2880]{2,1,0:T(8,128)(2,1)S(1)} %get-tuple-element.70), channel_id=1, source_target_pairs={{0,32},{16,48},{32,0},{48,16},{1,33},{17,49},{33,1},{49,17},{2,34}... | collective-permute-start | bytes 1105928 | tf_op jit(solution)/shard_map/ppermute | solution.py:375
  73.1 20.3 %collective-permute-start.24 = (bf16[8,8,2880]{2,1,0:T(8,128)(2,1)S(1)}, bf16[8,8,2880]{2,1,0:T(8,128)(2,1)S(1)}, u32[]{:S(2)}, u32[]{:S(2)}) collective-permute-start(bf16[8,8,2880]{2,1,0:T(8,128)(2,1)S(1)} %get-tuple-element.71), channel_id=1, source_target_pairs={{0,48},{16,0},{32,16},{48,32},{1,49},{17,1},{33,17},{49,33},{2,50}... | collective-permute-start | bytes 1105928 | tf_op jit(solution)/shard_map/ppermute | solution.py:375
  92.0 30.1 %collective-permute-start.28 = (bf16[180,2160]{1,0:T(8,128)(2,1)S(1)}, bf16[180,2160]{1,0:T(8,128)(2,1)S(1)}, u32[]{:S(2)}, u32[]{:S(2)}) collective-permute-start(bf16[180,2160]{1,0:T(8,128)(2,1)S(1)} %get-tuple-element.85), channel_id=1, source_target_pairs={{0,192},{64,0},{128,64},{192,128},{1,193},{65,1},{129,65},{193,129... | collective-permute-start | bytes 2332808 | tf_op jit(solution)/shard_map/ppermute | solution.py:375
  93.0 29.1 %collective-permute-start.31 = (bf16[180,2160]{1,0:T(8,128)(2,1)S(1)}, bf16[180,2160]{1,0:T(8,128)(2,1)S(1)}, u32[]{:S(2)}, u32[]{:S(2)}) collective-permute-start(bf16[180,2160]{1,0:T(8,128)(2,1)S(1)} %get-tuple-element.88), channel_id=1, source_target_pairs={{0,64},{64,128},{128,192},{192,0},{1,65},{65,129},{129,193},{193,1... | collective-permute-start | bytes 2332808 | tf_op jit(solution)/shard_map/ppermute | solution.py:375
  93.9 35.0 %collective-permute-start.30 = (bf16[180,2160]{1,0:T(8,128)(2,1)S(1)}, bf16[180,2160]{1,0:T(8,128)(2,1)S(1)}, u32[]{:S(2)}, u32[]{:S(2)}) collective-permute-start(bf16[180,2160]{1,0:T(8,128)(2,1)S(1)} %add.2), channel_id=1, source_target_pairs={{0,64},{64,128},{128,192},{192,0},{1,65},{65,129},{129,193},{193,1... | collective-permute-start | bytes 2332808 | tf_op jit(solution)/shard_map/ppermute | solution.py:375
  94.2 34.7 %collective-permute-start.33 = (bf16[180,2160]{1,0:T(8,128)(2,1)S(1)}, bf16[180,2160]{1,0:T(8,128)(2,1)S(1)}, u32[]{:S(2)}, u32[]{:S(2)}) collective-permute-start(bf16[180,2160]{1,0:T(8,128)(2,1)S(1)} %add.3), channel_id=1, source_target_pairs={{0,192},{64,0},{128,64},{192,128},{1,193},{65,1},{129,65},{193,129... | collective-permute-start | bytes 2332808 | tf_op jit(solution)/shard_map/ppermute | solution.py:375
  96.9 8.4 %collective-permute-start.25 = (bf16[4,8,2880]{2,1,0:T(8,128)(2,1)S(1)}, bf16[4,8,2880]{2,1,0:T(8,128)(2,1)S(1)}, u32[]{:S(2)}, u32[]{:S(2)}) collective-permute-start(bf16[4,8,2880]{2,1,0:T(8,128)(2,1)S(1)} %get-tuple-element.73), channel_id=1, source_target_pairs={{0,8},{1,9},{2,10},{3,11},{4,12},{5,13},{6,14},{7,15},{8,0},{9,1},... | collective-permute-start | bytes 552968 | tf_op jit(solution)/shard_map/ppermute | solution.py:375
  105.4 11.5 %collective-permute-start.26 = (bf16[2,8,2880]{2,1,0:T(8,128)(2,1)S(1)}, bf16[2,8,2880]{2,1,0:T(8,128)(2,1)S(1)}, u32[]{:S(2)}, u32[]{:S(2)}) collective-permute-start(bf16[2,8,2880]{2,1,0:T(8,128)(2,1)S(1)} %get-tuple-element.75), channel_id=1, source_target_pairs={{0,4},{1,5},{2,6},{3,7},{4,8},{5,9},{6,10},{7,11},{8,12},{9,13},{1... | collective-permute-start | bytes 276488 | tf_op jit(solution)/shard_map/ppermute | solution.py:375
  (5 other events, 19.2 us)

commit v3 on v2

--- a/solution.py
+++ b/solution.py
@@ -113,7 +113,36 @@
     )(w_gate, w_up, w_down)
 
 
-def forward(own, far, first, cat, down, width, n_exp, n_group, n_dp):
+def put_shares(act_ref, cat_ref, outs):
+    span = act_ref.shape[1] // 3
+    part = jnp.dot(act_ref[:, : 2 * span], cat_ref[...], preferred_element_type=jnp.float32).astype(jnp.bfloat16)
+    n_group, n_near, rows, _ = outs[0].shape
+    at = 0
+    for ref in outs:
+        for z in range(n_near):
+            for g in range(n_group):
+                ref[g, z] = part[at : at + rows]
+                at += rows
+
+
+def token_shares(act, cat, n_group, after):
+    width = cat.shape[1]
+
+    def kernel(act_ref, cat_ref, _, *outs):
+        put_shares(act_ref, cat_ref, outs)
+
+    sums = jax.ShapeDtypeStruct((n_group, act.shape[0] // (16 * n_group), 8, width), jnp.bfloat16)
+    return pl.pallas_call(
+        kernel,
+        out_shape=(sums, sums),
+        in_specs=[VMEM, VMEM, pl.BlockSpec(memory_space=pl.ANY)],
+        out_specs=(VMEM, VMEM),
+        compiler_params=pltpu.CompilerParams(vmem_limit_bytes=12 * MIB),
+        name="token_shares",
+    )(act, cat, after)
+
+
+def forward(own, far, first, cat, down, width, n_exp, n_group, n_dp, shares=True):
     half = sum(p.shape[1] for p in own)
     tall = 2 * half
     span = down.shape[0]
@@ -128,7 +157,8 @@
 
     def kernel(first_ref, *refs):
         rows = refs[: len(pieces)]
-        cat_ref, down_ref, act_ref, near_ref, away_ref, cut_ref = refs[len(pieces) :]
+        cat_ref, down_ref = refs[len(pieces) : len(pieces) + 2]
+        act_ref, cut_ref = refs[len(pieces) + 2], refs[-1]
         x = jnp.concatenate([r[0, :, :width] for r in rows], axis=0)
         y = jnp.concatenate([r[1, :, :width] for r in rows], axis=0)
         pre = lax.dot_general(x, cat_ref[...], nt, preferred_element_type=f32)
@@ -154,24 +184,19 @@
         act_ref[:, :span] = (back * up * sig * (1.0 + gate * (1.0 - sig))).astype(bf)
         act_ref[:, span : 2 * span] = (back * silu).astype(bf)
         act_ref[:, 2 * span :] = (coef * (silu * up)).astype(bf)
-        part = jnp.dot(act_ref[:, : 2 * span], cat_ref[...], preferred_element_type=f32).astype(bf)
-        for c, ref in enumerate((near_ref, away_ref)):
-            for z in range(n_near):
-                for g in range(n_group):
-                    at = c * half + z * block + g * 8
-                    ref[g, z] = part[at : at + 8]
-
-    sums = jax.ShapeDtypeStruct((n_group, n_near, 8, width), bf)
+        if shares:
+            put_shares(act_ref, cat_ref, refs[-3:-1])
+
+    sums = (jax.ShapeDtypeStruct((n_group, n_near, 8, width), bf),) * (2 * shares)
     return pl.pallas_call(
         kernel,
         out_shape=(
             jax.ShapeDtypeStruct((tall, 3 * span), bf),
-            sums,
-            sums,
+            *sums,
             jax.ShapeDtypeStruct((2, n_dp, tall, cols), bf),
         ),
         in_specs=[SMEM] + [VMEM] * (len(pieces) + 2),
-        out_specs=(VMEM,) * 4,
+        out_specs=(VMEM,) * (2 + len(sums)),
         compiler_params=pltpu.CompilerParams(vmem_limit_bytes=12 * MIB),
         cost_estimate=pl.CostEstimate(
             flops=2 * tall * width * 5 * span, bytes_accessed=12 * MIB, transcendentals=tall * span
@@ -345,7 +370,7 @@
             for r in refs[1 : len(parts)]:
                 total = total + r[j].astype(jnp.float32)
             ahead = offset % chips
-            outs[ahead // half][ahead % half] = total.astype(jnp.bfloat16)
+            outs[ahead % 2][ahead // 2] = total.astype(jnp.bfloat16)
 
     one = jax.ShapeDtypeStruct((half,) + parts[0].shape[1:], parts[0].dtype)
     return small(kernel, (one, one), tuple(parts))
@@ -357,7 +382,7 @@
     def kernel(a_ref, b_ref, *outs):
         for j in range(2 * half):
             total = a_ref[j].astype(jnp.float32) + b_ref[j].astype(jnp.float32)
-            outs[j // half][j % half] = total.astype(jnp.bfloat16)
+            outs[j % 2][j // 2] = total.astype(jnp.bfloat16)
 
     one = jax.ShapeDtypeStruct((half,) + kept.shape[1:], kept.dtype)
     return small(kernel, (one, one), (kept, arrived))
@@ -412,10 +437,10 @@
     top, bottom = halves(lo[3], hi[3])
     top = shifted(top, "member", -2)
     bottom = shifted(bottom, "member", 2)
-    act_2, near_2, away_2, cut_2 = forward(
+    act_2, cut_2 = forward(
         [lo[3], hi[3], top, bottom],
         [lo_far[2], hi_far[2], partner(top), partner(bottom)],
-        first, cat, down, width, n_exp, n_group, n_dp,
+        first, cat, down, width, n_exp, n_group, n_dp, shares=False,
     )
 
     def shares(offsets, after=()):
@@ -424,6 +449,7 @@
     ((far_0, far_1),) = shares((2,))
     right_0 = shifted(far_0, "dp", -1)
     left_1 = shifted(far_1, "dp", 1)
+    near_2, away_2 = token_shares(act_2, cat, n_group, far_0)
     away_1 = partner(away_1)
     away_2 = partner(away_2)
     both = merge_cores((near_1, near_2), (away_1, away_2))
@@ -434,14 +460,14 @@
     from_left_1 = shifted(next_1, "dp", -1)
     from_right_0 = shifted(prev_0, "dp", 1)
     kept, sent = by_chip([both[0]] + others)
-    sent = shifted(sent, "member", -8)
+    sent = shifted(sent, "member", -2)
     joined_0 = add(next_0, right_0, kept)
     joined_1 = add(prev_1, left_1, kept)
     from_left_0 = shifted(joined_0, "dp", -1)
     from_right_1 = shifted(joined_1, "dp", 1)
     kept, sent = fold(kept, sent)
     kept, sent = fold(kept, shifted(sent, "member", -4))
-    grad_tokens = total_of(kept, shifted(sent, "member", -2))
+    grad_tokens = total_of(kept, shifted(sent, "member", -8))
     grads = finish([[here_0, from_right_0, from_left_0], [here_1, from_left_1, from_right_1]])
     return (grad_tokens,) + tuple(grads)
 

time: 133 us -> 133 us (level)
  waiting for transfers between devices: 50.9 us -> 54.9 us
  starting transfers between devices: 53.5 us -> 50 us
    ppermute x23, waiting for transfers between devices: 50.8 us -> 54.8 us  [shifted(): return lax.ppermute(x, axis, [(i, (i - step) % n) for i in range(n)])]
    ppermute x23, starting transfers between devices: 38.7 us -> 35.2 us  [shifted(): return lax.ppermute(x, axis, [(i, (i - step) % n) for i in range(n)])]
    pallas_call x2, Pallas kernels: 9.35 us -> 7.67 us  [forward(): pl.pallas_call(kernel, out_shape=(jax.ShapeDtypeStruct((tall, 3 * span),...]
where the time goes in v3:
time: 133 us; the launch traced here: 131 us
  waiting for transfers between devices  54.9 us (41%)
  starting transfers between devices  50 us (38%)
  Pallas kernels  21.3 us (16%)
  local copies, waits for them, and re-layouts  4.51 us (3%)
    ppermute x23, waiting for transfers between devices, shifted(): return lax.ppermute(x, axis, [(i, (i - step) % n) for i in range(n)])  54.8 us
    ppermute x23, starting transfers between devices, shifted(): return lax.ppermute(x, axis, [(i, (i - step) % n) for i in range(n)])  35.2 us
    ppermute x11, starting transfers between devices, partner(): return lax.ppermute(x, 'member', [(i, i ^ 1) for i in range(n)])  14.8 us
    pallas_call x2, Pallas kernels, forward(): pl.pallas_call(kernel, out_shape=(jax.ShapeDtypeStruct((tall, 3 * span),...  7.67 us
    pallas_call x2, Pallas kernels, column_sums(): pl.pallas_call(kernel, out_shape=(jax.ShapeDtypeStruct((hid, 3 * cols), j...  5.77 us
    unnamed x9, local copies, waits for them, and re-layouts  4.51 us
  transfers between devices with their start and end apart: 34, of which 11 were waited for; matrix products, arithmetic and copies ran while one was open for 2% of the time, Pallas kernels for 13%

profile of v3, /device:TPU:1, one launch (start us, length us, event | category | flops | bytes accessed | tf_op | source)
XLA Modules:
  0.0 131.5 jit_solution(10712739054998583489)
XLA Ops:
  0.6 1.7 %prepare.1.refs_0_ = bf16[2,8,2944]{2,1,0:T(8,128)(2,1)} custom-call(bf16[8,2880]{1,0:T(8,128)(2,1)} %refs_0_.1, bf16[8,2880]{1,0:T(8,128)(2,1)} %refs_1_.1, s32[4,8]{1,0:T(4,128)} %bitcast.7, f32[4,8]{1,0:T(4,128)} %bitcast.8), custom_call_target="tpu_custom_call" | custom-call | tf_op jit(solution)/shard_map/prepare/pallas_call | solution.py:51
  2.3 3.6 %collective-permute-start = (bf16[2,8,2944]{2,1,0:T(8,128)(2,1)}, bf16[2,8,2944]{2,1,0:T(8,128)(2,1)S(1)}, u32[]{:S(2)}, u32[]{:S(2)}) collective-permute-start(bf16[2,8,2944]{2,1,0:T(8,128)(2,1)} %prepare.1.refs_0_), channel_id=1, source_target_pairs={{0,48},{16,0},{32,16},{48,32},{1,49},{17,1},{33,17},{49,33},{2,50}... | collective-permute-start | bytes 282632 | tf_op jit(solution)/shard_map/ppermute | solution.py:400
  7.9 3.3 %collective-permute-done.1.refs_2_ = bf16[2,8,2944]{2,1,0:T(8,128)(2,1)S(1)} collective-permute-done((bf16[2,8,2944]{2,1,0:T(8,128)(2,1)}, bf16[2,8,2944]{2,1,0:T(8,128)(2,1)S(1)}, u32[]{:S(2)}, u32[]{:S(2)}) %collective-permute-start.1) | collective-permute-done | bytes 94240 | tf_op jit(solution)/shard_map/ppermute | solution.py:400
  11.2 2.6 %collective-permute-done.2.refs_3_ = bf16[2,8,2944]{2,1,0:T(8,128)(2,1)S(1)} collective-permute-done((bf16[2,8,2944]{2,1,0:T(8,128)(2,1)}, bf16[2,8,2944]{2,1,0:T(8,128)(2,1)S(1)}, u32[]{:S(2)}, u32[]{:S(2)}) %collective-permute-start.2) | collective-permute-done | bytes 94240 | tf_op jit(solution)/shard_map/ppermute | solution.py:400
  14.8 1.7 %collective-permute-start.3 = (bf16[2,32,2944]{2,1,0:T(8,128)(2,1)S(1)}, bf16[2,32,2944]{2,1,0:T(8,128)(2,1)S(1)}, u32[]{:S(2)}, u32[]{:S(2)}) collective-permute-start(bf16[2,32,2944]{2,1,0:T(8,128)(2,1)S(1)} %join.1.refs_0_), channel_id=1, source_target_pairs={{0,2},{1,3},{2,4},{3,5},{4,6},{5,7},{6,8},{7,9},{8,10},{9,11},{10,... | collective-permute-start | bytes 1130504 | tf_op jit(solution)/shard_map/ppermute | solution.py:400
  16.5 4.0 %collective-permute-start.4 = (bf16[2,32,2944]{2,1,0:T(8,128)(2,1)S(1)}, bf16[2,32,2944]{2,1,0:T(8,128)(2,1)S(1)}, u32[]{:S(2)}, u32[]{:S(2)}) collective-permute-start(bf16[2,32,2944]{2,1,0:T(8,128)(2,1)S(1)} %join.1.refs_0_), channel_id=1, source_target_pairs={{0,14},{1,15},{2,0},{3,1},{4,2},{5,3},{6,4},{7,5},{8,6},{9,7},{10,... | collective-permute-start | bytes 1130504 | tf_op jit(solution)/shard_map/ppermute | solution.py:400
  20.5 1.8 %copy.11.g_ref = bf16[2,180,2880]{2,1,0:T(8,128)(2,1)S(1)} copy(bf16[2,180,2880]{2,0,1:T(2,128)(2,1)} %param.11) | data formatting | bytes 4147200 | tf_op args[4]
  26.2 2.4 %collective-permute-done.3.refs_1_ = bf16[2,32,2944]{2,1,0:T(8,128)(2,1)S(1)} collective-permute-done((bf16[2,32,2944]{2,1,0:T(8,128)(2,1)S(1)}, bf16[2,32,2944]{2,1,0:T(8,128)(2,1)S(1)}, u32[]{:S(2)}, u32[]{:S(2)}) %collective-permute-start.3) | collective-permute-done | bytes 376864 | tf_op jit(solution)/shard_map/ppermute | solution.py:400
  28.6 2.7 %collective-permute-start.6 = (bf16[2,32,2944]{2,1,0:T(8,128)(2,1)S(1)}, bf16[2,32,2944]{2,1,0:T(8,128)(2,1)S(1)}, u32[]{:S(2)}, u32[]{:S(2)}) collective-permute-start(bf16[2,32,2944]{2,1,0:T(8,128)(2,1)S(1)} %collective-permute-done.4.refs_2_), channel_id=1, source_target_pairs={{0,14},{1,15},{2,0},{3,1},{4,2},{5,3},{6,4},{7,5},{8,6},{9,7},{10,... | collective-permute-start | bytes 1130504 | tf_op jit(solution)/shard_map/ppermute | solution.py:400
  31.3 2.1 %collective-permute-start.8 = (bf16[2,32,2944]{2,1,0:T(8,128)(2,1)S(1)}, bf16[2,32,2944]{2,1,0:T(8,128)(2,1)S(1)}, u32[]{:S(2)}, u32[]{:S(2)}) collective-permute-start(bf16[2,32,2944]{2,1,0:T(8,128)(2,1)S(1)} %collective-permute-done.3.refs_1_), channel_id=1, source_target_pairs={{0,1},{1,0},{2,3},{3,2},{4,5},{5,4},{6,7},{7,6},{8,9},{9,8},{10,11... | collective-permute-start | bytes 1130504 | tf_op jit(solution)/shard_map/ppermute | solution.py:405
  33.4 5.2 %collective-permute-done.5.refs_3_ = bf16[2,32,2944]{2,1,0:T(8,128)(2,1)S(1)} collective-permute-done((bf16[2,32,2944]{2,1,0:T(8,128)(2,1)S(1)}, bf16[2,32,2944]{2,1,0:T(8,128)(2,1)S(1)}, u32[]{:S(2)}, u32[]{:S(2)}) %collective-permute-start.5) | collective-permute-done | bytes 376864 | tf_op jit(solution)/shard_map/ppermute | solution.py:400
  39.6 1.7 %collective-permute-start.13 = (bf16[2,32,2944]{2,1,0:T(8,128)(2,1)S(1)}, bf16[2,32,2944]{2,1,0:T(8,128)(2,1)S(1)}, u32[]{:S(2)}, u32[]{:S(2)}) collective-permute-start(bf16[2,32,2944]{2,1,0:T(8,128)(2,1)S(1)} %collective-permute-done.6.refs_4_), channel_id=1, source_target_pairs={{0,14},{1,15},{2,0},{3,1},{4,2},{5,3},{6,4},{7,5},{8,6},{9,7},{10,... | collective-permute-start | bytes 1130504 | tf_op jit(solution)/shard_map/ppermute | solution.py:400
  41.3 3.0 %collective-permute-start.10 = (bf16[2,32,2944]{2,1,0:T(8,128)(2,1)S(1)}, bf16[2,32,2944]{2,1,0:T(8,128)(2,1)S(1)}, u32[]{:S(2)}, u32[]{:S(2)}) collective-permute-start(bf16[2,32,2944]{2,1,0:T(8,128)(2,1)S(1)} %collective-permute-done.5.refs_3_), channel_id=1, source_target_pairs={{0,1},{1,0},{2,3},{3,2},{4,5},{5,4},{6,7},{7,6},{8,9},{9,8},{10,11... | collective-permute-start | bytes 1130504 | tf_op jit(solution)/shard_map/ppermute | solution.py:405
  44.3 3.5 %collective-permute-done.12.lo_ref.refs_0_ = bf16[2,32,2944]{2,1,0:T(8,128)(2,1)S(1)} collective-permute-done((bf16[2,32,2944]{2,1,0:T(8,128)(2,1)S(1)}, bf16[2,32,2944]{2,1,0:T(8,128)(2,1)S(1)}, u32[]{:S(2)}, u32[]{:S(2)}) %collective-permute-start.12) | collective-permute-done | bytes 376864 | tf_op jit(solution)/shard_map/ppermute | solution.py:400
  48.4 2.2 %collective-permute-start.15 = (bf16[2,16,2944]{2,1,0:T(8,128)(2,1)S(1)}, bf16[2,16,2944]{2,1,0:T(8,128)(2,1)S(1)}, u32[]{:S(2)}, u32[]{:S(2)}) collective-permute-start(bf16[2,16,2944]{2,1,0:T(8,128)(2,1)S(1)} %get-tuple-element.64), channel_id=1, source_target_pairs={{0,14},{1,15},{2,0},{3,1},{4,2},{5,3},{6,4},{7,5},{8,6},{9,7},{10,... | collective-permute-start | bytes 565256 | tf_op jit(solution)/shard_map/ppermute | solution.py:400
  50.6 3.8 %collective-permute-start.16 = (bf16[2,32,2944]{2,1,0:T(8,128)(2,1)S(1)}, bf16[2,32,2944]{2,1,0:T(8,128)(2,1)S(1)}, u32[]{:S(2)}, u32[]{:S(2)}) collective-permute-start(bf16[2,32,2944]{2,1,0:T(8,128)(2,1)S(1)} %collective-permute-done.12.lo_ref.refs_0_), channel_id=1, source_target_pairs={{0,1},{1,0},{2,3},{3,2},{4,5},{5,4},{6,7},{7,6},{8,9},{9,8},{10,11... | collective-permute-start | bytes 1130504 | tf_op jit(solution)/shard_map/ppermute | solution.py:405
  54.4 3.5 %collective-permute-start.18 = (bf16[2,16,2944]{2,1,0:T(8,128)(2,1)S(1)}, bf16[2,16,2944]{2,1,0:T(8,128)(2,1)S(1)}, u32[]{:S(2)}, u32[]{:S(2)}) collective-permute-start(bf16[2,16,2944]{2,1,0:T(8,128)(2,1)S(1)} %collective-permute-done.14.refs_2_), channel_id=1, source_target_pairs={{0,1},{1,0},{2,3},{3,2},{4,5},{5,4},{6,7},{7,6},{8,9},{9,8},{10,11... | collective-permute-start | bytes 565256 | tf_op jit(solution)/shard_map/ppermute | solution.py:405
  58.3 5.3 %forward.2 = (bf16[320,1152]{1,0:T(8,128)(2,1)S(1)}, bf16[4,5,8,2880]{3,2,1,0:T(8,128)(2,1)S(1)}, bf16[4,5,8,2880]{3,2,1,0:T(8,128)(2,1)S(1)}, bf16[2,4,320,720]{3,2,1,0:T(8,128)(2,1)S(1)}) custom-call(s32[1]{0:T(128)} %bitcast.3.first_ref, bf16[2,32,2944]{2,1,0:T(8,128)(2,1)S(1)} %join.1.refs_0_, bf16[2,32,2944]{2,1,0:T(8,128)(2,1)S(1)} %collective-permute-done.3.refs_1_, ...), custom_call_target="tpu_custom_call" | custom-call | flops 3538944000 | bytes 12582912 | tf_op jit(solution)/shard_map/forward/pallas_call | solution.py:191
  63.9 2.4 %forward.3 = (bf16[192,1152]{1,0:T(8,128)(2,1)S(1)}, bf16[2,4,192,720]{3,2,1,0:T(8,128)(2,1)S(1)}) custom-call(s32[1]{0:T(128)} %bitcast.3.first_ref, bf16[2,32,2944]{2,1,0:T(8,128)(2,1)S(1)} %collective-permute-done.12.lo_ref.refs_0_, bf16[2,32,2944]{2,1,0:T(8,128)(2,1)S(1)} %collective-permute-done.13.hi_ref.refs_1_, ...), custom_call_target="tpu_custom_call" | custom-call | flops 2123366400 | bytes 12582912 | tf_op jit(solution)/shard_map/forward/pallas_call | solution.py:191
  70.4 1.5 %collective-permute-start.32 = (bf16[180,2160]{1,0:T(8,128)(2,1)S(1)}, bf16[180,2160]{1,0:T(8,128)(2,1)S(1)}, u32[]{:S(2)}, u32[]{:S(2)}) collective-permute-start(bf16[180,2160]{1,0:T(8,128)(2,1)S(1)} %get-tuple-element.90), channel_id=1, source_target_pairs={{0,192},{64,0},{128,64},{192,128},{1,193},{65,1},{129,65},{193,129... | collective-permute-start | bytes 2332808 | tf_op jit(solution)/shard_map/ppermute | solution.py:400
  72.4 2.6 %collective-permute-start.24 = (bf16[8,8,2880]{2,1,0:T(8,128)(2,1)S(1)}, bf16[8,8,2880]{2,1,0:T(8,128)(2,1)S(1)}, u32[]{:S(2)}, u32[]{:S(2)}) collective-permute-start(bf16[8,8,2880]{2,1,0:T(8,128)(2,1)S(1)} %get-tuple-element.77), channel_id=1, source_target_pairs={{0,48},{16,0},{32,16},{48,32},{1,49},{17,1},{33,17},{49,33},{2,50}... | collective-permute-start | bytes 1105928 | tf_op jit(solution)/shard_map/ppermute | solution.py:400
  75.0 4.4 %column_sums.3 = (bf16[180,2160]{1,0:T(8,128)(2,1)S(1)}, bf16[180,2160]{1,0:T(8,128)(2,1)S(1)}, bf16[180,2160]{1,0:T(8,128)(2,1)S(1)}, bf16[180,2160]{1,0:T(8,12...) custom-call(s32[1]{0:T(128)} %bitcast.2.place_ref, ...), custom_call_target="tpu_custom_call" | custom-call | flops 2548039680 | bytes 12582912 | tf_op jit(solution)/shard_map/column_sums/pallas_call | solution.py:241
  79.4 11.8 %collective-permute-done.22.refs_1_ = bf16[8,8,2880]{2,1,0:T(8,128)(2,1)S(1)} collective-permute-done((bf16[8,8,2880]{2,1,0:T(8,128)(2,1)S(1)}, bf16[8,8,2880]{2,1,0:T(8,128)(2,1)S(1)}, u32[]{:S(2)}, u32[]{:S(2)}) %collective-permute-start.22) | collective-permute-done | bytes 368672 | tf_op jit(solution)/shard_map/ppermute | solution.py:400
  91.2 1.6 %collective-permute-start.28 = (bf16[180,2160]{1,0:T(8,128)(2,1)S(1)}, bf16[180,2160]{1,0:T(8,128)(2,1)S(1)}, u32[]{:S(2)}, u32[]{:S(2)}) collective-permute-start(bf16[180,2160]{1,0:T(8,128)(2,1)S(1)} %get-tuple-element.85), channel_id=1, source_target_pairs={{0,192},{64,0},{128,64},{192,128},{1,193},{65,1},{129,65},{193,129... | collective-permute-start | bytes 2332808 | tf_op jit(solution)/shard_map/ppermute | solution.py:400
  93.7 2.6 %collective-permute-start.33 = (bf16[180,2160]{1,0:T(8,128)(2,1)S(1)}, bf16[180,2160]{1,0:T(8,128)(2,1)S(1)}, u32[]{:S(2)}, u32[]{:S(2)}) collective-permute-start(bf16[180,2160]{1,0:T(8,128)(2,1)S(1)} %add.3), channel_id=1, source_target_pairs={{0,192},{64,0},{128,64},{192,128},{1,193},{65,1},{129,65},{193,129... | collective-permute-start | bytes 2332808 | tf_op jit(solution)/shard_map/ppermute | solution.py:400
  97.7 4.5 %collective-permute-done.25.b_ref = bf16[4,8,2880]{2,1,0:T(8,128)(2,1)S(1)} collective-permute-done((bf16[4,8,2880]{2,1,0:T(8,128)(2,1)S(1)}, bf16[4,8,2880]{2,1,0:T(8,128)(2,1)S(1)}, u32[]{:S(2)}, u32[]{:S(2)}) %collective-permute-start.25) | collective-permute-done | bytes 184352 | tf_op jit(solution)/shard_map/ppermute | solution.py:400
  102.3 1.6 %collective-permute-start.26 = (bf16[2,8,2880]{2,1,0:T(8,128)(2,1)S(1)}, bf16[2,8,2880]{2,1,0:T(8,128)(2,1)S(1)}, u32[]{:S(2)}, u32[]{:S(2)}) collective-permute-start(bf16[2,8,2880]{2,1,0:T(8,128)(2,1)S(1)} %get-tuple-element.81), channel_id=1, source_target_pairs={{0,4},{1,5},{2,6},{3,7},{4,8},{5,9},{6,10},{7,11},{8,12},{9,13},{1... | collective-permute-start | bytes 276488 | tf_op jit(solution)/shard_map/ppermute | solution.py:400
  103.9 5.0 %collective-permute-done.26.b_ref = bf16[2,8,2880]{2,1,0:T(8,128)(2,1)S(1)} collective-permute-done((bf16[2,8,2880]{2,1,0:T(8,128)(2,1)S(1)}, bf16[2,8,2880]{2,1,0:T(8,128)(2,1)S(1)}, u32[]{:S(2)}, u32[]{:S(2)}) %collective-permute-start.26) | collective-permute-done | bytes 92192 | tf_op jit(solution)/shard_map/ppermute | solution.py:400
  108.9 3.6 %collective-permute-start.27 = (bf16[1,8,2880]{2,1,0:T(8,128)(2,1)S(1)}, bf16[1,8,2880]{2,1,0:T(8,128)(2,1)S(1)}, u32[]{:S(2)}, u32[]{:S(2)}) collective-permute-start(bf16[1,8,2880]{2,1,0:T(8,128)(2,1)S(1)} %get-tuple-element.83), channel_id=1, source_target_pairs={{0,8},{1,9},{2,10},{3,11},{4,12},{5,13},{6,14},{7,15},{8,0},{9,1},... | collective-permute-start | bytes 138248 | tf_op jit(solution)/shard_map/ppermute | solution.py:400
  112.6 3.3 %collective-permute-done.27.b_ref = bf16[1,8,2880]{2,1,0:T(8,128)(2,1)S(1)} collective-permute-done((bf16[1,8,2880]{2,1,0:T(8,128)(2,1)S(1)}, bf16[1,8,2880]{2,1,0:T(8,128)(2,1)S(1)}, u32[]{:S(2)}, u32[]{:S(2)}) %collective-permute-start.27) | collective-permute-done | bytes 46112 | tf_op jit(solution)/shard_map/ppermute | solution.py:400
  116.5 12.4 %collective-permute-done.30.refs_2_ = bf16[180,2160]{1,0:T(8,128)(2,1)S(1)} collective-permute-done((bf16[180,2160]{1,0:T(8,128)(2,1)S(1)}, bf16[180,2160]{1,0:T(8,128)(2,1)S(1)}, u32[]{:S(2)}, u32[]{:S(2)}) %collective-permute-start.30) | collective-permute-done | bytes 777632 | tf_op jit(solution)/shard_map/ppermute | solution.py:400
  128.9 2.6 %finish.1 = (bf16[180,2,720]{2,1,0:T(2,128)(2,1)}, bf16[180,2,720]{2,1,0:T(2,128)(2,1)}, bf16[180,2,720]{2,1,0:T(2,128)(2,1)}) custom-call(bf16[180,2160]{1,0:T(8,128)(2,1)S(1)} %get-tuple-element.84.refs_0_, bf16[180,2160]{1,0:T(8,128)(2,1)S(1)} %collective-permute-done.28.refs_1_, bf16[180,2160]{1,0:T(8,128)(2,1)S(1)} %collective-permute-done.30.refs_2_, ...), custom_call_target="tpu_custom_call" | custom-call | tf_op jit(solution)/shard_map/finish/pallas_call | solution.py:284
  (62 shorter events, 16.7 us)
Async XLA Ops:
  2.3 5.5 %collective-permute-start = (bf16[2,8,2944]{2,1,0:T(8,128)(2,1)}, bf16[2,8,2944]{2,1,0:T(8,128)(2,1)S(1)}, u32[]{:S(2)}, u32[]{:S(2)}) collective-permute-start(bf16[2,8,2944]{2,1,0:T(8,128)(2,1)} %prepare.1.refs_0_), channel_id=1, source_target_pairs={{0,48},{16,0},{32,16},{48,32},{1,49},{17,1},{33,17},{49,33},{2,50}... | collective-permute-start | bytes 282632 | tf_op jit(solution)/shard_map/ppermute | solution.py:400
  5.9 5.2 %collective-permute-start.1 = (bf16[2,8,2944]{2,1,0:T(8,128)(2,1)}, bf16[2,8,2944]{2,1,0:T(8,128)(2,1)S(1)}, u32[]{:S(2)}, u32[]{:S(2)}) collective-permute-start(bf16[2,8,2944]{2,1,0:T(8,128)(2,1)} %prepare.1.refs_0_), channel_id=1, source_target_pairs={{0,32},{16,48},{32,0},{48,16},{1,33},{17,49},{33,1},{49,17},{2,34}... | collective-permute-start | bytes 282632 | tf_op jit(solution)/shard_map/ppermute | solution.py:400
  6.3 7.5 %collective-permute-start.2 = (bf16[2,8,2944]{2,1,0:T(8,128)(2,1)}, bf16[2,8,2944]{2,1,0:T(8,128)(2,1)S(1)}, u32[]{:S(2)}, u32[]{:S(2)}) collective-permute-start(bf16[2,8,2944]{2,1,0:T(8,128)(2,1)} %prepare.1.refs_0_), channel_id=1, source_target_pairs={{0,16},{16,32},{32,48},{48,0},{1,17},{17,33},{33,49},{49,1},{2,18}... | collective-permute-start | bytes 282632 | tf_op jit(solution)/shard_map/ppermute | solution.py:400
  14.8 13.8 %collective-permute-start.3 = (bf16[2,32,2944]{2,1,0:T(8,128)(2,1)S(1)}, bf16[2,32,2944]{2,1,0:T(8,128)(2,1)S(1)}, u32[]{:S(2)}, u32[]{:S(2)}) collective-permute-start(bf16[2,32,2944]{2,1,0:T(8,128)(2,1)S(1)} %join.1.refs_0_), channel_id=1, source_target_pairs={{0,2},{1,3},{2,4},{3,5},{4,6},{5,7},{6,8},{7,9},{8,10},{9,11},{10,... | collective-permute-start | bytes 1130504 | tf_op jit(solution)/shard_map/ppermute | solution.py:400
  16.5 12.1 %collective-permute-start.4 = (bf16[2,32,2944]{2,1,0:T(8,128)(2,1)S(1)}, bf16[2,32,2944]{2,1,0:T(8,128)(2,1)S(1)}, u32[]{:S(2)}, u32[]{:S(2)}) collective-permute-start(bf16[2,32,2944]{2,1,0:T(8,128)(2,1)S(1)} %join.1.refs_0_), channel_id=1, source_target_pairs={{0,14},{1,15},{2,0},{3,1},{4,2},{5,3},{6,4},{7,5},{8,6},{9,7},{10,... | collective-permute-start | bytes 1130504 | tf_op jit(solution)/shard_map/ppermute | solution.py:400
  24.9 8.5 %collective-permute-start.7 = (bf16[2,32,2944]{2,1,0:T(8,128)(2,1)S(1)}, bf16[2,32,2944]{2,1,0:T(8,128)(2,1)S(1)}, u32[]{:S(2)}, u32[]{:S(2)}) collective-permute-start(bf16[2,32,2944]{2,1,0:T(8,128)(2,1)S(1)} %join.1.refs_0_), channel_id=1, source_target_pairs={{0,1},{1,0},{2,3},{3,2},{4,5},{5,4},{6,7},{7,6},{8,9},{9,8},{10,11... | collective-permute-start | bytes 1130504 | tf_op jit(solution)/shard_map/ppermute | solution.py:405
  28.6 10.0 %collective-permute-start.5 = (bf16[2,32,2944]{2,1,0:T(8,128)(2,1)S(1)}, bf16[2,32,2944]{2,1,0:T(8,128)(2,1)S(1)}, u32[]{:S(2)}, u32[]{:S(2)}) collective-permute-start(bf16[2,32,2944]{2,1,0:T(8,128)(2,1)S(1)} %collective-permute-done.3.refs_1_), channel_id=1, source_target_pairs={{0,2},{1,3},{2,4},{3,5},{4,6},{5,7},{6,8},{7,9},{8,10},{9,11},{10,... | collective-permute-start | bytes 1130504 | tf_op jit(solution)/shard_map/ppermute | solution.py:400
  28.6 10.0 %collective-permute-start.6 = (bf16[2,32,2944]{2,1,0:T(8,128)(2,1)S(1)}, bf16[2,32,2944]{2,1,0:T(8,128)(2,1)S(1)}, u32[]{:S(2)}, u32[]{:S(2)}) collective-permute-start(bf16[2,32,2944]{2,1,0:T(8,128)(2,1)S(1)} %collective-permute-done.4.refs_2_), channel_id=1, source_target_pairs={{0,14},{1,15},{2,0},{3,1},{4,2},{5,3},{6,4},{7,5},{8,6},{9,7},{10,... | collective-permute-start | bytes 1130504 | tf_op jit(solution)/shard_map/ppermute | solution.py:400
  31.3 7.3 %collective-permute-start.8 = (bf16[2,32,2944]{2,1,0:T(8,128)(2,1)S(1)}, bf16[2,32,2944]{2,1,0:T(8,128)(2,1)S(1)}, u32[]{:S(2)}, u32[]{:S(2)}) collective-permute-start(bf16[2,32,2944]{2,1,0:T(8,128)(2,1)S(1)} %collective-permute-done.3.refs_1_), channel_id=1, source_target_pairs={{0,1},{1,0},{2,3},{3,2},{4,5},{5,4},{6,7},{7,6},{8,9},{9,8},{10,11... | collective-permute-start | bytes 1130504 | tf_op jit(solution)/shard_map/ppermute | solution.py:405
  38.6 9.2 %collective-permute-start.12 = (bf16[2,32,2944]{2,1,0:T(8,128)(2,1)S(1)}, bf16[2,32,2944]{2,1,0:T(8,128)(2,1)S(1)}, u32[]{:S(2)}, u32[]{:S(2)}) collective-permute-start(bf16[2,32,2944]{2,1,0:T(8,128)(2,1)S(1)} %collective-permute-done.5.refs_3_), channel_id=1, source_target_pairs={{0,2},{1,3},{2,4},{3,5},{4,6},{5,7},{6,8},{7,9},{8,10},{9,11},{10,... | collective-permute-start | bytes 1130504 | tf_op jit(solution)/shard_map/ppermute | solution.py:400
  39.6 8.2 %collective-permute-start.13 = (bf16[2,32,2944]{2,1,0:T(8,128)(2,1)S(1)}, bf16[2,32,2944]{2,1,0:T(8,128)(2,1)S(1)}, u32[]{:S(2)}, u32[]{:S(2)}) collective-permute-start(bf16[2,32,2944]{2,1,0:T(8,128)(2,1)S(1)} %collective-permute-done.6.refs_4_), channel_id=1, source_target_pairs={{0,14},{1,15},{2,0},{3,1},{4,2},{5,3},{6,4},{7,5},{8,6},{9,7},{10,... | collective-permute-start | bytes 1130504 | tf_op jit(solution)/shard_map/ppermute | solution.py:400
  41.3 13.1 %collective-permute-start.10 = (bf16[2,32,2944]{2,1,0:T(8,128)(2,1)S(1)}, bf16[2,32,2944]{2,1,0:T(8,128)(2,1)S(1)}, u32[]{:S(2)}, u32[]{:S(2)}) collective-permute-start(bf16[2,32,2944]{2,1,0:T(8,128)(2,1)S(1)} %collective-permute-done.5.refs_3_), channel_id=1, source_target_pairs={{0,1},{1,0},{2,3},{3,2},{4,5},{5,4},{6,7},{7,6},{8,9},{9,8},{10,11... | collective-permute-start | bytes 1130504 | tf_op jit(solution)/shard_map/ppermute | solution.py:405
  44.3 14.0 %collective-permute-start.11 = (bf16[2,32,2944]{2,1,0:T(8,128)(2,1)S(1)}, bf16[2,32,2944]{2,1,0:T(8,128)(2,1)S(1)}, u32[]{:S(2)}, u32[]{:S(2)}) collective-permute-start(bf16[2,32,2944]{2,1,0:T(8,128)(2,1)S(1)} %collective-permute-done.6.refs_4_), channel_id=1, source_target_pairs={{0,1},{1,0},{2,3},{3,2},{4,5},{5,4},{6,7},{7,6},{8,9},{9,8},{10,11... | collective-permute-start | bytes 1130504 | tf_op jit(solution)/shard_map/ppermute | solution.py:405
  47.8 6.6 %collective-permute-start.14 = (bf16[2,16,2944]{2,1,0:T(8,128)(2,1)S(1)}, bf16[2,16,2944]{2,1,0:T(8,128)(2,1)S(1)}, u32[]{:S(2)}, u32[]{:S(2)}) collective-permute-start(bf16[2,16,2944]{2,1,0:T(8,128)(2,1)S(1)} %get-tuple-element.63), channel_id=1, source_target_pairs={{0,2},{1,3},{2,4},{3,5},{4,6},{5,7},{6,8},{7,9},{8,10},{9,11},{10,... | collective-permute-start | bytes 565256 | tf_op jit(solution)/shard_map/ppermute | solution.py:400
  48.4 9.6 %collective-permute-start.15 = (bf16[2,16,2944]{2,1,0:T(8,128)(2,1)S(1)}, bf16[2,16,2944]{2,1,0:T(8,128)(2,1)S(1)}, u32[]{:S(2)}, u32[]{:S(2)}) collective-permute-start(bf16[2,16,2944]{2,1,0:T(8,128)(2,1)S(1)} %get-tuple-element.64), channel_id=1, source_target_pairs={{0,14},{1,15},{2,0},{3,1},{4,2},{5,3},{6,4},{7,5},{8,6},{9,7},{10,... | collective-permute-start | bytes 565256 | tf_op jit(solution)/shard_map/ppermute | solution.py:400
  50.6 13.3 %collective-permute-start.16 = (bf16[2,32,2944]{2,1,0:T(8,128)(2,1)S(1)}, bf16[2,32,2944]{2,1,0:T(8,128)(2,1)S(1)}, u32[]{:S(2)}, u32[]{:S(2)}) collective-permute-start(bf16[2,32,2944]{2,1,0:T(8,128)(2,1)S(1)} %collective-permute-done.12.lo_ref.refs_0_), channel_id=1, source_target_pairs={{0,1},{1,0},{2,3},{3,2},{4,5},{5,4},{6,7},{7,6},{8,9},{9,8},{10,11... | collective-permute-start | bytes 1130504 | tf_op jit(solution)/shard_map/ppermute | solution.py:405
  54.4 9.4 %collective-permute-start.17 = (bf16[2,32,2944]{2,1,0:T(8,128)(2,1)S(1)}, bf16[2,32,2944]{2,1,0:T(8,128)(2,1)S(1)}, u32[]{:S(2)}, u32[]{:S(2)}) collective-permute-start(bf16[2,32,2944]{2,1,0:T(8,128)(2,1)S(1)} %collective-permute-done.13.hi_ref.refs_1_), channel_id=1, source_target_pairs={{0,1},{1,0},{2,3},{3,2},{4,5},{5,4},{6,7},{7,6},{8,9},{9,8},{10,11... | collective-permute-start | bytes 1130504 | tf_op jit(solution)/shard_map/ppermute | solution.py:405
  54.4 9.4 %collective-permute-start.18 = (bf16[2,16,2944]{2,1,0:T(8,128)(2,1)S(1)}, bf16[2,16,2944]{2,1,0:T(8,128)(2,1)S(1)}, u32[]{:S(2)}, u32[]{:S(2)}) collective-permute-start(bf16[2,16,2944]{2,1,0:T(8,128)(2,1)S(1)} %collective-permute-done.14.refs_2_), channel_id=1, source_target_pairs={{0,1},{1,0},{2,3},{3,2},{4,5},{5,4},{6,7},{7,6},{8,9},{9,8},{10,11... | collective-permute-start | bytes 565256 | tf_op jit(solution)/shard_map/ppermute | solution.py:405
  58.0 5.9 %collective-permute-start.19 = (bf16[2,16,2944]{2,1,0:T(8,128)(2,1)S(1)}, bf16[2,16,2944]{2,1,0:T(8,128)(2,1)S(1)}, u32[]{:S(2)}, u32[]{:S(2)}) collective-permute-start(bf16[2,16,2944]{2,1,0:T(8,128)(2,1)S(1)} %collective-permute-done.15.refs_3_), channel_id=1, source_target_pairs={{0,1},{1,0},{2,3},{3,2},{4,5},{5,4},{6,7},{7,6},{8,9},{9,8},{10,11... | collective-permute-start | bytes 565256 | tf_op jit(solution)/shard_map/ppermute | solution.py:405
  63.6 8.3 %collective-permute-start.20 = (bf16[4,5,8,2880]{3,2,1,0:T(8,128)(2,1)S(1)}, bf16[4,5,8,2880]{3,2,1,0:T(8,128)(2,1)S(1)}, u32[]{:S(2)}, u32[]{:S(2)}) collective-permute-start(bf16[4,5,8,2880]{3,2,1,0:T(8,128)(2,1)S(1)} %get-tuple-element.72), channel_id=1, source_target_pairs={{0,1},{1,0},{2,3},{3,2},{4,5},{5,4},{6,7},{7,6},{8,9},{9,8},{10,11... | collective-permute-start | bytes 2764808 | tf_op jit(solution)/shard_map/ppermute | solution.py:405
  69.2 23.8 %collective-permute-start.29 = (bf16[180,2160]{1,0:T(8,128)(2,1)S(1)}, bf16[180,2160]{1,0:T(8,128)(2,1)S(1)}, u32[]{:S(2)}, u32[]{:S(2)}) collective-permute-start(bf16[180,2160]{1,0:T(8,128)(2,1)S(1)} %get-tuple-element.70._.rest_0_), channel_id=1, source_target_pairs={{0,64},{64,128},{128,192},{192,0},{1,65},{65,129},{129,193},{193,1... | collective-permute-start | bytes 2332808 | tf_op jit(solution)/shard_map/ppermute | solution.py:400
  70.4 23.1 %collective-permute-start.32 = (bf16[180,2160]{1,0:T(8,128)(2,1)S(1)}, bf16[180,2160]{1,0:T(8,128)(2,1)S(1)}, u32[]{:S(2)}, u32[]{:S(2)}) collective-permute-start(bf16[180,2160]{1,0:T(8,128)(2,1)S(1)} %get-tuple-element.90), channel_id=1, source_target_pairs={{0,192},{64,0},{128,64},{192,128},{1,193},{65,1},{129,65},{193,129... | collective-permute-start | bytes 2332808 | tf_op jit(solution)/shard_map/ppermute | solution.py:400
  72.3 18.9 %collective-permute-start.22 = (bf16[8,8,2880]{2,1,0:T(8,128)(2,1)S(1)}, bf16[8,8,2880]{2,1,0:T(8,128)(2,1)S(1)}, u32[]{:S(2)}, u32[]{:S(2)}) collective-permute-start(bf16[8,8,2880]{2,1,0:T(8,128)(2,1)S(1)} %get-tuple-element.75), channel_id=1, source_target_pairs={{0,16},{16,32},{32,48},{48,0},{1,17},{17,33},{33,49},{49,1},{2,18}... | collective-permute-start | bytes 1105928 | tf_op jit(solution)/shard_map/ppermute | solution.py:400
  72.3 20.5 %collective-permute-start.23 = (bf16[8,8,2880]{2,1,0:T(8,128)(2,1)S(1)}, bf16[8,8,2880]{2,1,0:T(8,128)(2,1)S(1)}, u32[]{:S(2)}, u32[]{:S(2)}) collective-permute-start(bf16[8,8,2880]{2,1,0:T(8,128)(2,1)S(1)} %get-tuple-element.76), channel_id=1, source_target_pairs={{0,32},{16,48},{32,0},{48,16},{1,33},{17,49},{33,1},{49,17},{2,34}... | collective-permute-start | bytes 1105928 | tf_op jit(solution)/shard_map/ppermute | solution.py:400
  72.4 20.4 %collective-permute-start.24 = (bf16[8,8,2880]{2,1,0:T(8,128)(2,1)S(1)}, bf16[8,8,2880]{2,1,0:T(8,128)(2,1)S(1)}, u32[]{:S(2)}, u32[]{:S(2)}) collective-permute-start(bf16[8,8,2880]{2,1,0:T(8,128)(2,1)S(1)} %get-tuple-element.77), channel_id=1, source_target_pairs={{0,48},{16,0},{32,16},{48,32},{1,49},{17,1},{33,17},{49,33},{2,50}... | collective-permute-start | bytes 1105928 | tf_op jit(solution)/shard_map/ppermute | solution.py:400
  91.2 25.3 %collective-permute-start.28 = (bf16[180,2160]{1,0:T(8,128)(2,1)S(1)}, bf16[180,2160]{1,0:T(8,128)(2,1)S(1)}, u32[]{:S(2)}, u32[]{:S(2)}) collective-permute-start(bf16[180,2160]{1,0:T(8,128)(2,1)S(1)} %get-tuple-element.85), channel_id=1, source_target_pairs={{0,192},{64,0},{128,64},{192,128},{1,193},{65,1},{129,65},{193,129... | collective-permute-start | bytes 2332808 | tf_op jit(solution)/shard_map/ppermute | solution.py:400
  92.8 23.7 %collective-permute-start.31 = (bf16[180,2160]{1,0:T(8,128)(2,1)S(1)}, bf16[180,2160]{1,0:T(8,128)(2,1)S(1)}, u32[]{:S(2)}, u32[]{:S(2)}) collective-permute-start(bf16[180,2160]{1,0:T(8,128)(2,1)S(1)} %get-tuple-element.88), channel_id=1, source_target_pairs={{0,64},{64,128},{128,192},{192,0},{1,65},{65,129},{129,193},{193,1... | collective-permute-start | bytes 2332808 | tf_op jit(solution)/shard_map/ppermute | solution.py:400
  93.2 35.6 %collective-permute-start.30 = (bf16[180,2160]{1,0:T(8,128)(2,1)S(1)}, bf16[180,2160]{1,0:T(8,128)(2,1)S(1)}, u32[]{:S(2)}, u32[]{:S(2)}) collective-permute-start(bf16[180,2160]{1,0:T(8,128)(2,1)S(1)} %add.2), channel_id=1, source_target_pairs={{0,64},{64,128},{128,192},{192,0},{1,65},{65,129},{129,193},{193,1... | collective-permute-start | bytes 2332808 | tf_op jit(solution)/shard_map/ppermute | solution.py:400
  93.7 35.2 %collective-permute-start.33 = (bf16[180,2160]{1,0:T(8,128)(2,1)S(1)}, bf16[180,2160]{1,0:T(8,128)(2,1)S(1)}, u32[]{:S(2)}, u32[]{:S(2)}) collective-permute-start(bf16[180,2160]{1,0:T(8,128)(2,1)S(1)} %add.3), channel_id=1, source_target_pairs={{0,192},{64,0},{128,64},{192,128},{1,193},{65,1},{129,65},{193,129... | collective-permute-start | bytes 2332808 | tf_op jit(solution)/shard_map/ppermute | solution.py:400
  96.3 5.9 %collective-permute-start.25 = (bf16[4,8,2880]{2,1,0:T(8,128)(2,1)S(1)}, bf16[4,8,2880]{2,1,0:T(8,128)(2,1)S(1)}, u32[]{:S(2)}, u32[]{:S(2)}) collective-permute-start(bf16[4,8,2880]{2,1,0:T(8,128)(2,1)S(1)} %get-tuple-element.79), channel_id=1, source_target_pairs={{0,2},{1,3},{2,4},{3,5},{4,6},{5,7},{6,8},{7,9},{8,10},{9,11},{10,... | collective-permute-start | bytes 552968 | tf_op jit(solution)/shard_map/ppermute | solution.py:400
  102.3 6.6 %collective-permute-start.26 = (bf16[2,8,2880]{2,1,0:T(8,128)(2,1)S(1)}, bf16[2,8,2880]{2,1,0:T(8,128)(2,1)S(1)}, u32[]{:S(2)}, u32[]{:S(2)}) collective-permute-start(bf16[2,8,2880]{2,1,0:T(8,128)(2,1)S(1)} %get-tuple-element.81), channel_id=1, source_target_pairs={{0,4},{1,5},{2,6},{3,7},{4,8},{5,9},{6,10},{7,11},{8,12},{9,13},{1... | collective-permute-start | bytes 276488 | tf_op jit(solution)/shard_map/ppermute | solution.py:400
  108.9 6.9 %collective-permute-start.27 = (bf16[1,8,2880]{2,1,0:T(8,128)(2,1)S(1)}, bf16[1,8,2880]{2,1,0:T(8,128)(2,1)S(1)}, u32[]{:S(2)}, u32[]{:S(2)}) collective-permute-start(bf16[1,8,2880]{2,1,0:T(8,128)(2,1)S(1)} %get-tuple-element.83), channel_id=1, source_target_pairs={{0,8},{1,9},{2,10},{3,11},{4,12},{5,13},{6,14},{7,15},{8,0},{9,1},... | collective-permute-start | bytes 138248 | tf_op jit(solution)/shard_map/ppermute | solution.py:400
  (5 other events, 18.4 us)
